TPU v7x, 256 devices: a whole 4x4x8 slice. The times are simulated.
256 devices in a mesh: cls: 128 (over z, y, x), dp: 2 (over core).
Axes of the slice: x: 4, y: 4, z: 8, core: 2. Of those that a mesh axis runs over, the one named last changes fastest.
Arguments:
- images: bfloat16 [4096, 4096], P(('cls', 'dp')), may hold values from -6 to 6
- references: bfloat16 [128, 72, 4096], P('cls'), may hold values from -1 to 1
- candidates: int32 [4096, 8], P(('cls', 'dp')), may hold values from 0 to 127, all different within a row; in each aligned block of 16 rows (0 to 15, 16 to 31, ...) at most 2 rows name the same one
- inv_noise: bfloat16 [4096], P(('cls', 'dp')), may hold values from 0.5 to 150
Outputs:
- class_sums: float32 [128, 72, 4096], P('cls', 'dp')
- class_weights: float32 [128, 72], P('cls', 'dp')
Inputs may be any that keep to these rules, and one draw needn't show every extreme that they name: `candidates`: the classes of one row differ. In each aligned block of 16 rows (the rows of one device) no class is named by more than 2 rows, a bound that some block reaches.
All inputs are finite; a program needn't handle non-finite values.
Results may differ from a plain program's by a relative error of at most 0.006.
Values may be sent and summed in bfloat16 or wider, within the bound.
No kernel may reach another device: no remote copies, remote signals or barrier semaphores. Data moves between devices by JAX's collectives and lax.ppermute only.
A program may use at most 64 MiB of HBM per device.

v0:
```python
import functools
import math

import jax
import jax.numpy as jnp
from jax import lax
from jax.experimental import pallas as pl
from jax.experimental.pallas import tpu as pltpu
from jax.sharding import Mesh
from jax.sharding import PartitionSpec as P

LANES = 128
SLOTS = 2
PLANES = 8
FAR = 1e30
ROW_SHIFTS = (0, 1, -1)
COL_SHIFTS = (0, 1, -1)
MIB = 1024 * 1024
F32, BF16 = jnp.float32, jnp.bfloat16


def tile_of(t):
    return slice(t * LANES, (t + 1) * LANES)


def lane_row():
    return lax.broadcasted_iota(jnp.int32, (1, LANES), 1)


def fold_tile(load, q, tiles, low):
    first, second = load(q // 2), load(tiles // 2 + q // 2)
    half = LANES // 2
    if q % 2 == 0:
        return jnp.where(low, first, pltpu.roll(second, half, 1))
    return jnp.where(low, pltpu.roll(first, half, 1), second)


def unfold_tile(load, t, tiles, low):
    half = LANES // 2
    if t < tiles // 2:
        return jnp.where(low, load(2 * t), pltpu.roll(load(2 * t + 1), half, 1))
    first = 2 * t - tiles
    return jnp.where(low, pltpu.roll(load(first), half, 1), load(first + 1))


def pack_kernel(cand_ref, noise_ref, img_ref, send_ref, hold_ref):
    rows, top = cand_ref.shape
    planes, depth, _ = send_ref.shape
    tiles = img_ref.shape[1] // LANES
    low = lane_row() < LANES // 2
    for q in range(tiles):
        tile = fold_tile(lambda t: img_ref[:, tile_of(t)].astype(F32), q, tiles, low)
        hold_ref[q * rows : (q + 1) * rows] = tile.astype(BF16)
    row_id = lax.broadcasted_iota(jnp.int32, (rows, LANES), 0)
    lane_id = lax.broadcasted_iota(jnp.int32, (rows, LANES), 1)
    noise = jnp.sum(
        jnp.where(
            lax.broadcasted_iota(jnp.int32, (rows, rows), 0)
            == lax.broadcasted_iota(jnp.int32, (rows, rows), 1),
            noise_ref[...].astype(F32),
            0.0,
        ),
        axis=1,
        keepdims=True,
    )
    facts = jnp.where(lane_id == 0, noise, 0.0)
    facts = jnp.where(lane_id == 1, (row_id + 1).astype(F32), facts)
    hold_ref[tiles * rows :] = facts.astype(BF16)
    for plane in range(planes):
        send_ref[plane, : (tiles + 1) * rows] = hold_ref[...]
    named = [jnp.broadcast_to(cand_ref[:, k : k + 1], (rows, LANES)) for k in range(top)]
    earlier = (
        lax.broadcasted_iota(jnp.int32, (rows, rows), 0)
        > lax.broadcasted_iota(jnp.int32, (rows, rows), 1)
    ).astype(BF16)
    group = SLOTS * planes
    slot = (lane_id // planes) % SLOTS
    from_here = lane_id % planes == lax.axis_index("z")
    wide = depth // rows - tiles - 1
    for plane in range(planes):
        for part in range(wide):
            first = (plane * wide + part) * (LANES // group)
            cls = first + lane_id // group
            member = named[0] == cls
            for k in range(1, top):
                member = member | (named[k] == cls)
            before = jnp.dot(
                earlier, member.astype(F32).astype(BF16), preferred_element_type=F32
            )
            pick = member & (before == slot.astype(F32)) & from_here
            at = (tiles + 1 + part) * rows
            send_ref[plane, at : at + rows] = pick.astype(F32).astype(BF16)


def pick_kernel(recv_ref, send_ref, column_ref, pick_ref):
    planes = recv_ref.shape[0]
    owners, depth, _ = send_ref.shape
    rows = column_ref.shape[0] // planes
    tiles = column_ref.shape[1] // LANES
    wide = pick_ref.shape[1] // LANES
    for z in range(planes):
        for t in range(tiles):
            column_ref[z * rows : (z + 1) * rows, tile_of(t)] = recv_ref[
                z, t * rows : (t + 1) * rows
            ]
        for t in range(wide):
            pick_ref[z * rows : (z + 1) * rows, tile_of(t)] = recv_ref[
                z, (tiles + t) * rows : (tiles + t + 1) * rows
            ]
    pick = pick_ref[...].astype(F32).T.astype(BF16)
    group = depth // tiles
    width = 3
    for t in range(0, tiles, width):
        lanes = slice(t * LANES, (t + width) * LANES)
        got = jnp.dot(pick, column_ref[:, lanes], preferred_element_type=F32).astype(BF16)
        for i in range(width):
            for c in range(owners):
                send_ref[c, (t + i) * group : (t + i + 1) * group] = got[
                    c * group : (c + 1) * group, tile_of(i)
                ]


def shift_kernel(rot_ref, out_ref, half_ref):
    count, pixels = rot_ref.shape
    tiles = pixels // LANES
    side = LANES // 2
    groups = len(COL_SHIFTS) * count
    lane = lane_row()
    low = lane < side
    column = lane % side
    square = jnp.zeros((count, LANES), F32)
    for q in range(tiles):
        tile = fold_tile(lambda t: rot_ref[:, tile_of(t)].astype(F32), q, tiles, low)
        square = square + tile * tile
        right = jnp.where(
            column == 0, pltpu.roll(tile, LANES - side + 1, 1), pltpu.roll(tile, 1, 1)
        )
        left = jnp.where(
            column == side - 1, pltpu.roll(tile, side - 1, 1), pltpu.roll(tile, LANES - 1, 1)
        )
        for i, moved in enumerate((tile, right, left)):
            plain = moved.astype(BF16)
            for j, shift in enumerate(ROW_SHIFTS):
                to = q + shift
                value = plain
                if not 0 <= to < tiles:
                    to = to % tiles
                    value = pltpu.roll(moved, side, 1).astype(BF16)
                at = j * groups + i * count
                out_ref[at : at + count, tile_of(to)] = value
    half = 0.5 * jnp.sum(square, axis=1, keepdims=True)
    half_ref[...] = jnp.broadcast_to(half, half_ref.shape)


def score_kernel(recv_ref, shifted_ref, half_ref, x_ref, s_ref, tile_ref, *, pad):
    owners, depth, _ = recv_ref.shape
    tiles = x_ref.shape[1] // LANES - 2
    group = depth // (tiles + 1)
    slots = owners * group
    groups = s_ref.shape[0]
    count = half_ref.shape[0]
    for c in range(owners):
        for t in range(tiles):
            x_ref[c * group : (c + 1) * group, tile_of(t + 1)] = recv_ref[
                c, t * group : (t + 1) * group
            ]
    half_turn = LANES // 2
    x_ref[:, tile_of(0)] = pltpu.roll(x_ref[:, tile_of(tiles)].astype(F32), half_turn, 1).astype(
        BF16
    )
    x_ref[:, tile_of(tiles + 1)] = pltpu.roll(x_ref[:, tile_of(1)].astype(F32), half_turn, 1).astype(
        BF16
    )
    facts = recv_ref[:, tiles * group :, :].reshape(slots, LANES)
    choose = (
        lax.broadcasted_iota(jnp.int32, (16, LANES), 0)
        == lax.broadcasted_iota(jnp.int32, (16, LANES), 1)
    ).astype(F32).astype(BF16)
    turned = lax.dot_general(
        choose, facts, (((1,), (1,)), ((), ())), preferred_element_type=F32
    )
    noise, number = turned[0:1], turned[1:2]
    products = lax.dot_general(
        shifted_ref[...],
        x_ref[:, LANES : (tiles + 1) * LANES],
        (((1,), (1,)), ((), ())),
        preferred_element_type=F32,
    )
    half = half_ref[:, 0:1]
    row = lax.broadcasted_iota(jnp.int32, half.shape, 0)
    half = jnp.where(row % (count // 2) >= count // 2 - pad, FAR, half)
    half = jnp.concatenate([half] * len(COL_SHIFTS), axis=0)
    peak = None
    for i in range(len(ROW_SHIFTS)):
        scores = noise * (products[i * groups : (i + 1) * groups] - half)
        s_ref[:, i * slots : (i + 1) * slots] = scores
        top = jnp.max(scores, axis=0, keepdims=True)
        peak = top if peak is None else jnp.maximum(peak, top)
    total = jnp.zeros_like(peak)
    for i in range(len(ROW_SHIFTS)):
        scores = s_ref[:, i * slots : (i + 1) * slots]
        total = total + jnp.sum(jnp.exp(scores - peak), axis=0, keepdims=True)
    parts = slots // LANES
    for i, value in enumerate((peak, total, number)):
        for h in range(parts):
            tile_ref[i * parts + h : i * parts + h + 1] = value[:, tile_of(h)]
    tile_ref[3 * parts :] = jnp.zeros_like(tile_ref[3 * parts :])


def sum_kernel(s_ref, x_ref, mine_ref, all_ref, keep_ref, give_ref, w_ref, y_ref):
    groups = s_ref.shape[0]
    slots = x_ref.shape[0]
    pixels = x_ref.shape[1] - 2 * LANES
    owners = all_ref.shape[0] // 8
    count = groups // len(COL_SHIFTS)
    half_count = count // 2
    parts = slots // LANES
    side = LANES // 2
    lane = lane_row()
    second = (lane // PLANES) % SLOTS == 1

    def partner(row):
        return jnp.where(second, pltpu.roll(row, PLANES, 1), pltpu.roll(row, LANES - PLANES, 1))

    peaks, scales = [], []
    for h in range(parts):
        own = mine_ref[2 * parts + h : 2 * parts + h + 1]
        across = partner(own)
        shown = [all_ref[pl.ds(i * parts + h, owners, stride=8), :] for i in range(3)]
        found = []
        for slot in range(SLOTS):
            target = jnp.where(second == (slot == 1), own, across)
            same = shown[2] == target
            peak = jnp.max(jnp.where(same, shown[0], -jnp.inf), axis=0, keepdims=True)
            peak = jnp.maximum(peak, partner(peak))
            part = shown[1] * jnp.exp(jnp.minimum(shown[0] - peak, 0.0))
            total = jnp.sum(jnp.where(same, part, 0.0), axis=0, keepdims=True)
            found.append((peak, total + partner(total)))
        peaks.append(jnp.where(second, found[1][0], found[0][0]))
        total = jnp.where(second, found[1][1], found[0][1])
        scales.append(jnp.where(own > 0, 1.0 / total, 0.0))
    peak = jnp.concatenate(peaks, axis=1)
    scale = jnp.concatenate(scales, axis=1)
    row_total = jnp.zeros((groups, 1), F32)
    for i in range(len(ROW_SHIFTS)):
        part = slice(i * slots, (i + 1) * slots)
        weights = (jnp.exp(jnp.minimum(s_ref[:, part] - peak, 0.0)) * scale).astype(BF16)
        w_ref[:, part] = weights
        row_total = row_total + jnp.sum(weights.astype(F32), axis=1, keepdims=True)
    class_total = sum(row_total[i * count : (i + 1) * count] for i in range(len(COL_SHIFTS)))
    keep_ref[:, pixels:] = jnp.broadcast_to(class_total[:half_count], (half_count, LANES))
    give_ref[:, pixels:] = jnp.broadcast_to(class_total[half_count:], (half_count, LANES))
    width = y_ref.shape[1]
    column = lane % side
    for first in range(0, pixels, width):
        y_ref[...] = sum(
            jnp.dot(
                w_ref[:, i * slots : (i + 1) * slots],
                x_ref[:, (1 + shift) * LANES + first : (1 + shift) * LANES + first + width],
                preferred_element_type=F32,
            )
            for i, shift in enumerate(ROW_SHIFTS)
        )
        for t in range(width // LANES):
            plain = y_ref[:count, tile_of(t)]
            right = y_ref[count : 2 * count, tile_of(t)]
            left = y_ref[2 * count :, tile_of(t)]
            back = jnp.where(
                column == side - 1,
                pltpu.roll(right, side - 1, 1),
                pltpu.roll(right, LANES - 1, 1),
            )
            forth = jnp.where(
                column == 0, pltpu.roll(left, LANES - side + 1, 1), pltpu.roll(left, 1, 1)
            )
            moved = plain + back + forth
            at = slice(first + t * LANES, first + (t + 1) * LANES)
            keep_ref[:, at] = moved[:half_count]
            give_ref[:, at] = moved[half_count:]


def finish_kernel(keep_ref, other_ref, sums_ref, totals_ref):
    rots = totals_ref.shape[1]
    tiles = sums_ref.shape[0] // rots
    low = lane_row() < LANES // 2

    def load(t):
        return keep_ref[:rots, tile_of(t)] + other_ref[:rots, tile_of(t)]

    for t in range(tiles):
        sums_ref[pl.ds(t, rots, stride=tiles), :] = unfold_tile(load, t, tiles, low)
    total = load(tiles)
    here = lax.broadcasted_iota(jnp.int32, (rots, LANES), 0) == lax.broadcasted_iota(
        jnp.int32, (rots, LANES), 1
    )
    totals_ref[...] = jnp.sum(jnp.where(here, total, 0.0), axis=0, keepdims=True)[:, :rots]


def call(kernel, out_shape, count, limit, scratch=(), flops=0, moved=0):
    in_vmem = pl.BlockSpec(memory_space=pltpu.VMEM)
    return pl.pallas_call(
        kernel,
        out_shape=out_shape,
        in_specs=[in_vmem] * count,
        out_specs=jax.tree.map(lambda _: in_vmem, out_shape),
        scratch_shapes=list(scratch),
        cost_estimate=pl.CostEstimate(flops=flops, bytes_accessed=moved, transcendentals=0),
        compiler_params=pltpu.CompilerParams(vmem_limit_bytes=limit * MIB),
    )


def on_device(images, references, candidates, inv_noise):
    rows, top = candidates.shape
    cls_dev, rots, pixels = references.shape
    planes, owners = lax.axis_size("z"), lax.axis_size("xy")
    side = math.isqrt(pixels)
    tiles = pixels // LANES
    group = SLOTS * planes
    slots = owners * group
    assert cls_dev == 1 and planes == PLANES and LANES == 2 * side and rows == group
    wide = slots // LANES
    shape = jax.ShapeDtypeStruct
    exchange = functools.partial(lax.all_to_all, split_axis=0, concat_axis=0, tiled=True)

    packed = call(
        pack_kernel,
        shape((planes, (tiles + 1 + wide) * rows, LANES), BF16),
        3,
        8,
        [pltpu.VMEM(((tiles + 1) * rows, LANES), BF16)],
        moved=2 * MIB,
    )(candidates, inv_noise[None, :], images)
    column = exchange(packed, "z")

    half_rots = rots // 2
    half_count = -(-half_rots // 8) * 8
    own = references[0]
    flipped = jnp.where(
        lax.axis_index("dp") == 0, own, jnp.concatenate([own[half_rots:], own[:half_rots]], axis=0)
    )
    pad = half_count - half_rots
    padded = jnp.pad(flipped.reshape(2, half_rots, pixels), ((0, 0), (0, pad), (0, 0)))
    count = 2 * half_count
    groups = len(COL_SHIFTS) * count
    shifted, half_norm = call(
        shift_kernel,
        (shape((len(ROW_SHIFTS) * groups, pixels), BF16), shape((count, LANES), F32)),
        1,
        12,
        moved=12 * MIB,
    )(padded.reshape(count, pixels))

    picked = call(
        pick_kernel,
        shape((owners, (tiles + 1) * group, LANES), BF16),
        1,
        12,
        [
            pltpu.VMEM((planes * rows, (tiles + 1) * LANES), BF16),
            pltpu.VMEM((planes * rows, slots), BF16),
        ],
        moved=3 * MIB,
    )(column)
    received = exchange(picked, "xy")
    work = 2 * len(ROW_SHIFTS) * groups * slots * pixels
    x, scores, tile = call(
        functools.partial(score_kernel, pad=pad),
        (
            shape((slots, pixels + 2 * LANES), BF16),
            shape((groups, len(ROW_SHIFTS) * slots), F32),
            shape((8, LANES), F32),
        ),
        3,
        24,
        flops=work,
        moved=10 * MIB,
    )(received, shifted, half_norm)
    by_plane = exchange(jnp.broadcast_to(tile[None], (planes, 8, LANES)), "z")
    by_plane = by_plane.reshape(1, planes * 8, LANES)
    everyone = exchange(jnp.broadcast_to(by_plane, (owners, planes * 8, LANES)), "xy")
    half_shape = shape((half_count, pixels + LANES), F32)
    keep, give = call(
        sum_kernel,
        (half_shape, half_shape),
        4,
        24,
        [
            pltpu.VMEM((groups, len(ROW_SHIFTS) * slots), BF16),
            pltpu.VMEM((groups, 4 * LANES), F32),
        ],
        flops=work,
        moved=5 * MIB,
    )(scores, x, tile, everyone.reshape(owners * planes * 8, LANES))
    other = lax.ppermute(give, "dp", [(0, 1), (1, 0)])
    sums, totals = call(
        finish_kernel,
        (shape((half_rots * tiles, LANES), F32), shape((1, half_rots), F32)),
        2,
        8,
        moved=2 * MIB,
    )(keep, other)
    return sums.reshape(1, half_rots, pixels), totals


def solution(mesh):
    split = (PLANES, mesh.shape["cls"] // PLANES, mesh.shape["dp"])
    cube = Mesh(mesh.devices.reshape(split), ("z", "xy", "dp"))
    every = ("z", "xy", "dp")
    by_class = ("z", "xy")
    return jax.shard_map(
        on_device,
        mesh=cube,
        in_specs=(P(every, None), P(by_class, None, None), P(every, None), P(every)),
        out_specs=(P(by_class, "dp", None), P(by_class, "dp")),
        check_vma=False,
    )
```

profile of v0, /device:TPU:1, one launch (start us, length us, event | category | flops | bytes accessed | tf_op | source)
XLA Modules:
  0.0 122.2 jit_solution(6231877481514641011)
XLA Ops:
  0.6 0.8 copy.8.cand_ref
  1.4 0.0 copy-start.3
  1.4 0.9 copy-done.3
  2.3 0.0 copy-start.4
  2.3 0.7 copy-done.4
  2.9 1.4 %shard_map.59 = bf16[8,560,128]{2,1,0:T(8,128)(2,1)} custom-call(s32[16,8]{1,0:T(8,128)S(1)} %copy.8.cand_ref, bf16[1,16]{1,0:T(2,128)(2,1)S(1)} %bitcast.11, bf16[16,4096]{1,0:T(8,128)(2,1)S(1)} %copy-done.3), custom_call_target="tpu_custom_call" | custom-call | bytes 2097152 | tf_op jit(solution)/shard_map/pallas_call | solution.py:325
  4.4 0.0 copy-start.5
  4.4 9.1 %all-to-all-start = ((bf16[8,560,128]{2,1,0:T(8,128)(2,1)}), bf16[8,560,128]{2,1,0:T(8,128)(2,1)S(1)}, u32[]{:S(2)}, u32[]{:S(2)}) async-start(bf16[8,560,128]{2,1,0:T(8,128)(2,1)} %shard_map.59), calls=%async_computation | async-start | bytes 2293760 | tf_op jit(solution)/shard_map/all_to_all | solution.py:333
  13.5 0.0 copy-done.5
  13.5 0.1 squeeze.3
  13.7 31.2 %all-to-all-done.recv_ref = bf16[8,560,128]{2,1,0:T(8,128)(2,1)S(1)} async-done(((bf16[8,560,128]{2,1,0:T(8,128)(2,1)}), bf16[8,560,128]{2,1,0:T(8,128)(2,1)S(1)}, u32[]{:S(2)}, u32[]{:S(2)}) %all-to-all-start) | async-done | bytes 1146912 | tf_op jit(solution)/shard_map/all_to_all | solution.py:333
  44.9 0.8 shard_map.60
  45.7 0.0 copy-start
  45.7 1.4 %copy-done = bf16[16,528,128]{2,1,0:T(8,128)(2,1)} copy-done((bf16[16,528,128]{2,1,0:T(8,128)(2,1)}, bf16[16,528,128]{2,1,0:T(8,128)(2,1)S(1)}, u32[]{:S(2)}) %copy-start) | copy-done | bytes 2162712
  47.0 6.8 %all-to-all-start.1 = ((bf16[16,528,128]{2,1,0:T(8,128)(2,1)}), bf16[16,528,128]{2,1,0:T(8,128)(2,1)S(1)}, u32[]{:S(2)}, u32[]{:S(2)}) async-start(bf16[16,528,128]{2,1,0:T(8,128)(2,1)} %copy-done), calls=%async_computation.1 | async-start | bytes 4325376 | tf_op jit(solution)/shard_map/all_to_all | solution.py:364
  53.8 0.1 slice_bitcast_fusion.1
  53.9 0.9 pad_maximum_fusion
  54.8 1.2 concatenate.6
  56.0 0.1 broadcast_select_fusion
  56.1 3.0 %shard_map.61 = (bf16[720,4096]{1,0:T(8,128)(2,1)S(1)}, f32[80,128]{1,0:T(8,128)S(1)}) custom-call(bf16[80,4096]{1,0:T(8,128)(2,1)S(1)} %bitcast.9), custom_call_target="tpu_custom_call" | custom-call | bytes 12582912 | tf_op jit(solution)/shard_map/pallas_call | solution.py:345
  59.2 0.0 copy-start.1
  59.2 2.5 %copy-done.1 = bf16[720,4096]{1,0:T(8,128)(2,1)} copy-done((bf16[720,4096]{1,0:T(8,128)(2,1)}, bf16[720,4096]{1,0:T(8,128)(2,1)S(1)}, u32[]{:S(2)}) %copy-start.1) | copy-done | bytes 5898264
  61.7 24.5 %all-to-all-done.1.recv_ref = bf16[16,528,128]{2,1,0:T(8,128)(2,1)S(1)} async-done(((bf16[16,528,128]{2,1,0:T(8,128)(2,1)}), bf16[16,528,128]{2,1,0:T(8,128)(2,1)S(1)}, u32[]{:S(2)}, u32[]{:S(2)}) %all-to-all-start.1) | async-done | bytes 2162720 | tf_op jit(solution)/shard_map/all_to_all | solution.py:364
  86.2 0.0 copy-start.2
  86.2 2.7 %copy-done.2 = bf16[720,4096]{1,0:T(8,128)(2,1)S(1)} copy-done((bf16[720,4096]{1,0:T(8,128)(2,1)S(1)}, bf16[720,4096]{1,0:T(8,128)(2,1)}, u32[]{:S(2)}) %copy-start.2) | copy-done | bytes 5898264
  88.9 2.1 %shard_map.62 = (bf16[256,4352]{1,0:T(8,128)(2,1)S(1)}, f32[240,768]{1,0:T(8,128)S(1)}, f32[8,128]{1,0:T(8,128)S(1)}) custom-call(bf16[16,528,128]{2,1,0:T(8,128)(2,1)S(1)} %all-to-all-done.1.recv_ref, bf16[720,4096]{1,0:T(8,128)(2,1)S(1)} %copy-done.2, f32[80,128]{1,0:T(8,128)S(1)} %get-tuple-element.12.half_ref), custom_call_target="tpu_custom_call" | custom-call | flops 1509949440 | bytes 10485760 | tf_op jit(solution)/shard_map/pallas_call | solution.py:366
  91.0 9.3 %all_to_all.20 = f32[8,8,128]{2,1,0:T(8,128)S(1)} all-to-all(f32[8,8,128]{2,1,0:T(8,128)S(1)} %broadcast_in_dim.17), channel_id=1, replica_groups=mesh['z'=8,'xy'=16,'dp'=2] {'z'}, dimensions={0} | all-to-all | bytes 65536 | tf_op jit(solution)/shard_map/all_to_all | solution.py:378
  100.4 12.2 %all_to_all.21 = f32[16,64,128]{2,1,0:T(8,128)S(1)} all-to-all(f32[16,64,128]{2,1,0:T(8,128)S(1)} %broadcast_in_dim.19), channel_id=1, replica_groups=mesh['z'=8,'xy'=16,'dp'=2] {'xy'}, dimensions={0} | all-to-all | bytes 1048576 | tf_op jit(solution)/shard_map/all_to_all | solution.py:380
  112.6 2.2 %shard_map.63 = (f32[40,4224]{1,0:T(8,128)S(1)}, f32[40,4224]{1,0:T(8,128)S(1)}) custom-call(f32[240,768]{1,0:T(8,128)S(1)} %get-tuple-element.13.s_ref, bf16[256,4352]{1,0:T(8,128)(2,1)S(1)} %get-tuple-element.14.x_ref, f32[8,128]{1,0:T(8,128)S(1)} %get-tuple-element.15.mine_ref, f32[1024,128]{1,0:T(8,128)S(1)} %bitcast.10), custom_call_target="tpu_custom_call" | custom-call | flops 1509949440 | bytes 5242880 | tf_op jit(solution)/shard_map/pallas_call | solution.py:382
  114.8 4.2 %collective-permute-start = (f32[40,4224]{1,0:T(8,128)S(1)}, f32[40,4224]{1,0:T(8,128)S(1)}, u32[]{:S(2)}, u32[]{:S(2)}) collective-permute-start(f32[40,4224]{1,0:T(8,128)S(1)} %get-tuple-element.17), channel_id=1, source_target_pairs={{0,1},{1,0},{2,3},{3,2},{4,5},{5,4},{6,7},{7,6},{8,9},{9,8},{10,11... | collective-permute-start | bytes 2027528 | tf_op jit(solution)/shard_map/ppermute | solution.py:394
  119.0 1.8 %collective-permute-done.other_ref = f32[40,4224]{1,0:T(8,128)S(1)} collective-permute-done((f32[40,4224]{1,0:T(8,128)S(1)}, f32[40,4224]{1,0:T(8,128)S(1)}, u32[]{:S(2)}, u32[]{:S(2)}) %collective-permute-start) | collective-permute-done | bytes 675872 | tf_op jit(solution)/shard_map/ppermute | solution.py:394
  120.7 1.5 %shard_map.64 = (f32[1152,128]{1,0:T(8,128)}, f32[1,36]{1,0:T(1,128)}) custom-call(f32[40,4224]{1,0:T(8,128)S(1)} %get-tuple-element.16.keep_ref, f32[40,4224]{1,0:T(8,128)S(1)} %collective-permute-done.other_ref), custom_call_target="tpu_custom_call" | custom-call | bytes 2097152 | tf_op jit(solution)/shard_map/pallas_call | solution.py:395
  (3 shorter events, 0.1 us)
Async XLA Ops:
  1.4 0.9 copy-start.3
  2.3 0.7 copy-start.4
  4.4 9.2 %copy-start.5 = (bf16[1,72,4096]{2,1,0:T(8,128)(2,1)S(1)}, bf16[1,72,4096]{2,1,0:T(8,128)(2,1)}, u32[]{:S(2)}) copy-start(bf16[1,72,4096]{2,1,0:T(8,128)(2,1)} %param.5) | copy-start | bytes 1769476
  4.4 40.5 %all-to-all-start = ((bf16[8,560,128]{2,1,0:T(8,128)(2,1)}), bf16[8,560,128]{2,1,0:T(8,128)(2,1)S(1)}, u32[]{:S(2)}, u32[]{:S(2)}) async-start(bf16[8,560,128]{2,1,0:T(8,128)(2,1)} %shard_map.59), calls=%async_computation | async-start | bytes 2293760 | tf_op jit(solution)/shard_map/all_to_all | solution.py:333
  45.7 1.4 %copy-start = (bf16[16,528,128]{2,1,0:T(8,128)(2,1)}, bf16[16,528,128]{2,1,0:T(8,128)(2,1)S(1)}, u32[]{:S(2)}) copy-start(bf16[16,528,128]{2,1,0:T(8,128)(2,1)S(1)} %shard_map.60) | copy-start | bytes 6488068
  47.0 39.2 %all-to-all-start.1 = ((bf16[16,528,128]{2,1,0:T(8,128)(2,1)}), bf16[16,528,128]{2,1,0:T(8,128)(2,1)S(1)}, u32[]{:S(2)}, u32[]{:S(2)}) async-start(bf16[16,528,128]{2,1,0:T(8,128)(2,1)} %copy-done), calls=%async_computation.1 | async-start | bytes 4325376 | tf_op jit(solution)/shard_map/all_to_all | solution.py:364
  59.2 2.5 %copy-start.1 = (bf16[720,4096]{1,0:T(8,128)(2,1)}, bf16[720,4096]{1,0:T(8,128)(2,1)S(1)}, u32[]{:S(2)}) copy-start(bf16[720,4096]{1,0:T(8,128)(2,1)S(1)} %get-tuple-element.11.shifted_ref) | copy-start | bytes 17694724
  86.2 2.7 %copy-start.2 = (bf16[720,4096]{1,0:T(8,128)(2,1)S(1)}, bf16[720,4096]{1,0:T(8,128)(2,1)}, u32[]{:S(2)}) copy-start(bf16[720,4096]{1,0:T(8,128)(2,1)} %copy-done.1) | copy-start | bytes 17694724
  114.8 5.9 %collective-permute-start = (f32[40,4224]{1,0:T(8,128)S(1)}, f32[40,4224]{1,0:T(8,128)S(1)}, u32[]{:S(2)}, u32[]{:S(2)}) collective-permute-start(f32[40,4224]{1,0:T(8,128)S(1)} %get-tuple-element.17), channel_id=1, source_target_pairs={{0,1},{1,0},{2,3},{3,2},{4,5},{5,4},{6,7},{7,6},{8,9},{9,8},{10,11... | collective-permute-start | bytes 2027528 | tf_op jit(solution)/shard_map/ppermute | solution.py:394
where the time goes:
time: 123 us; the launch traced here: 122 us
  waiting for transfers between devices  57.5 us (47%)
  blocking collectives  21.6 us (18%)
  starting transfers between devices  20.1 us (16%)
  Pallas kernels  11 us (9%)
  local copies, waits for them, and re-layouts  10.4 us (8%)
    all_to_all x1, waiting for transfers between devices, on_device(): column = exchange(packed, 'z')  31.2 us
    all_to_all x1, waiting for transfers between devices, on_device(): received = exchange(picked, 'xy')  24.5 us
    all_to_all x1, blocking collectives, on_device(): exchange(jnp.broadcast_to(by_plane, (owners, planes * 8, LANES)), 'xy')  12.2 us
    all_to_all x1, blocking collectives, on_device(): by_plane = exchange(jnp.broadcast_to(tile[None], (planes, 8, LANES)), 'z')  9.34 us
    all_to_all x1, starting transfers between devices, on_device(): column = exchange(packed, 'z')  9.15 us
    unnamed x13, local copies, waits for them, and re-layouts  8.87 us
    all_to_all x1, starting transfers between devices, on_device(): received = exchange(picked, 'xy')  6.75 us
    ppermute x1, starting transfers between devices, on_device(): other = lax.ppermute(give, 'dp', [(0, 1), (1, 0)])  4.16 us
  transfers between devices with their start and end apart: 3, of which 3 were waited for; matrix products, arithmetic and copies ran while one was open for 2% of the time, Pallas kernels for 2%

commit v1 on v0

--- a/solution.py
+++ b/solution.py
@@ -43,72 +43,75 @@
     return jnp.where(low, pltpu.roll(load(first), half, 1), load(first + 1))
 
 
-def pack_kernel(cand_ref, noise_ref, img_ref, send_ref, hold_ref):
-    rows, top = cand_ref.shape
-    planes, depth, _ = send_ref.shape
+def pack_kernel(cand_ref, noise_ref, img_ref, send_ref):
+    top, rows = cand_ref.shape
     tiles = img_ref.shape[1] // LANES
     low = lane_row() < LANES // 2
+    row_id = lax.broadcasted_iota(jnp.int32, (rows, LANES), 0)
+    lane_id = lax.broadcasted_iota(jnp.int32, (rows, LANES), 1)
+    diagonal = lax.broadcasted_iota(jnp.int32, (rows, rows), 0) == lax.broadcasted_iota(
+        jnp.int32, (rows, rows), 1
+    )
+    noise = jnp.sum(
+        jnp.where(diagonal, noise_ref[...].astype(F32), 0.0), axis=1, keepdims=True
+    )
+    place = lax.broadcasted_iota(jnp.int32, (top, LANES), 1) == (
+        lax.broadcasted_iota(jnp.int32, (top, LANES), 0) + 2
+    )
+    facts = lax.dot_general(
+        cand_ref[...].astype(F32).astype(BF16),
+        place.astype(F32).astype(BF16),
+        (((0,), (0,)), ((), ())),
+        preferred_element_type=F32,
+    )
+    facts = jnp.where(lane_id == 0, noise, facts)
+    facts = jnp.where(lane_id == 1, (row_id + 1).astype(F32), facts)
+    send_ref[tiles * rows :] = facts.astype(BF16)
     for q in range(tiles):
         tile = fold_tile(lambda t: img_ref[:, tile_of(t)].astype(F32), q, tiles, low)
-        hold_ref[q * rows : (q + 1) * rows] = tile.astype(BF16)
-    row_id = lax.broadcasted_iota(jnp.int32, (rows, LANES), 0)
-    lane_id = lax.broadcasted_iota(jnp.int32, (rows, LANES), 1)
-    noise = jnp.sum(
-        jnp.where(
-            lax.broadcasted_iota(jnp.int32, (rows, rows), 0)
-            == lax.broadcasted_iota(jnp.int32, (rows, rows), 1),
-            noise_ref[...].astype(F32),
-            0.0,
-        ),
-        axis=1,
-        keepdims=True,
-    )
-    facts = jnp.where(lane_id == 0, noise, 0.0)
-    facts = jnp.where(lane_id == 1, (row_id + 1).astype(F32), facts)
-    hold_ref[tiles * rows :] = facts.astype(BF16)
-    for plane in range(planes):
-        send_ref[plane, : (tiles + 1) * rows] = hold_ref[...]
-    named = [jnp.broadcast_to(cand_ref[:, k : k + 1], (rows, LANES)) for k in range(top)]
-    earlier = (
-        lax.broadcasted_iota(jnp.int32, (rows, rows), 0)
-        > lax.broadcasted_iota(jnp.int32, (rows, rows), 1)
-    ).astype(BF16)
-    group = SLOTS * planes
-    slot = (lane_id // planes) % SLOTS
-    from_here = lane_id % planes == lax.axis_index("z")
-    wide = depth // rows - tiles - 1
-    for plane in range(planes):
-        for part in range(wide):
-            first = (plane * wide + part) * (LANES // group)
-            cls = first + lane_id // group
-            member = named[0] == cls
-            for k in range(1, top):
-                member = member | (named[k] == cls)
-            before = jnp.dot(
-                earlier, member.astype(F32).astype(BF16), preferred_element_type=F32
-            )
-            pick = member & (before == slot.astype(F32)) & from_here
-            at = (tiles + 1 + part) * rows
-            send_ref[plane, at : at + rows] = pick.astype(F32).astype(BF16)
-
-
-def pick_kernel(recv_ref, send_ref, column_ref, pick_ref):
-    planes = recv_ref.shape[0]
+        send_ref[q * rows : (q + 1) * rows] = tile.astype(BF16)
+
+
+def pick_kernel(*refs, steps, top):
+    recv_refs, send_ref, column_ref = refs[: len(steps)], refs[-2], refs[-1]
+    planes = len(steps) - 1
     owners, depth, _ = send_ref.shape
     rows = column_ref.shape[0] // planes
     tiles = column_ref.shape[1] // LANES
-    wide = pick_ref.shape[1] // LANES
-    for z in range(planes):
+    group = depth // tiles
+    slots = owners * group
+    cut = recv_refs[-2].shape[0] // rows
+    for j in range(planes):
         for t in range(tiles):
-            column_ref[z * rows : (z + 1) * rows, tile_of(t)] = recv_ref[
-                z, t * rows : (t + 1) * rows
+            from_ref, at = recv_refs[j], t
+            if j == planes - 1 and t >= cut:
+                from_ref, at = recv_refs[j + 1], t - cut
+            column_ref[j * rows : (j + 1) * rows, tile_of(t)] = from_ref[
+                at * rows : (at + 1) * rows
             ]
-        for t in range(wide):
-            pick_ref[z * rows : (z + 1) * rows, tile_of(t)] = recv_ref[
-                z, (tiles + t) * rows : (tiles + t + 1) * rows
-            ]
-    pick = pick_ref[...].astype(F32).T.astype(BF16)
-    group = depth // tiles
+    count = planes * rows
+    facts = column_ref[:, tile_of(tiles - 1)].astype(F32)
+    here = lax.axis_index("z")
+    row = lax.broadcasted_iota(jnp.int32, (count, 1), 0)
+    sender = jnp.zeros((count, 1), jnp.int32)
+    for j in range(planes):
+        plane = lax.rem(here + steps[j] + planes, planes)
+        sender = jnp.where(row // rows == j, plane, sender)
+    lane = lax.broadcasted_iota(jnp.int32, (1, slots), 1)
+    cls = (here * owners + lane // group).astype(F32)
+    member = facts[:, 2:3] == cls
+    for k in range(1, top):
+        member = member | (facts[:, 2 + k : 3 + k] == cls)
+    one, other = (lax.broadcasted_iota(jnp.int32, (count, count), i) for i in range(2))
+    earlier = (one > other) & (one // rows == other // rows)
+    before = jnp.dot(
+        earlier.astype(F32).astype(BF16),
+        member.astype(F32).astype(BF16),
+        preferred_element_type=F32,
+    )
+    slot = (lane // planes) % SLOTS
+    pick = member & (before == slot.astype(F32)) & (lane % planes == sender)
+    pick = pick.astype(F32).T.astype(BF16)
     width = 3
     for t in range(0, tiles, width):
         lanes = slice(t * LANES, (t + width) * LANES)
@@ -120,8 +123,20 @@
                 ]
 
 
-def shift_kernel(rot_ref, out_ref, half_ref):
+def shift_kernel(from_ref, out_ref, half_ref, rot_ref):
     count, pixels = rot_ref.shape
+    rots = from_ref.shape[0]
+    half_count, half_rots = count // 2, rots // 2
+    to = lax.broadcasted_iota(jnp.int32, (count, rots), 0)
+    place = jnp.where(to < half_count, to, to - half_count + half_rots)
+    real = to % half_count < half_rots
+    place = jnp.where(place < rots, place, 0)
+    own_first = lax.axis_index("dp") * half_rots
+    place = jnp.where(place + own_first < rots, place + own_first, place + own_first - rots)
+    chosen = (place == lax.broadcasted_iota(jnp.int32, (count, rots), 1)) & real
+    rot_ref[...] = jnp.dot(
+        chosen.astype(F32).astype(BF16), from_ref[...], preferred_element_type=F32
+    )
     tiles = pixels // LANES
     side = LANES // 2
     groups = len(COL_SHIFTS) * count
@@ -130,7 +145,7 @@
     column = lane % side
     square = jnp.zeros((count, LANES), F32)
     for q in range(tiles):
-        tile = fold_tile(lambda t: rot_ref[:, tile_of(t)].astype(F32), q, tiles, low)
+        tile = fold_tile(lambda t: rot_ref[:, tile_of(t)], q, tiles, low)
         square = square + tile * tile
         right = jnp.where(
             column == 0, pltpu.roll(tile, LANES - side + 1, 1), pltpu.roll(tile, 1, 1)
@@ -296,12 +311,12 @@
     totals_ref[...] = jnp.sum(jnp.where(here, total, 0.0), axis=0, keepdims=True)[:, :rots]
 
 
-def call(kernel, out_shape, count, limit, scratch=(), flops=0, moved=0):
+def call(kernel, out_shape, count, limit, scratch=(), flops=0, moved=0, space=pltpu.VMEM):
     in_vmem = pl.BlockSpec(memory_space=pltpu.VMEM)
     return pl.pallas_call(
         kernel,
         out_shape=out_shape,
-        in_specs=[in_vmem] * count,
+        in_specs=[pl.BlockSpec(memory_space=space)] * count,
         out_specs=jax.tree.map(lambda _: in_vmem, out_shape),
         scratch_shapes=list(scratch),
         cost_estimate=pl.CostEstimate(flops=flops, bytes_accessed=moved, transcendentals=0),
@@ -318,49 +333,54 @@
     group = SLOTS * planes
     slots = owners * group
     assert cls_dev == 1 and planes == PLANES and LANES == 2 * side and rows == group
-    wide = slots // LANES
     shape = jax.ShapeDtypeStruct
     exchange = functools.partial(lax.all_to_all, split_axis=0, concat_axis=0, tiled=True)
 
     packed = call(
         pack_kernel,
-        shape((planes, (tiles + 1 + wide) * rows, LANES), BF16),
+        shape(((tiles + 1) * rows, LANES), BF16),
         3,
-        8,
-        [pltpu.VMEM(((tiles + 1) * rows, LANES), BF16)],
-        moved=2 * MIB,
-    )(candidates, inv_noise[None, :], images)
-    column = exchange(packed, "z")
+        4,
+        moved=MIB // 4,
+    )(candidates.T, inv_noise[None, :], images)
+    up = [(i, (i + 1) % planes) for i in range(planes)]
+    down = [((i + 1) % planes, i) for i in range(planes)]
+    rising = falling = packed
+    column, steps = [packed], [0]
+    for step in range(1, planes // 2):
+        rising = lax.ppermute(rising, "z", up)
+        falling = lax.ppermute(falling, "z", down)
+        column += [rising, falling]
+        steps += [-step, step]
+    cut = (tiles + 1) // 2 * rows
+    column += [
+        lax.ppermute(rising[:cut], "z", up),
+        lax.ppermute(falling[cut:], "z", down),
+    ]
+    steps += [planes // 2] * 2
 
     half_rots = rots // 2
     half_count = -(-half_rots // 8) * 8
-    own = references[0]
-    flipped = jnp.where(
-        lax.axis_index("dp") == 0, own, jnp.concatenate([own[half_rots:], own[:half_rots]], axis=0)
-    )
     pad = half_count - half_rots
-    padded = jnp.pad(flipped.reshape(2, half_rots, pixels), ((0, 0), (0, pad), (0, 0)))
     count = 2 * half_count
     groups = len(COL_SHIFTS) * count
     shifted, half_norm = call(
         shift_kernel,
         (shape((len(ROW_SHIFTS) * groups, pixels), BF16), shape((count, LANES), F32)),
         1,
-        12,
+        6,
+        [pltpu.VMEM((count, pixels), F32)],
         moved=12 * MIB,
-    )(padded.reshape(count, pixels))
-
+    )(references[0])
+    column, shifted, half_norm = lax.optimization_barrier((column, shifted, half_norm))
     picked = call(
-        pick_kernel,
+        functools.partial(pick_kernel, steps=steps, top=top),
         shape((owners, (tiles + 1) * group, LANES), BF16),
-        1,
-        12,
-        [
-            pltpu.VMEM((planes * rows, (tiles + 1) * LANES), BF16),
-            pltpu.VMEM((planes * rows, slots), BF16),
-        ],
+        len(column),
+        6,
+        [pltpu.VMEM((planes * rows, (tiles + 1) * LANES), BF16)],
         moved=3 * MIB,
-    )(column)
+    )(*column)
     received = exchange(picked, "xy")
     work = 2 * len(ROW_SHIFTS) * groups * slots * pixels
     x, scores, tile = call(
@@ -371,7 +391,7 @@
             shape((8, LANES), F32),
         ),
         3,
-        24,
+        8,
         flops=work,
         moved=10 * MIB,
     )(received, shifted, half_norm)
@@ -383,7 +403,7 @@
         sum_kernel,
         (half_shape, half_shape),
         4,
-        24,
+        8,
         [
             pltpu.VMEM((groups, len(ROW_SHIFTS) * slots), BF16),
             pltpu.VMEM((groups, 4 * LANES), F32),

time: 123 us -> 101 us (0.82)
  waiting for transfers between devices: 57.5 us -> 8.45 us
  blocking collectives: 21.6 us -> 53.2 us
  local copies, waits for them, and re-layouts: 10.4 us -> 3.36 us
  starting transfers between devices: 20.1 us -> 24.7 us
    all_to_all x2 -> x0, waiting for transfers between devices: 55.7 us -> none  [the longest x1 31.2 us: on_device(): column = exchange(packed, 'z')]
    all_to_all x0 -> x1, blocking collectives: none -> 30.4 us  [on_device(): received = exchange(picked, 'xy')]
    ppermute x0 -> x8, starting transfers between devices: none -> 16.1 us  [the longest x3 12.9 us: on_device(): falling = lax.ppermute(falling, 'z', down)]
    all_to_all x2 -> x0, starting transfers between devices: 15.9 us -> none  [the longest x1 9.15 us: on_device(): column = exchange(packed, 'z')]
    ppermute x0 -> x8, waiting for transfers between devices: none -> 6.7 us  [the longest x3 6.21 us: on_device(): falling = lax.ppermute(falling, 'z', down)]
    unnamed x13 -> x8, local copies, waits for them, and re-layouts: 8.87 us -> 3.3 us
    ppermute x1, starting transfers between devices: 4.16 us -> 8.6 us  [on_device(): other = lax.ppermute(give, 'dp', [(0, 1), (1, 0)])]
    all_to_all x1, blocking collectives: 9.34 us -> 11 us  [on_device(): by_plane = exchange(jnp.broadcast_to(tile[None], (planes, 8, LANES)), 'z')]
  transfers between devices with their start and end apart: 3 -> 9, of which waited for: 3 -> 5; matrix products, arithmetic and copies ran while one was open for 2% -> 0% of each run, Pallas kernels for 2% -> 3%
where the time goes in v1:
time: 101 us; the launch traced here: 100 us
  blocking collectives  53.2 us (53%)
  starting transfers between devices  24.7 us (24%)
  Pallas kernels  10 us (10%)
  waiting for transfers between devices  8.45 us (8%)
  local copies, waits for them, and re-layouts  3.36 us (3%)
    all_to_all x1, blocking collectives, on_device(): received = exchange(picked, 'xy')  30.4 us
    ppermute x3, starting transfers between devices, on_device(): falling = lax.ppermute(falling, 'z', down)  12.9 us
    all_to_all x1, blocking collectives, on_device(): exchange(jnp.broadcast_to(by_plane, (owners, planes * 8, LANES)), 'xy')  11.8 us
    all_to_all x1, blocking collectives, on_device(): by_plane = exchange(jnp.broadcast_to(tile[None], (planes, 8, LANES)), 'z')  11 us
    ppermute x1, starting transfers between devices, on_device(): other = lax.ppermute(give, 'dp', [(0, 1), (1, 0)])  8.6 us
    ppermute x3, waiting for transfers between devices, on_device(): falling = lax.ppermute(falling, 'z', down)  6.21 us
    unnamed x8, local copies, waits for them, and re-layouts  3.3 us
    ppermute x1, starting transfers between devices, on_device(): lax.ppermute(falling[cut:], 'z', down)  3.09 us
  transfers between devices with their start and end apart: 9, of which 5 were waited for; matrix products, arithmetic and copies ran while one was open for 0% of the time, Pallas kernels for 3%

profile of v1, /device:TPU:1, one launch (start us, length us, event | category | flops | bytes accessed | tf_op | source)
XLA Modules:
  0.0 100.4 jit_solution(8834544349143162450)
XLA Ops:
  0.6 0.0 copy-start.1
  0.6 0.9 copy-done.1
  1.5 0.0 copy-start.2
  1.5 0.7 copy-done.2
  2.2 0.0 copy-start.3
  2.2 0.7 copy-done.3
  2.9 0.2 shard_map.59.refs_0_
  3.0 6.4 %collective-permute-start.1 = (bf16[528,128]{1,0:T(8,128)(2,1)S(1)}, bf16[528,128]{1,0:T(8,128)(2,1)S(1)}, u32[]{:S(2)}, u32[]{:S(2)}) collective-permute-start(bf16[528,128]{1,0:T(8,128)(2,1)S(1)} %shard_map.59.refs_0_), channel_id=1, source_target_pairs={{32,0},{64,32},{96,64},{128,96},{160,128},{192,160},{224,192},{0,2... | collective-permute-start | bytes 405512 | tf_op jit(solution)/shard_map/ppermute | solution.py:352
  9.5 0.0 collective-permute-start
  9.5 2.2 %collective-permute-done.1.refs_2_ = bf16[528,128]{1,0:T(8,128)(2,1)S(1)} collective-permute-done((bf16[528,128]{1,0:T(8,128)(2,1)S(1)}, bf16[528,128]{1,0:T(8,128)(2,1)S(1)}, u32[]{:S(2)}, u32[]{:S(2)}) %collective-permute-start.1) | collective-permute-done | bytes 135200 | tf_op jit(solution)/shard_map/ppermute | solution.py:352
  11.7 3.4 %collective-permute-start.3 = (bf16[528,128]{1,0:T(8,128)(2,1)S(1)}, bf16[528,128]{1,0:T(8,128)(2,1)S(1)}, u32[]{:S(2)}, u32[]{:S(2)}) collective-permute-start(bf16[528,128]{1,0:T(8,128)(2,1)S(1)} %collective-permute-done.1.refs_2_), channel_id=1, source_target_pairs={{32,0},{64,32},{96,64},{128,96},{160,128},{192,160},{224,192},{0,2... | collective-permute-start | bytes 405512 | tf_op jit(solution)/shard_map/ppermute | solution.py:352
  15.2 0.0 collective-permute-done.refs_1_
  15.2 0.0 collective-permute-start.2
  15.2 2.0 %collective-permute-done.3.refs_4_ = bf16[528,128]{1,0:T(8,128)(2,1)S(1)} collective-permute-done((bf16[528,128]{1,0:T(8,128)(2,1)S(1)}, bf16[528,128]{1,0:T(8,128)(2,1)S(1)}, u32[]{:S(2)}, u32[]{:S(2)}) %collective-permute-start.3) | collective-permute-done | bytes 135200 | tf_op jit(solution)/shard_map/ppermute | solution.py:352
  17.1 3.1 %collective-permute-start.5 = (bf16[528,128]{1,0:T(8,128)(2,1)S(1)}, bf16[528,128]{1,0:T(8,128)(2,1)S(1)}, u32[]{:S(2)}, u32[]{:S(2)}) collective-permute-start(bf16[528,128]{1,0:T(8,128)(2,1)S(1)} %collective-permute-done.3.refs_4_), channel_id=1, source_target_pairs={{32,0},{64,32},{96,64},{128,96},{160,128},{192,160},{224,192},{0,2... | collective-permute-start | bytes 405512 | tf_op jit(solution)/shard_map/ppermute | solution.py:352
  20.2 0.0 collective-permute-done.2.refs_3_
  20.2 0.0 collective-permute-start.4
  20.2 2.0 %collective-permute-done.5.refs_6_ = bf16[528,128]{1,0:T(8,128)(2,1)S(1)} collective-permute-done((bf16[528,128]{1,0:T(8,128)(2,1)S(1)}, bf16[528,128]{1,0:T(8,128)(2,1)S(1)}, u32[]{:S(2)}, u32[]{:S(2)}) %collective-permute-start.5) | collective-permute-done | bytes 135200 | tf_op jit(solution)/shard_map/ppermute | solution.py:352
  22.2 3.1 %collective-permute-start.7 = (bf16[272,128]{1,0:T(8,128)(2,1)S(1)}, bf16[272,128]{1,0:T(8,128)(2,1)S(1)}, u32[]{:S(2)}, u32[]{:S(2)}) collective-permute-start(bf16[272,128]{1,0:T(8,128)(2,1)S(1)} %slice.9), channel_id=1, source_target_pairs={{32,0},{64,32},{96,64},{128,96},{160,128},{192,160},{224,192},{0,2... | collective-permute-start | bytes 208904 | tf_op jit(solution)/shard_map/ppermute | solution.py:358
  25.3 0.0 collective-permute-done.4.refs_5_
  25.3 0.1 collective-permute-start.6
  25.4 0.0 copy-start
  25.4 1.1 %copy-done = bf16[1,72,4096]{2,1,0:T(8,128)(2,1)S(1)} copy-done((bf16[1,72,4096]{2,1,0:T(8,128)(2,1)S(1)}, bf16[1,72,4096]{2,1,0:T(8,128)(2,1)}, u32[]{:S(2)}) %copy-start) | copy-done | bytes 589848
  26.5 2.8 %shard_map.60 = (bf16[720,4096]{1,0:T(8,128)(2,1)S(1)}, f32[80,128]{1,0:T(8,128)S(1)}) custom-call(bf16[72,4096]{1,0:T(8,128)(2,1)S(1)} %bitcast.6), custom_call_target="tpu_custom_call" | custom-call | bytes 12582912 | tf_op jit(solution)/shard_map/pallas_call | solution.py:367
  29.2 0.5 collective-permute-done.6.refs_7_
  29.7 0.0 collective-permute-done.7.refs_8_
  29.7 1.2 %shard_map.61 = bf16[16,528,128]{2,1,0:T(8,128)(2,1)S(1)} custom-call(bf16[528,128]{1,0:T(8,128)(2,1)S(1)} %shard_map.59.refs_0_, bf16[528,128]{1,0:T(8,128)(2,1)S(1)} %collective-permute-done.refs_1_, bf16[528,128]{1,0:T(8,128)(2,1)S(1)} %collective-permute-done.1.refs_2_, bf16[528,128]{1,0:T(8,128)(2,1)S(1)} %collective-permute-done.2.refs_3_, ...), custom_call_target="tpu_custom_call" | custom-call | bytes 3145728 | tf_op jit(solution)/shard_map/pallas_call | solution.py:376
  30.9 30.4 %all_to_all.15.recv_ref = bf16[16,528,128]{2,1,0:T(8,128)(2,1)S(1)} all-to-all(bf16[16,528,128]{2,1,0:T(8,128)(2,1)S(1)} %shard_map.61), channel_id=1, replica_groups=mesh['z'=8,'xy'=16,'dp'=2] {'xy'}, dimensions={0} | all-to-all | bytes 4325376 | tf_op jit(solution)/shard_map/all_to_all | solution.py:384
  61.3 2.1 %shard_map.62 = (bf16[256,4352]{1,0:T(8,128)(2,1)S(1)}, f32[240,768]{1,0:T(8,128)S(1)}, f32[8,128]{1,0:T(8,128)S(1)}) custom-call(bf16[16,528,128]{2,1,0:T(8,128)(2,1)S(1)} %all_to_all.15.recv_ref, bf16[720,4096]{1,0:T(8,128)(2,1)S(1)} %get-tuple-element.33.shifted_ref, f32[80,128]{1,0:T(8,128)S(1)} %get-tuple-element.34.half_ref), custom_call_target="tpu_custom_call" | custom-call | flops 1509949440 | bytes 10485760 | tf_op jit(solution)/shard_map/pallas_call | solution.py:386
  63.4 11.0 %all_to_all.16 = f32[8,8,128]{2,1,0:T(8,128)S(1)} all-to-all(f32[8,8,128]{2,1,0:T(8,128)S(1)} %broadcast_in_dim.17), channel_id=1, replica_groups=mesh['z'=8,'xy'=16,'dp'=2] {'z'}, dimensions={0} | all-to-all | bytes 65536 | tf_op jit(solution)/shard_map/all_to_all | solution.py:398
  74.5 11.8 %all_to_all.17 = f32[16,64,128]{2,1,0:T(8,128)S(1)} all-to-all(f32[16,64,128]{2,1,0:T(8,128)S(1)} %broadcast_in_dim.19), channel_id=1, replica_groups=mesh['z'=8,'xy'=16,'dp'=2] {'xy'}, dimensions={0} | all-to-all | bytes 1048576 | tf_op jit(solution)/shard_map/all_to_all | solution.py:400
  86.2 2.3 %shard_map.63 = (f32[40,4224]{1,0:T(8,128)S(1)}, f32[40,4224]{1,0:T(8,128)S(1)}) custom-call(f32[240,768]{1,0:T(8,128)S(1)} %get-tuple-element.35.s_ref, bf16[256,4352]{1,0:T(8,128)(2,1)S(1)} %get-tuple-element.36.x_ref, f32[8,128]{1,0:T(8,128)S(1)} %get-tuple-element.37.mine_ref, f32[1024,128]{1,0:T(8,128)S(1)} %bitcast.7), custom_call_target="tpu_custom_call" | custom-call | flops 1509949440 | bytes 5242880 | tf_op jit(solution)/shard_map/pallas_call | solution.py:402
  88.6 8.6 %collective-permute-start.8 = (f32[40,4224]{1,0:T(8,128)S(1)}, f32[40,4224]{1,0:T(8,128)S(1)}, u32[]{:S(2)}, u32[]{:S(2)}) collective-permute-start(f32[40,4224]{1,0:T(8,128)S(1)} %get-tuple-element.39), channel_id=1, source_target_pairs={{0,1},{1,0},{2,3},{3,2},{4,5},{5,4},{6,7},{7,6},{8,9},{9,8},{10,11... | collective-permute-start | bytes 2027528 | tf_op jit(solution)/shard_map/ppermute | solution.py:414
  97.2 1.8 %collective-permute-done.8.other_ref = f32[40,4224]{1,0:T(8,128)S(1)} collective-permute-done((f32[40,4224]{1,0:T(8,128)S(1)}, f32[40,4224]{1,0:T(8,128)S(1)}, u32[]{:S(2)}, u32[]{:S(2)}) %collective-permute-start.8) | collective-permute-done | bytes 675872 | tf_op jit(solution)/shard_map/ppermute | solution.py:414
  98.9 1.5 %shard_map.64 = (f32[1152,128]{1,0:T(8,128)}, f32[1,36]{1,0:T(1,128)}) custom-call(f32[40,4224]{1,0:T(8,128)S(1)} %get-tuple-element.38.keep_ref, f32[40,4224]{1,0:T(8,128)S(1)} %collective-permute-done.8.other_ref), custom_call_target="tpu_custom_call" | custom-call | bytes 2097152 | tf_op jit(solution)/shard_map/pallas_call | solution.py:415
  (4 shorter events, 0.1 us)
Async XLA Ops:
  0.6 0.9 copy-start.1
  1.5 0.7 copy-start.2
  2.2 0.7 copy-start.3
  3.0 8.7 %collective-permute-start.1 = (bf16[528,128]{1,0:T(8,128)(2,1)S(1)}, bf16[528,128]{1,0:T(8,128)(2,1)S(1)}, u32[]{:S(2)}, u32[]{:S(2)}) collective-permute-start(bf16[528,128]{1,0:T(8,128)(2,1)S(1)} %shard_map.59.refs_0_), channel_id=1, source_target_pairs={{32,0},{64,32},{96,64},{128,96},{160,128},{192,160},{224,192},{0,2... | collective-permute-start | bytes 405512 | tf_op jit(solution)/shard_map/ppermute | solution.py:352
  9.5 5.7 %collective-permute-start = (bf16[528,128]{1,0:T(8,128)(2,1)S(1)}, bf16[528,128]{1,0:T(8,128)(2,1)S(1)}, u32[]{:S(2)}, u32[]{:S(2)}) collective-permute-start(bf16[528,128]{1,0:T(8,128)(2,1)S(1)} %shard_map.59.refs_0_), channel_id=1, source_target_pairs={{0,32},{32,64},{64,96},{96,128},{128,160},{160,192},{192,224},{224... | collective-permute-start | bytes 405512 | tf_op jit(solution)/shard_map/ppermute | solution.py:351
  11.7 5.4 %collective-permute-start.3 = (bf16[528,128]{1,0:T(8,128)(2,1)S(1)}, bf16[528,128]{1,0:T(8,128)(2,1)S(1)}, u32[]{:S(2)}, u32[]{:S(2)}) collective-permute-start(bf16[528,128]{1,0:T(8,128)(2,1)S(1)} %collective-permute-done.1.refs_2_), channel_id=1, source_target_pairs={{32,0},{64,32},{96,64},{128,96},{160,128},{192,160},{224,192},{0,2... | collective-permute-start | bytes 405512 | tf_op jit(solution)/shard_map/ppermute | solution.py:352
  15.2 5.1 %collective-permute-start.2 = (bf16[528,128]{1,0:T(8,128)(2,1)S(1)}, bf16[528,128]{1,0:T(8,128)(2,1)S(1)}, u32[]{:S(2)}, u32[]{:S(2)}) collective-permute-start(bf16[528,128]{1,0:T(8,128)(2,1)S(1)} %collective-permute-done.refs_1_), channel_id=1, source_target_pairs={{0,32},{32,64},{64,96},{96,128},{128,160},{160,192},{192,224},{224... | collective-permute-start | bytes 405512 | tf_op jit(solution)/shard_map/ppermute | solution.py:351
  17.1 5.1 %collective-permute-start.5 = (bf16[528,128]{1,0:T(8,128)(2,1)S(1)}, bf16[528,128]{1,0:T(8,128)(2,1)S(1)}, u32[]{:S(2)}, u32[]{:S(2)}) collective-permute-start(bf16[528,128]{1,0:T(8,128)(2,1)S(1)} %collective-permute-done.3.refs_4_), channel_id=1, source_target_pairs={{32,0},{64,32},{96,64},{128,96},{160,128},{192,160},{224,192},{0,2... | collective-permute-start | bytes 405512 | tf_op jit(solution)/shard_map/ppermute | solution.py:352
  20.2 5.1 %collective-permute-start.4 = (bf16[528,128]{1,0:T(8,128)(2,1)S(1)}, bf16[528,128]{1,0:T(8,128)(2,1)S(1)}, u32[]{:S(2)}, u32[]{:S(2)}) collective-permute-start(bf16[528,128]{1,0:T(8,128)(2,1)S(1)} %collective-permute-done.2.refs_3_), channel_id=1, source_target_pairs={{0,32},{32,64},{64,96},{96,128},{128,160},{160,192},{192,224},{224... | collective-permute-start | bytes 405512 | tf_op jit(solution)/shard_map/ppermute | solution.py:351
  22.2 7.5 %collective-permute-start.7 = (bf16[272,128]{1,0:T(8,128)(2,1)S(1)}, bf16[272,128]{1,0:T(8,128)(2,1)S(1)}, u32[]{:S(2)}, u32[]{:S(2)}) collective-permute-start(bf16[272,128]{1,0:T(8,128)(2,1)S(1)} %slice.9), channel_id=1, source_target_pairs={{32,0},{64,32},{96,64},{128,96},{160,128},{192,160},{224,192},{0,2... | collective-permute-start | bytes 208904 | tf_op jit(solution)/shard_map/ppermute | solution.py:358
  25.3 4.4 %collective-permute-start.6 = (bf16[256,128]{1,0:T(8,128)(2,1)S(1)}, bf16[256,128]{1,0:T(8,128)(2,1)S(1)}, u32[]{:S(2)}, u32[]{:S(2)}) collective-permute-start(bf16[256,128]{1,0:T(8,128)(2,1)S(1)} %slice.8), channel_id=1, source_target_pairs={{0,32},{32,64},{64,96},{96,128},{128,160},{160,192},{192,224},{224... | collective-permute-start | bytes 196616 | tf_op jit(solution)/shard_map/ppermute | solution.py:357
  25.4 1.1 %copy-start = (bf16[1,72,4096]{2,1,0:T(8,128)(2,1)S(1)}, bf16[1,72,4096]{2,1,0:T(8,128)(2,1)}, u32[]{:S(2)}) copy-start(bf16[1,72,4096]{2,1,0:T(8,128)(2,1)} %param.5) | copy-start | bytes 1769476
  88.6 10.4 %collective-permute-start.8 = (f32[40,4224]{1,0:T(8,128)S(1)}, f32[40,4224]{1,0:T(8,128)S(1)}, u32[]{:S(2)}, u32[]{:S(2)}) collective-permute-start(f32[40,4224]{1,0:T(8,128)S(1)} %get-tuple-element.39), channel_id=1, source_target_pairs={{0,1},{1,0},{2,3},{3,2},{4,5},{5,4},{6,7},{7,6},{8,9},{9,8},{10,11... | collective-permute-start | bytes 2027528 | tf_op jit(solution)/shard_map/ppermute | solution.py:414

commit v2 on v1

--- a/solution.py
+++ b/solution.py
@@ -43,8 +43,9 @@
     return jnp.where(low, pltpu.roll(load(first), half, 1), load(first + 1))
 
 
-def pack_kernel(cand_ref, noise_ref, img_ref, send_ref):
+def pack_kernel(cand_ref, noise_ref, img_ref, send_ref, late_ref):
     top, rows = cand_ref.shape
+    early = send_ref.shape[0] // rows
     tiles = img_ref.shape[1] // LANES
     low = lane_row() < LANES // 2
     row_id = lax.broadcasted_iota(jnp.int32, (rows, LANES), 0)
@@ -66,26 +67,27 @@
     )
     facts = jnp.where(lane_id == 0, noise, facts)
     facts = jnp.where(lane_id == 1, (row_id + 1).astype(F32), facts)
-    send_ref[tiles * rows :] = facts.astype(BF16)
+    late_ref[(tiles - early) * rows :] = facts.astype(BF16)
     for q in range(tiles):
         tile = fold_tile(lambda t: img_ref[:, tile_of(t)].astype(F32), q, tiles, low)
-        send_ref[q * rows : (q + 1) * rows] = tile.astype(BF16)
+        to_ref, at = (send_ref, q) if q < early else (late_ref, q - early)
+        to_ref[at * rows : (at + 1) * rows] = tile.astype(BF16)
 
 
 def pick_kernel(*refs, steps, top):
-    recv_refs, send_ref, column_ref = refs[: len(steps)], refs[-2], refs[-1]
-    planes = len(steps) - 1
+    planes = len(steps)
+    recv_refs, send_ref, column_ref = refs[: 2 * planes], refs[-2], refs[-1]
     owners, depth, _ = send_ref.shape
     rows = column_ref.shape[0] // planes
     tiles = column_ref.shape[1] // LANES
     group = depth // tiles
     slots = owners * group
-    cut = recv_refs[-2].shape[0] // rows
+    cut = recv_refs[0].shape[0] // rows
     for j in range(planes):
         for t in range(tiles):
-            from_ref, at = recv_refs[j], t
-            if j == planes - 1 and t >= cut:
-                from_ref, at = recv_refs[j + 1], t - cut
+            from_ref, at = recv_refs[2 * j], t
+            if t >= cut:
+                from_ref, at = recv_refs[2 * j + 1], t - cut
             column_ref[j * rows : (j + 1) * rows, tile_of(t)] = from_ref[
                 at * rows : (at + 1) * rows
             ]
@@ -130,41 +132,42 @@
     to = lax.broadcasted_iota(jnp.int32, (count, rots), 0)
     place = jnp.where(to < half_count, to, to - half_count + half_rots)
     real = to % half_count < half_rots
-    place = jnp.where(place < rots, place, 0)
     own_first = lax.axis_index("dp") * half_rots
     place = jnp.where(place + own_first < rots, place + own_first, place + own_first - rots)
     chosen = (place == lax.broadcasted_iota(jnp.int32, (count, rots), 1)) & real
-    rot_ref[...] = jnp.dot(
-        chosen.astype(F32).astype(BF16), from_ref[...], preferred_element_type=F32
-    )
+    picked = jnp.dot(chosen.astype(F32).astype(BF16), from_ref[...], preferred_element_type=F32)
+    half = 0.5 * jnp.sum(picked * picked, axis=1, keepdims=True)
+    half_ref[...] = jnp.broadcast_to(half, half_ref.shape)
+    rot_ref[...] = picked.astype(BF16)
     tiles = pixels // LANES
     side = LANES // 2
     groups = len(COL_SHIFTS) * count
-    lane = lane_row()
-    low = lane < side
-    column = lane % side
-    square = jnp.zeros((count, LANES), F32)
-    for q in range(tiles):
-        tile = fold_tile(lambda t: rot_ref[:, tile_of(t)], q, tiles, low)
-        square = square + tile * tile
-        right = jnp.where(
-            column == 0, pltpu.roll(tile, LANES - side + 1, 1), pltpu.roll(tile, 1, 1)
+    source = lax.broadcasted_iota(jnp.int32, (2 * LANES, LANES), 0)
+    lane = lax.broadcasted_iota(jnp.int32, (2 * LANES, LANES), 1)
+    moves = []
+    for parity in range(2):
+        for shift in COL_SHIFTS:
+            col = (lane - shift + side) % side
+            home = (lane // side) * LANES + parity * side + col
+            moves.append((source == home).astype(F32).astype(BF16))
+    moves = jnp.concatenate(moves, axis=1)
+    turn = ((lane[:LANES] + side) % LANES == source[:LANES]).astype(F32).astype(BF16)
+    for h in range(tiles // 2):
+        pair = jnp.concatenate(
+            [rot_ref[:, tile_of(h)], rot_ref[:, tile_of(tiles // 2 + h)]], axis=1
         )
-        left = jnp.where(
-            column == side - 1, pltpu.roll(tile, side - 1, 1), pltpu.roll(tile, LANES - 1, 1)
-        )
-        for i, moved in enumerate((tile, right, left)):
-            plain = moved.astype(BF16)
-            for j, shift in enumerate(ROW_SHIFTS):
-                to = q + shift
-                value = plain
-                if not 0 <= to < tiles:
-                    to = to % tiles
-                    value = pltpu.roll(moved, side, 1).astype(BF16)
-                at = j * groups + i * count
-                out_ref[at : at + count, tile_of(to)] = value
-    half = 0.5 * jnp.sum(square, axis=1, keepdims=True)
-    half_ref[...] = jnp.broadcast_to(half, half_ref.shape)
+        moved = jnp.dot(pair, moves, preferred_element_type=F32).astype(BF16)
+        for parity in range(2):
+            for i in range(len(COL_SHIFTS)):
+                plain = moved[:, tile_of(parity * len(COL_SHIFTS) + i)]
+                for j, shift in enumerate(ROW_SHIFTS):
+                    at = 2 * h + parity + shift
+                    value = plain
+                    if not 0 <= at < tiles:
+                        at = at % tiles
+                        value = jnp.dot(plain, turn, preferred_element_type=F32).astype(BF16)
+                    first = j * groups + i * count
+                    out_ref[first : first + count, tile_of(at)] = value
 
 
 def score_kernel(recv_ref, shifted_ref, half_ref, x_ref, s_ref, tile_ref, *, pad):
@@ -336,29 +339,21 @@
     shape = jax.ShapeDtypeStruct
     exchange = functools.partial(lax.all_to_all, split_axis=0, concat_axis=0, tiled=True)
 
+    cut = (tiles + 1) // 2
     packed = call(
         pack_kernel,
-        shape(((tiles + 1) * rows, LANES), BF16),
+        (shape((cut * rows, LANES), BF16), shape(((tiles + 1 - cut) * rows, LANES), BF16)),
         3,
-        4,
+        56,
         moved=MIB // 4,
     )(candidates.T, inv_noise[None, :], images)
     up = [(i, (i + 1) % planes) for i in range(planes)]
     down = [((i + 1) % planes, i) for i in range(planes)]
-    rising = falling = packed
-    column, steps = [packed], [0]
-    for step in range(1, planes // 2):
-        rising = lax.ppermute(rising, "z", up)
-        falling = lax.ppermute(falling, "z", down)
-        column += [rising, falling]
-        steps += [-step, step]
-    cut = (tiles + 1) // 2 * rows
-    column += [
-        lax.ppermute(rising[:cut], "z", up),
-        lax.ppermute(falling[cut:], "z", down),
-    ]
-    steps += [planes // 2] * 2
-
+
+    def move(parts, way):
+        return [lax.ppermute(part, "z", way) for part in parts]
+
+    rising, falling = move(packed, up), move(packed, down)
     half_rots = rots // 2
     half_count = -(-half_rots // 8) * 8
     pad = half_count - half_rots
@@ -369,10 +364,19 @@
         (shape((len(ROW_SHIFTS) * groups, pixels), BF16), shape((count, LANES), F32)),
         1,
         6,
-        [pltpu.VMEM((count, pixels), F32)],
+        [pltpu.VMEM((count, pixels), BF16)],
         moved=12 * MIB,
     )(references[0])
-    column, shifted, half_norm = lax.optimization_barrier((column, shifted, half_norm))
+    rising, falling, shifted, half_norm = lax.optimization_barrier(
+        (rising, falling, shifted, half_norm)
+    )
+    column, steps = [*packed, *rising, *falling], [0, -1, 1]
+    for step in range(2, planes // 2):
+        rising, falling = move(rising, up), move(falling, down)
+        column += [*rising, *falling]
+        steps += [-step, step]
+    column += [*move(rising[:1], up), *move(falling[1:], down)]
+    steps.append(planes // 2)
     picked = call(
         functools.partial(pick_kernel, steps=steps, top=top),
         shape((owners, (tiles + 1) * group, LANES), BF16),

time: 101 us -> 103 us (1.020)
  starting transfers between devices: 24.7 us -> 27.3 us
    ppermute x8 -> x14, starting transfers between devices: 16.1 us -> 18.1 us  [move(): return [lax.ppermute(part, 'z', way) for part in parts]]
    pallas_call x1, Pallas kernels: 0.17 us -> 1.74 us  [on_device(): call(pack_kernel, (shape((cut * rows, LANES), BF16), shape(((tiles + 1 -...]
    pallas_call x1, Pallas kernels: 2.77 us -> 1.59 us  [on_device(): call(shift_kernel, (shape((len(ROW_SHIFTS) * groups, pixels), BF16), shap...]
    ppermute x8 -> x14, waiting for transfers between devices: 6.7 us -> 7.61 us  [move(): return [lax.ppermute(part, 'z', way) for part in parts]]
    unnamed x8 -> x6, local copies, waits for them, and re-layouts: 3.3 us -> 2.79 us
  transfers between devices with their start and end apart: 9 -> 15, of which waited for: 5 -> 6; matrix products, arithmetic and copies ran while one was open for 0% -> 0% of each run, Pallas kernels for 3% -> 2%
where the time goes in v2:
time: 103 us
  blocking collectives  52.5 us (51%)
  starting transfers between devices  27.3 us (27%)
  Pallas kernels  10.4 us (10%)
  waiting for transfers between devices  9.37 us (9%)
  local copies, waits for them, and re-layouts  2.83 us (3%)
    all_to_all x1, blocking collectives, on_device(): received = exchange(picked, 'xy')  29.4 us
    ppermute x14, starting transfers between devices, move(): return [lax.ppermute(part, 'z', way) for part in parts]  18.1 us
    all_to_all x1, blocking collectives, on_device(): exchange(jnp.broadcast_to(by_plane, (owners, planes * 8, LANES)), 'xy')  12 us
    all_to_all x1, blocking collectives, on_device(): by_plane = exchange(jnp.broadcast_to(tile[None], (planes, 8, LANES)), 'z')  11.1 us
    ppermute x1, starting transfers between devices, on_device(): other = lax.ppermute(give, 'dp', [(0, 1), (1, 0)])  9.27 us
    ppermute x14, waiting for transfers between devices, move(): return [lax.ppermute(part, 'z', way) for part in parts]  7.61 us
    unnamed x6, local copies, waits for them, and re-layouts  2.79 us
    pallas_call x1, Pallas kernels, on_device(): call(sum_kernel, (half_shape, half_shape), 4, 8, [pltpu.VMEM((groups, len...  2.35 us
  transfers between devices with their start and end apart: 15, of which 6 were waited for; matrix products, arithmetic and copies ran while one was open for 0% of the time, Pallas kernels for 2%

profile of v2, /device:TPU:1, one launch (start us, length us, event | category | flops | bytes accessed | tf_op | source)
XLA Modules:
  0.0 103.1 jit_solution(4905656793438186303)
XLA Ops:
  0.6 1.7 %shard_map.59 = (bf16[256,128]{1,0:T(8,128)(2,1)}, bf16[272,128]{1,0:T(8,128)(2,1)}) custom-call(s32[8,16]{1,0:T(8,128)} %bitcast.9, bf16[1,16]{1,0:T(2,128)(2,1)} %bitcast.10, bf16[16,4096]{1,0:T(8,128)(2,1)} %img_ref.1), custom_call_target="tpu_custom_call" | custom-call | bytes 262144 | tf_op jit(solution)/shard_map/pallas_call | solution.py:343
  2.4 6.4 %collective-permute-start.3 = (bf16[272,128]{1,0:T(8,128)(2,1)}, bf16[272,128]{1,0:T(8,128)(2,1)S(1)}, u32[]{:S(2)}, u32[]{:S(2)}) collective-permute-start(bf16[272,128]{1,0:T(8,128)(2,1)} %get-tuple-element.20.refs_1_), channel_id=1, source_target_pairs={{32,0},{64,32},{96,64},{128,96},{160,128},{192,160},{224,192},{0,2... | collective-permute-start | bytes 208904 | tf_op jit(solution)/shard_map/ppermute | solution.py:354
  8.8 0.0 collective-permute-start.1
  8.8 2.7 %collective-permute-start.2 = (bf16[256,128]{1,0:T(8,128)(2,1)}, bf16[256,128]{1,0:T(8,128)(2,1)S(1)}, u32[]{:S(2)}, u32[]{:S(2)}) collective-permute-start(bf16[256,128]{1,0:T(8,128)(2,1)} %get-tuple-element.19.refs_0_), channel_id=1, source_target_pairs={{32,0},{64,32},{96,64},{128,96},{160,128},{192,160},{224,192},{0,2... | collective-permute-start | bytes 196616 | tf_op jit(solution)/shard_map/ppermute | solution.py:354
  11.5 0.0 collective-permute-start
  11.5 0.0 copy-start
  11.5 1.1 %copy-done = bf16[1,72,4096]{2,1,0:T(8,128)(2,1)S(1)} copy-done((bf16[1,72,4096]{2,1,0:T(8,128)(2,1)S(1)}, bf16[1,72,4096]{2,1,0:T(8,128)(2,1)}, u32[]{:S(2)}) %copy-start) | copy-done | bytes 589848
  12.5 1.6 %shard_map.60 = (bf16[720,4096]{1,0:T(8,128)(2,1)S(1)}, f32[80,128]{1,0:T(8,128)S(1)}) custom-call(bf16[72,4096]{1,0:T(8,128)(2,1)S(1)} %bitcast.6), custom_call_target="tpu_custom_call" | custom-call | bytes 12582912 | tf_op jit(solution)/shard_map/pallas_call | solution.py:362
  14.1 0.0 collective-permute-done.2.refs_4_
  14.1 1.9 %collective-permute-done.refs_2_ = bf16[256,128]{1,0:T(8,128)(2,1)S(1)} collective-permute-done((bf16[256,128]{1,0:T(8,128)(2,1)}, bf16[256,128]{1,0:T(8,128)(2,1)S(1)}, u32[]{:S(2)}, u32[]{:S(2)}) %collective-permute-start) | collective-permute-done | bytes 65568 | tf_op jit(solution)/shard_map/ppermute | solution.py:354
  16.0 0.0 collective-permute-done.3.refs_5_
  16.0 0.0 collective-permute-done.1.refs_3_
  16.0 0.9 collective-permute-start.7
  16.9 0.6 collective-permute-start.4
  17.5 0.0 collective-permute-start.5
  17.5 1.7 %collective-permute-done.7.refs_9_ = bf16[272,128]{1,0:T(8,128)(2,1)S(1)} collective-permute-done((bf16[272,128]{1,0:T(8,128)(2,1)S(1)}, bf16[272,128]{1,0:T(8,128)(2,1)S(1)}, u32[]{:S(2)}, u32[]{:S(2)}) %collective-permute-start.7) | collective-permute-done | bytes 69664 | tf_op jit(solution)/shard_map/ppermute | solution.py:354
  19.2 2.1 %collective-permute-start.11 = (bf16[272,128]{1,0:T(8,128)(2,1)S(1)}, bf16[272,128]{1,0:T(8,128)(2,1)S(1)}, u32[]{:S(2)}, u32[]{:S(2)}) collective-permute-start(bf16[272,128]{1,0:T(8,128)(2,1)S(1)} %collective-permute-done.7.refs_9_), channel_id=1, source_target_pairs={{32,0},{64,32},{96,64},{128,96},{160,128},{192,160},{224,192},{0,2... | collective-permute-start | bytes 208904 | tf_op jit(solution)/shard_map/ppermute | solution.py:354
  21.3 0.0 collective-permute-start.6
  21.3 0.0 collective-permute-done.4.refs_6_
  21.3 1.4 %collective-permute-start.8 = (bf16[256,128]{1,0:T(8,128)(2,1)S(1)}, bf16[256,128]{1,0:T(8,128)(2,1)S(1)}, u32[]{:S(2)}, u32[]{:S(2)}) collective-permute-start(bf16[256,128]{1,0:T(8,128)(2,1)S(1)} %collective-permute-done.4.refs_6_), channel_id=1, source_target_pairs={{0,32},{32,64},{64,96},{96,128},{128,160},{160,192},{192,224},{224... | collective-permute-start | bytes 196616 | tf_op jit(solution)/shard_map/ppermute | solution.py:354
  22.8 0.0 collective-permute-done.5.refs_7_
  22.8 0.1 collective-permute-start.9
  22.8 0.4 collective-permute-done.11.refs_13_
  23.3 2.4 %collective-permute-start.13 = (bf16[272,128]{1,0:T(8,128)(2,1)S(1)}, bf16[272,128]{1,0:T(8,128)(2,1)S(1)}, u32[]{:S(2)}, u32[]{:S(2)}) collective-permute-start(bf16[272,128]{1,0:T(8,128)(2,1)S(1)} %collective-permute-done.11.refs_13_), channel_id=1, source_target_pairs={{32,0},{64,32},{96,64},{128,96},{160,128},{192,160},{224,192},{0,2... | collective-permute-start | bytes 208904 | tf_op jit(solution)/shard_map/ppermute | solution.py:354
  25.7 0.0 collective-permute-done.6.refs_8_
  25.7 0.7 collective-permute-start.10
  26.4 0.0 collective-permute-done.8.refs_10_
  26.4 0.7 collective-permute-start.12
  27.1 1.9 %collective-permute-done.10.refs_12_ = bf16[256,128]{1,0:T(8,128)(2,1)S(1)} collective-permute-done((bf16[256,128]{1,0:T(8,128)(2,1)S(1)}, bf16[256,128]{1,0:T(8,128)(2,1)S(1)}, u32[]{:S(2)}, u32[]{:S(2)}) %collective-permute-start.10) | collective-permute-done | bytes 65568 | tf_op jit(solution)/shard_map/ppermute | solution.py:354
  29.1 0.0 collective-permute-done.9.refs_11_
  29.1 1.6 %collective-permute-done.12.refs_14_ = bf16[256,128]{1,0:T(8,128)(2,1)S(1)} collective-permute-done((bf16[256,128]{1,0:T(8,128)(2,1)S(1)}, bf16[256,128]{1,0:T(8,128)(2,1)S(1)}, u32[]{:S(2)}, u32[]{:S(2)}) %collective-permute-start.12) | collective-permute-done | bytes 65568 | tf_op jit(solution)/shard_map/ppermute | solution.py:354
  30.7 0.0 collective-permute-done.13.refs_15_
  30.7 0.0 copy-start.1
  30.7 0.9 copy-done.1
  31.6 0.0 copy-start.2
  31.6 0.8 copy-done.2
  32.5 1.2 %shard_map.61 = bf16[16,528,128]{2,1,0:T(8,128)(2,1)S(1)} custom-call(bf16[256,128]{1,0:T(8,128)(2,1)S(1)} %copy-done.2, bf16[272,128]{1,0:T(8,128)(2,1)S(1)} %copy-done.1, bf16[256,128]{1,0:T(8,128)(2,1)S(1)} %collective-permute-done.refs_2_, bf16[272,128]{1,0:T(8,128)(2,1)S(1)} %collective-permute-done.1.refs_3_, ...), custom_call_target="tpu_custom_call" | custom-call | bytes 3145728 | tf_op jit(solution)/shard_map/pallas_call | solution.py:380
  33.6 29.4 %all_to_all.15.recv_ref = bf16[16,528,128]{2,1,0:T(8,128)(2,1)S(1)} all-to-all(bf16[16,528,128]{2,1,0:T(8,128)(2,1)S(1)} %shard_map.61), channel_id=1, replica_groups=mesh['z'=8,'xy'=16,'dp'=2] {'xy'}, dimensions={0} | all-to-all | bytes 4325376 | tf_op jit(solution)/shard_map/all_to_all | solution.py:388
  63.0 2.1 %shard_map.62 = (bf16[256,4352]{1,0:T(8,128)(2,1)S(1)}, f32[240,768]{1,0:T(8,128)S(1)}, f32[8,128]{1,0:T(8,128)S(1)}) custom-call(bf16[16,528,128]{2,1,0:T(8,128)(2,1)S(1)} %all_to_all.15.recv_ref, bf16[720,4096]{1,0:T(8,128)(2,1)S(1)} %get-tuple-element.27.shifted_ref, f32[80,128]{1,0:T(8,128)S(1)} %get-tuple-element.28.half_ref), custom_call_target="tpu_custom_call" | custom-call | flops 1509949440 | bytes 10485760 | tf_op jit(solution)/shard_map/pallas_call | solution.py:390
  65.1 11.1 %all_to_all.16 = f32[8,8,128]{2,1,0:T(8,128)S(1)} all-to-all(f32[8,8,128]{2,1,0:T(8,128)S(1)} %broadcast_in_dim.17), channel_id=1, replica_groups=mesh['z'=8,'xy'=16,'dp'=2] {'z'}, dimensions={0} | all-to-all | bytes 65536 | tf_op jit(solution)/shard_map/all_to_all | solution.py:402
  76.3 12.0 %all_to_all.17 = f32[16,64,128]{2,1,0:T(8,128)S(1)} all-to-all(f32[16,64,128]{2,1,0:T(8,128)S(1)} %broadcast_in_dim.19), channel_id=1, replica_groups=mesh['z'=8,'xy'=16,'dp'=2] {'xy'}, dimensions={0} | all-to-all | bytes 1048576 | tf_op jit(solution)/shard_map/all_to_all | solution.py:404
  88.3 2.3 %shard_map.63 = (f32[40,4224]{1,0:T(8,128)S(1)}, f32[40,4224]{1,0:T(8,128)S(1)}) custom-call(f32[240,768]{1,0:T(8,128)S(1)} %get-tuple-element.29.s_ref, bf16[256,4352]{1,0:T(8,128)(2,1)S(1)} %get-tuple-element.30.x_ref, f32[8,128]{1,0:T(8,128)S(1)} %get-tuple-element.31.mine_ref, f32[1024,128]{1,0:T(8,128)S(1)} %bitcast.7), custom_call_target="tpu_custom_call" | custom-call | flops 1509949440 | bytes 5242880 | tf_op jit(solution)/shard_map/pallas_call | solution.py:406
  90.6 9.3 %collective-permute-start.14 = (f32[40,4224]{1,0:T(8,128)S(1)}, f32[40,4224]{1,0:T(8,128)S(1)}, u32[]{:S(2)}, u32[]{:S(2)}) collective-permute-start(f32[40,4224]{1,0:T(8,128)S(1)} %get-tuple-element.33), channel_id=1, source_target_pairs={{0,1},{1,0},{2,3},{3,2},{4,5},{5,4},{6,7},{7,6},{8,9},{9,8},{10,11... | collective-permute-start | bytes 2027528 | tf_op jit(solution)/shard_map/ppermute | solution.py:418
  99.9 1.8 %collective-permute-done.14.other_ref = f32[40,4224]{1,0:T(8,128)S(1)} collective-permute-done((f32[40,4224]{1,0:T(8,128)S(1)}, f32[40,4224]{1,0:T(8,128)S(1)}, u32[]{:S(2)}, u32[]{:S(2)}) %collective-permute-start.14) | collective-permute-done | bytes 675872 | tf_op jit(solution)/shard_map/ppermute | solution.py:418
  101.6 1.5 %shard_map.64 = (f32[1152,128]{1,0:T(8,128)}, f32[1,36]{1,0:T(1,128)}) custom-call(f32[40,4224]{1,0:T(8,128)S(1)} %get-tuple-element.32.keep_ref, f32[40,4224]{1,0:T(8,128)S(1)} %collective-permute-done.14.other_ref), custom_call_target="tpu_custom_call" | custom-call | bytes 2097152 | tf_op jit(solution)/shard_map/pallas_call | solution.py:419
  (2 shorter events, 0.0 us)
Async XLA Ops:
  2.4 13.6 %collective-permute-start.3 = (bf16[272,128]{1,0:T(8,128)(2,1)}, bf16[272,128]{1,0:T(8,128)(2,1)S(1)}, u32[]{:S(2)}, u32[]{:S(2)}) collective-permute-start(bf16[272,128]{1,0:T(8,128)(2,1)} %get-tuple-element.20.refs_1_), channel_id=1, source_target_pairs={{32,0},{64,32},{96,64},{128,96},{160,128},{192,160},{224,192},{0,2... | collective-permute-start | bytes 208904 | tf_op jit(solution)/shard_map/ppermute | solution.py:354
  8.8 7.2 %collective-permute-start.1 = (bf16[272,128]{1,0:T(8,128)(2,1)}, bf16[272,128]{1,0:T(8,128)(2,1)S(1)}, u32[]{:S(2)}, u32[]{:S(2)}) collective-permute-start(bf16[272,128]{1,0:T(8,128)(2,1)} %get-tuple-element.20.refs_1_), channel_id=1, source_target_pairs={{0,32},{32,64},{64,96},{96,128},{128,160},{160,192},{192,224},{224... | collective-permute-start | bytes 208904 | tf_op jit(solution)/shard_map/ppermute | solution.py:354
  8.8 5.3 %collective-permute-start.2 = (bf16[256,128]{1,0:T(8,128)(2,1)}, bf16[256,128]{1,0:T(8,128)(2,1)S(1)}, u32[]{:S(2)}, u32[]{:S(2)}) collective-permute-start(bf16[256,128]{1,0:T(8,128)(2,1)} %get-tuple-element.19.refs_0_), channel_id=1, source_target_pairs={{32,0},{64,32},{96,64},{128,96},{160,128},{192,160},{224,192},{0,2... | collective-permute-start | bytes 196616 | tf_op jit(solution)/shard_map/ppermute | solution.py:354
  11.5 4.5 %collective-permute-start = (bf16[256,128]{1,0:T(8,128)(2,1)}, bf16[256,128]{1,0:T(8,128)(2,1)S(1)}, u32[]{:S(2)}, u32[]{:S(2)}) collective-permute-start(bf16[256,128]{1,0:T(8,128)(2,1)} %get-tuple-element.19.refs_0_), channel_id=1, source_target_pairs={{0,32},{32,64},{64,96},{96,128},{128,160},{160,192},{192,224},{224... | collective-permute-start | bytes 196616 | tf_op jit(solution)/shard_map/ppermute | solution.py:354
  11.5 1.1 %copy-start = (bf16[1,72,4096]{2,1,0:T(8,128)(2,1)S(1)}, bf16[1,72,4096]{2,1,0:T(8,128)(2,1)}, u32[]{:S(2)}) copy-start(bf16[1,72,4096]{2,1,0:T(8,128)(2,1)} %param.5) | copy-start | bytes 1769476
  16.0 3.2 %collective-permute-start.7 = (bf16[272,128]{1,0:T(8,128)(2,1)S(1)}, bf16[272,128]{1,0:T(8,128)(2,1)S(1)}, u32[]{:S(2)}, u32[]{:S(2)}) collective-permute-start(bf16[272,128]{1,0:T(8,128)(2,1)S(1)} %collective-permute-done.3.refs_5_), channel_id=1, source_target_pairs={{32,0},{64,32},{96,64},{128,96},{160,128},{192,160},{224,192},{0,2... | collective-permute-start | bytes 208904 | tf_op jit(solution)/shard_map/ppermute | solution.py:354
  16.9 4.4 %collective-permute-start.4 = (bf16[256,128]{1,0:T(8,128)(2,1)S(1)}, bf16[256,128]{1,0:T(8,128)(2,1)S(1)}, u32[]{:S(2)}, u32[]{:S(2)}) collective-permute-start(bf16[256,128]{1,0:T(8,128)(2,1)S(1)} %collective-permute-done.refs_2_), channel_id=1, source_target_pairs={{0,32},{32,64},{64,96},{96,128},{128,160},{160,192},{192,224},{224... | collective-permute-start | bytes 196616 | tf_op jit(solution)/shard_map/ppermute | solution.py:354
  17.5 5.3 %collective-permute-start.5 = (bf16[272,128]{1,0:T(8,128)(2,1)S(1)}, bf16[272,128]{1,0:T(8,128)(2,1)S(1)}, u32[]{:S(2)}, u32[]{:S(2)}) collective-permute-start(bf16[272,128]{1,0:T(8,128)(2,1)S(1)} %collective-permute-done.1.refs_3_), channel_id=1, source_target_pairs={{0,32},{32,64},{64,96},{96,128},{128,160},{160,192},{192,224},{224... | collective-permute-start | bytes 208904 | tf_op jit(solution)/shard_map/ppermute | solution.py:354
  19.2 4.1 %collective-permute-start.11 = (bf16[272,128]{1,0:T(8,128)(2,1)S(1)}, bf16[272,128]{1,0:T(8,128)(2,1)S(1)}, u32[]{:S(2)}, u32[]{:S(2)}) collective-permute-start(bf16[272,128]{1,0:T(8,128)(2,1)S(1)} %collective-permute-done.7.refs_9_), channel_id=1, source_target_pairs={{32,0},{64,32},{96,64},{128,96},{160,128},{192,160},{224,192},{0,2... | collective-permute-start | bytes 208904 | tf_op jit(solution)/shard_map/ppermute | solution.py:354
  21.3 4.4 %collective-permute-start.6 = (bf16[256,128]{1,0:T(8,128)(2,1)S(1)}, bf16[256,128]{1,0:T(8,128)(2,1)S(1)}, u32[]{:S(2)}, u32[]{:S(2)}) collective-permute-start(bf16[256,128]{1,0:T(8,128)(2,1)S(1)} %collective-permute-done.2.refs_4_), channel_id=1, source_target_pairs={{32,0},{64,32},{96,64},{128,96},{160,128},{192,160},{224,192},{0,2... | collective-permute-start | bytes 196616 | tf_op jit(solution)/shard_map/ppermute | solution.py:354
  21.3 5.1 %collective-permute-start.8 = (bf16[256,128]{1,0:T(8,128)(2,1)S(1)}, bf16[256,128]{1,0:T(8,128)(2,1)S(1)}, u32[]{:S(2)}, u32[]{:S(2)}) collective-permute-start(bf16[256,128]{1,0:T(8,128)(2,1)S(1)} %collective-permute-done.4.refs_6_), channel_id=1, source_target_pairs={{0,32},{32,64},{64,96},{96,128},{128,160},{160,192},{192,224},{224... | collective-permute-start | bytes 196616 | tf_op jit(solution)/shard_map/ppermute | solution.py:354
  22.8 6.3 %collective-permute-start.9 = (bf16[272,128]{1,0:T(8,128)(2,1)S(1)}, bf16[272,128]{1,0:T(8,128)(2,1)S(1)}, u32[]{:S(2)}, u32[]{:S(2)}) collective-permute-start(bf16[272,128]{1,0:T(8,128)(2,1)S(1)} %collective-permute-done.5.refs_7_), channel_id=1, source_target_pairs={{0,32},{32,64},{64,96},{96,128},{128,160},{160,192},{192,224},{224... | collective-permute-start | bytes 208904 | tf_op jit(solution)/shard_map/ppermute | solution.py:354
  23.3 7.4 %collective-permute-start.13 = (bf16[272,128]{1,0:T(8,128)(2,1)S(1)}, bf16[272,128]{1,0:T(8,128)(2,1)S(1)}, u32[]{:S(2)}, u32[]{:S(2)}) collective-permute-start(bf16[272,128]{1,0:T(8,128)(2,1)S(1)} %collective-permute-done.11.refs_13_), channel_id=1, source_target_pairs={{32,0},{64,32},{96,64},{128,96},{160,128},{192,160},{224,192},{0,2... | collective-permute-start | bytes 208904 | tf_op jit(solution)/shard_map/ppermute | solution.py:354
  25.7 3.4 %collective-permute-start.10 = (bf16[256,128]{1,0:T(8,128)(2,1)S(1)}, bf16[256,128]{1,0:T(8,128)(2,1)S(1)}, u32[]{:S(2)}, u32[]{:S(2)}) collective-permute-start(bf16[256,128]{1,0:T(8,128)(2,1)S(1)} %collective-permute-done.6.refs_8_), channel_id=1, source_target_pairs={{32,0},{64,32},{96,64},{128,96},{160,128},{192,160},{224,192},{0,2... | collective-permute-start | bytes 196616 | tf_op jit(solution)/shard_map/ppermute | solution.py:354
  26.4 4.3 %collective-permute-start.12 = (bf16[256,128]{1,0:T(8,128)(2,1)S(1)}, bf16[256,128]{1,0:T(8,128)(2,1)S(1)}, u32[]{:S(2)}, u32[]{:S(2)}) collective-permute-start(bf16[256,128]{1,0:T(8,128)(2,1)S(1)} %collective-permute-done.8.refs_10_), channel_id=1, source_target_pairs={{0,32},{32,64},{64,96},{96,128},{128,160},{160,192},{192,224},{224... | collective-permute-start | bytes 196616 | tf_op jit(solution)/shard_map/ppermute | solution.py:354
  30.7 0.9 copy-start.1
  31.6 0.8 copy-start.2
  90.6 11.0 %collective-permute-start.14 = (f32[40,4224]{1,0:T(8,128)S(1)}, f32[40,4224]{1,0:T(8,128)S(1)}, u32[]{:S(2)}, u32[]{:S(2)}) collective-permute-start(f32[40,4224]{1,0:T(8,128)S(1)} %get-tuple-element.33), channel_id=1, source_target_pairs={{0,1},{1,0},{2,3},{3,2},{4,5},{5,4},{6,7},{7,6},{8,9},{9,8},{10,11... | collective-permute-start | bytes 2027528 | tf_op jit(solution)/shard_map/ppermute | solution.py:418

commit v3 on v2

--- a/solution.py
+++ b/solution.py
@@ -43,9 +43,8 @@
     return jnp.where(low, pltpu.roll(load(first), half, 1), load(first + 1))
 
 
-def pack_kernel(cand_ref, noise_ref, img_ref, send_ref, late_ref):
+def pack_kernel(cand_ref, noise_ref, img_ref, send_ref):
     top, rows = cand_ref.shape
-    early = send_ref.shape[0] // rows
     tiles = img_ref.shape[1] // LANES
     low = lane_row() < LANES // 2
     row_id = lax.broadcasted_iota(jnp.int32, (rows, LANES), 0)
@@ -67,27 +66,26 @@
     )
     facts = jnp.where(lane_id == 0, noise, facts)
     facts = jnp.where(lane_id == 1, (row_id + 1).astype(F32), facts)
-    late_ref[(tiles - early) * rows :] = facts.astype(BF16)
+    send_ref[tiles * rows :] = facts.astype(BF16)
     for q in range(tiles):
         tile = fold_tile(lambda t: img_ref[:, tile_of(t)].astype(F32), q, tiles, low)
-        to_ref, at = (send_ref, q) if q < early else (late_ref, q - early)
-        to_ref[at * rows : (at + 1) * rows] = tile.astype(BF16)
+        send_ref[q * rows : (q + 1) * rows] = tile.astype(BF16)
 
 
 def pick_kernel(*refs, steps, top):
-    planes = len(steps)
-    recv_refs, send_ref, column_ref = refs[: 2 * planes], refs[-2], refs[-1]
+    planes = len(steps) - 1
+    recv_refs, send_ref, column_ref = refs[: len(steps)], refs[-2], refs[-1]
     owners, depth, _ = send_ref.shape
     rows = column_ref.shape[0] // planes
     tiles = column_ref.shape[1] // LANES
     group = depth // tiles
     slots = owners * group
-    cut = recv_refs[0].shape[0] // rows
+    cut = recv_refs[-2].shape[0] // rows
     for j in range(planes):
         for t in range(tiles):
-            from_ref, at = recv_refs[2 * j], t
-            if t >= cut:
-                from_ref, at = recv_refs[2 * j + 1], t - cut
+            from_ref, at = recv_refs[j], t
+            if j == planes - 1 and t >= cut:
+                from_ref, at = recv_refs[j + 1], t - cut
             column_ref[j * rows : (j + 1) * rows, tile_of(t)] = from_ref[
                 at * rows : (at + 1) * rows
             ]
@@ -339,21 +337,19 @@
     shape = jax.ShapeDtypeStruct
     exchange = functools.partial(lax.all_to_all, split_axis=0, concat_axis=0, tiled=True)
 
-    cut = (tiles + 1) // 2
     packed = call(
         pack_kernel,
-        (shape((cut * rows, LANES), BF16), shape(((tiles + 1 - cut) * rows, LANES), BF16)),
+        shape(((tiles + 1) * rows, LANES), BF16),
         3,
-        56,
+        4,
         moved=MIB // 4,
     )(candidates.T, inv_noise[None, :], images)
-    up = [(i, (i + 1) % planes) for i in range(planes)]
-    down = [((i + 1) % planes, i) for i in range(planes)]
-
-    def move(parts, way):
-        return [lax.ppermute(part, "z", way) for part in parts]
-
-    rising, falling = move(packed, up), move(packed, down)
+
+    def move(part, step):
+        return lax.ppermute(part, "z", [(i, (i + step) % planes) for i in range(planes)])
+
+    near = [move(packed, step) for step in (1, -1)]
+    next_near = [move(packed, step) for step in (2, -2)]
     half_rots = rots // 2
     half_count = -(-half_rots // 8) * 8
     pad = half_count - half_rots
@@ -367,16 +363,12 @@
         [pltpu.VMEM((count, pixels), BF16)],
         moved=12 * MIB,
     )(references[0])
-    rising, falling, shifted, half_norm = lax.optimization_barrier(
-        (rising, falling, shifted, half_norm)
-    )
-    column, steps = [*packed, *rising, *falling], [0, -1, 1]
-    for step in range(2, planes // 2):
-        rising, falling = move(rising, up), move(falling, down)
-        column += [*rising, *falling]
-        steps += [-step, step]
-    column += [*move(rising[:1], up), *move(falling[1:], down)]
-    steps.append(planes // 2)
+    next_near, shifted, half_norm = lax.optimization_barrier((next_near, shifted, half_norm))
+    cut = (tiles + 1) // 2 * rows
+    far = [move(next_near[0], 1), move(next_near[1], -1)]
+    far += [move(next_near[0][:cut], 2), move(next_near[1][cut:], -2)]
+    column = [packed, *near, *next_near, *far]
+    steps = [0, -1, 1, -2, 2, -3, 3, 4, 4]
     picked = call(
         functools.partial(pick_kernel, steps=steps, top=top),
         shape((owners, (tiles + 1) * group, LANES), BF16),

time: 103 us -> 99 us (0.961)
  starting transfers between devices: 27.3 us -> 23.5 us
  blocking collectives: 52.5 us -> 54.8 us
  waiting for transfers between devices: 9.37 us -> 7.56 us
  Pallas kernels: 10.4 us -> 8.84 us
    ppermute x14 -> x8, starting transfers between devices: 18.1 us -> 15.1 us  [move(): lax.ppermute(part, 'z', [(i, (i + step) % planes) for i in range(planes)])]
    all_to_all x1, blocking collectives: 29.4 us -> 31.3 us  [on_device(): received = exchange(picked, 'xy')]
    ppermute x14 -> x8, waiting for transfers between devices: 7.61 us -> 5.81 us  [move(): lax.ppermute(part, 'z', [(i, (i + step) % planes) for i in range(planes)])]
    pallas_call x1, Pallas kernels: 1.74 us -> 0.17 us  [on_device(): call(pack_kernel, shape(((tiles + 1) * rows, LANES), BF16), 3, 4, moved=M...]
    unnamed x6 -> x8, local copies, waits for them, and re-layouts: 2.79 us -> 3.3 us
  transfers between devices with their start and end apart: 15 -> 9, of which waited for: 6 -> 3; matrix products, arithmetic and copies ran while one was open for 0% -> 0% of each run, Pallas kernels for 2% -> 2%
where the time goes in v3:
time: 99 us; the launch traced here: 98.7 us
  blocking collectives  54.8 us (55%)
  starting transfers between devices  23.5 us (24%)
  Pallas kernels  8.84 us (9%)
  waiting for transfers between devices  7.56 us (8%)
  local copies, waits for them, and re-layouts  3.36 us (3%)
    all_to_all x1, blocking collectives, on_device(): received = exchange(picked, 'xy')  31.3 us
    ppermute x8, starting transfers between devices, move(): lax.ppermute(part, 'z', [(i, (i + step) % planes) for i in range(planes)])  15.1 us
    all_to_all x1, blocking collectives, on_device(): exchange(jnp.broadcast_to(by_plane, (owners, planes * 8, LANES)), 'xy')  11.8 us
    all_to_all x1, blocking collectives, on_device(): by_plane = exchange(jnp.broadcast_to(tile[None], (planes, 8, LANES)), 'z')  11.6 us
    ppermute x1, starting transfers between devices, on_device(): other = lax.ppermute(give, 'dp', [(0, 1), (1, 0)])  8.35 us
    ppermute x8, waiting for transfers between devices, move(): lax.ppermute(part, 'z', [(i, (i + step) % planes) for i in range(planes)])  5.81 us
    unnamed x8, local copies, waits for them, and re-layouts  3.3 us
    pallas_call x1, Pallas kernels, on_device(): call(sum_kernel, (half_shape, half_shape), 4, 8, [pltpu.VMEM((groups, len...  2.34 us
  transfers between devices with their start and end apart: 9, of which 3 were waited for; matrix products, arithmetic and copies ran while one was open for 0% of the time, Pallas kernels for 2%

profile of v3, /device:TPU:1, one launch (start us, length us, event | category | flops | bytes accessed | tf_op | source)
XLA Modules:
  0.0 98.7 jit_solution(4312097441787458580)
XLA Ops:
  0.6 0.0 copy-start.1
  0.6 0.9 copy-done.1
  1.5 0.0 copy-start.2
  1.5 0.7 copy-done.2
  2.2 0.0 copy-start.3
  2.2 0.7 copy-done.3
  2.9 0.2 shard_map.59.refs_0_
  3.0 6.9 %collective-permute-start.3 = (bf16[528,128]{1,0:T(8,128)(2,1)S(1)}, bf16[528,128]{1,0:T(8,128)(2,1)S(1)}, u32[]{:S(2)}, u32[]{:S(2)}) collective-permute-start(bf16[528,128]{1,0:T(8,128)(2,1)S(1)} %shard_map.59.refs_0_), channel_id=1, source_target_pairs={{0,192},{32,224},{64,0},{96,32},{128,64},{160,96},{192,128},{224,1... | collective-permute-start | bytes 405512 | tf_op jit(solution)/shard_map/ppermute | solution.py:349
  9.9 0.0 collective-permute-start.2
  9.9 3.1 %collective-permute-start.1 = (bf16[528,128]{1,0:T(8,128)(2,1)S(1)}, bf16[528,128]{1,0:T(8,128)(2,1)S(1)}, u32[]{:S(2)}, u32[]{:S(2)}) collective-permute-start(bf16[528,128]{1,0:T(8,128)(2,1)S(1)} %shard_map.59.refs_0_), channel_id=1, source_target_pairs={{0,224},{32,0},{64,32},{96,64},{128,96},{160,128},{192,160},{224,1... | collective-permute-start | bytes 405512 | tf_op jit(solution)/shard_map/ppermute | solution.py:349
  13.1 0.0 collective-permute-start
  13.1 0.0 copy-start
  13.1 1.1 %copy-done = bf16[1,72,4096]{2,1,0:T(8,128)(2,1)S(1)} copy-done((bf16[1,72,4096]{2,1,0:T(8,128)(2,1)S(1)}, bf16[1,72,4096]{2,1,0:T(8,128)(2,1)}, u32[]{:S(2)}) %copy-start) | copy-done | bytes 589848
  14.1 1.6 %shard_map.60 = (bf16[720,4096]{1,0:T(8,128)(2,1)S(1)}, f32[80,128]{1,0:T(8,128)S(1)}) custom-call(bf16[72,4096]{1,0:T(8,128)(2,1)S(1)} %bitcast.6), custom_call_target="tpu_custom_call" | custom-call | bytes 12582912 | tf_op jit(solution)/shard_map/pallas_call | solution.py:358
  15.7 0.0 collective-permute-done.3.refs_4_
  15.7 1.8 %collective-permute-done.2.refs_3_ = bf16[528,128]{1,0:T(8,128)(2,1)S(1)} collective-permute-done((bf16[528,128]{1,0:T(8,128)(2,1)S(1)}, bf16[528,128]{1,0:T(8,128)(2,1)S(1)}, u32[]{:S(2)}, u32[]{:S(2)}) %collective-permute-start.2) | collective-permute-done | bytes 135200 | tf_op jit(solution)/shard_map/ppermute | solution.py:349
  17.5 2.2 %collective-permute-start.4 = (bf16[528,128]{1,0:T(8,128)(2,1)S(1)}, bf16[528,128]{1,0:T(8,128)(2,1)S(1)}, u32[]{:S(2)}, u32[]{:S(2)}) collective-permute-start(bf16[528,128]{1,0:T(8,128)(2,1)S(1)} %collective-permute-done.2.refs_3_), channel_id=1, source_target_pairs={{0,32},{32,64},{64,96},{96,128},{128,160},{160,192},{192,224},{224... | collective-permute-start | bytes 405512 | tf_op jit(solution)/shard_map/ppermute | solution.py:349
  19.7 0.5 collective-permute-start.5
  20.2 0.9 collective-permute-start.7
  21.1 0.0 collective-permute-done.1.refs_2_
  21.1 1.5 %collective-permute-start.6 = (bf16[256,128]{1,0:T(8,128)(2,1)S(1)}, bf16[256,128]{1,0:T(8,128)(2,1)S(1)}, u32[]{:S(2)}, u32[]{:S(2)}) collective-permute-start(bf16[256,128]{1,0:T(8,128)(2,1)S(1)} %slice.6), channel_id=1, source_target_pairs={{0,64},{32,96},{64,128},{96,160},{128,192},{160,224},{192,0},{224,... | collective-permute-start | bytes 196616 | tf_op jit(solution)/shard_map/ppermute | solution.py:349
  22.7 0.0 collective-permute-done.refs_1_
  22.7 4.0 %collective-permute-done.6.refs_7_ = bf16[256,128]{1,0:T(8,128)(2,1)S(1)} collective-permute-done((bf16[256,128]{1,0:T(8,128)(2,1)S(1)}, bf16[256,128]{1,0:T(8,128)(2,1)S(1)}, u32[]{:S(2)}, u32[]{:S(2)}) %collective-permute-start.6) | collective-permute-done | bytes 65568 | tf_op jit(solution)/shard_map/ppermute | solution.py:349
  26.7 0.0 collective-permute-done.7.refs_8_
  26.7 0.0 collective-permute-done.4.refs_5_
  26.7 0.0 collective-permute-done.5.refs_6_
  26.7 1.2 %shard_map.61 = bf16[16,528,128]{2,1,0:T(8,128)(2,1)S(1)} custom-call(bf16[528,128]{1,0:T(8,128)(2,1)S(1)} %shard_map.59.refs_0_, bf16[528,128]{1,0:T(8,128)(2,1)S(1)} %collective-permute-done.refs_1_, bf16[528,128]{1,0:T(8,128)(2,1)S(1)} %collective-permute-done.1.refs_2_, bf16[528,128]{1,0:T(8,128)(2,1)S(1)} %collective-permute-done.2.refs_3_, ...), custom_call_target="tpu_custom_call" | custom-call | bytes 3145728 | tf_op jit(solution)/shard_map/pallas_call | solution.py:372
  27.9 31.3 %all_to_all.15.recv_ref = bf16[16,528,128]{2,1,0:T(8,128)(2,1)S(1)} all-to-all(bf16[16,528,128]{2,1,0:T(8,128)(2,1)S(1)} %shard_map.61), channel_id=1, replica_groups=mesh['z'=8,'xy'=16,'dp'=2] {'xy'}, dimensions={0} | all-to-all | bytes 4325376 | tf_op jit(solution)/shard_map/all_to_all | solution.py:380
  59.2 2.1 %shard_map.62 = (bf16[256,4352]{1,0:T(8,128)(2,1)S(1)}, f32[240,768]{1,0:T(8,128)S(1)}, f32[8,128]{1,0:T(8,128)S(1)}) custom-call(bf16[16,528,128]{2,1,0:T(8,128)(2,1)S(1)} %all_to_all.15.recv_ref, bf16[720,4096]{1,0:T(8,128)(2,1)S(1)} %get-tuple-element.19.shifted_ref, f32[80,128]{1,0:T(8,128)S(1)} %get-tuple-element.20.half_ref), custom_call_target="tpu_custom_call" | custom-call | flops 1509949440 | bytes 10485760 | tf_op jit(solution)/shard_map/pallas_call | solution.py:382
  61.3 11.6 %all_to_all.16 = f32[8,8,128]{2,1,0:T(8,128)S(1)} all-to-all(f32[8,8,128]{2,1,0:T(8,128)S(1)} %broadcast_in_dim.17), channel_id=1, replica_groups=mesh['z'=8,'xy'=16,'dp'=2] {'z'}, dimensions={0} | all-to-all | bytes 65536 | tf_op jit(solution)/shard_map/all_to_all | solution.py:394
  72.9 11.8 %all_to_all.17 = f32[16,64,128]{2,1,0:T(8,128)S(1)} all-to-all(f32[16,64,128]{2,1,0:T(8,128)S(1)} %broadcast_in_dim.19), channel_id=1, replica_groups=mesh['z'=8,'xy'=16,'dp'=2] {'xy'}, dimensions={0} | all-to-all | bytes 1048576 | tf_op jit(solution)/shard_map/all_to_all | solution.py:396
  84.8 2.3 %shard_map.63 = (f32[40,4224]{1,0:T(8,128)S(1)}, f32[40,4224]{1,0:T(8,128)S(1)}) custom-call(f32[240,768]{1,0:T(8,128)S(1)} %get-tuple-element.21.s_ref, bf16[256,4352]{1,0:T(8,128)(2,1)S(1)} %get-tuple-element.22.x_ref, f32[8,128]{1,0:T(8,128)S(1)} %get-tuple-element.23.mine_ref, f32[1024,128]{1,0:T(8,128)S(1)} %bitcast.7), custom_call_target="tpu_custom_call" | custom-call | flops 1509949440 | bytes 5242880 | tf_op jit(solution)/shard_map/pallas_call | solution.py:398
  87.1 8.4 %collective-permute-start.8 = (f32[40,4224]{1,0:T(8,128)S(1)}, f32[40,4224]{1,0:T(8,128)S(1)}, u32[]{:S(2)}, u32[]{:S(2)}) collective-permute-start(f32[40,4224]{1,0:T(8,128)S(1)} %get-tuple-element.25), channel_id=1, source_target_pairs={{0,1},{1,0},{2,3},{3,2},{4,5},{5,4},{6,7},{7,6},{8,9},{9,8},{10,11... | collective-permute-start | bytes 2027528 | tf_op jit(solution)/shard_map/ppermute | solution.py:410
  95.5 1.8 %collective-permute-done.8.other_ref = f32[40,4224]{1,0:T(8,128)S(1)} collective-permute-done((f32[40,4224]{1,0:T(8,128)S(1)}, f32[40,4224]{1,0:T(8,128)S(1)}, u32[]{:S(2)}, u32[]{:S(2)}) %collective-permute-start.8) | collective-permute-done | bytes 675872 | tf_op jit(solution)/shard_map/ppermute | solution.py:410
  97.2 1.5 %shard_map.64 = (f32[1152,128]{1,0:T(8,128)}, f32[1,36]{1,0:T(1,128)}) custom-call(f32[40,4224]{1,0:T(8,128)S(1)} %get-tuple-element.24.keep_ref, f32[40,4224]{1,0:T(8,128)S(1)} %collective-permute-done.8.other_ref), custom_call_target="tpu_custom_call" | custom-call | bytes 2097152 | tf_op jit(solution)/shard_map/pallas_call | solution.py:411
  (4 shorter events, 0.1 us)
Async XLA Ops:
  0.6 0.9 copy-start.1
  1.5 0.7 copy-start.2
  2.2 0.7 copy-start.3
  3.0 12.7 %collective-permute-start.3 = (bf16[528,128]{1,0:T(8,128)(2,1)S(1)}, bf16[528,128]{1,0:T(8,128)(2,1)S(1)}, u32[]{:S(2)}, u32[]{:S(2)}) collective-permute-start(bf16[528,128]{1,0:T(8,128)(2,1)S(1)} %shard_map.59.refs_0_), channel_id=1, source_target_pairs={{0,192},{32,224},{64,0},{96,32},{128,64},{160,96},{192,128},{224,1... | collective-permute-start | bytes 405512 | tf_op jit(solution)/shard_map/ppermute | solution.py:349
  9.9 7.6 %collective-permute-start.2 = (bf16[528,128]{1,0:T(8,128)(2,1)S(1)}, bf16[528,128]{1,0:T(8,128)(2,1)S(1)}, u32[]{:S(2)}, u32[]{:S(2)}) collective-permute-start(bf16[528,128]{1,0:T(8,128)(2,1)S(1)} %shard_map.59.refs_0_), channel_id=1, source_target_pairs={{0,64},{32,96},{64,128},{96,160},{128,192},{160,224},{192,0},{224,... | collective-permute-start | bytes 405512 | tf_op jit(solution)/shard_map/ppermute | solution.py:349
  9.9 11.2 %collective-permute-start.1 = (bf16[528,128]{1,0:T(8,128)(2,1)S(1)}, bf16[528,128]{1,0:T(8,128)(2,1)S(1)}, u32[]{:S(2)}, u32[]{:S(2)}) collective-permute-start(bf16[528,128]{1,0:T(8,128)(2,1)S(1)} %shard_map.59.refs_0_), channel_id=1, source_target_pairs={{0,224},{32,0},{64,32},{96,64},{128,96},{160,128},{192,160},{224,1... | collective-permute-start | bytes 405512 | tf_op jit(solution)/shard_map/ppermute | solution.py:349
  13.1 9.6 %collective-permute-start = (bf16[528,128]{1,0:T(8,128)(2,1)S(1)}, bf16[528,128]{1,0:T(8,128)(2,1)S(1)}, u32[]{:S(2)}, u32[]{:S(2)}) collective-permute-start(bf16[528,128]{1,0:T(8,128)(2,1)S(1)} %shard_map.59.refs_0_), channel_id=1, source_target_pairs={{0,32},{32,64},{64,96},{96,128},{128,160},{160,192},{192,224},{224... | collective-permute-start | bytes 405512 | tf_op jit(solution)/shard_map/ppermute | solution.py:349
  13.1 1.1 %copy-start = (bf16[1,72,4096]{2,1,0:T(8,128)(2,1)S(1)}, bf16[1,72,4096]{2,1,0:T(8,128)(2,1)}, u32[]{:S(2)}) copy-start(bf16[1,72,4096]{2,1,0:T(8,128)(2,1)} %param.5) | copy-start | bytes 1769476
  17.5 9.2 %collective-permute-start.4 = (bf16[528,128]{1,0:T(8,128)(2,1)S(1)}, bf16[528,128]{1,0:T(8,128)(2,1)S(1)}, u32[]{:S(2)}, u32[]{:S(2)}) collective-permute-start(bf16[528,128]{1,0:T(8,128)(2,1)S(1)} %collective-permute-done.2.refs_3_), channel_id=1, source_target_pairs={{0,32},{32,64},{64,96},{96,128},{128,160},{160,192},{192,224},{224... | collective-permute-start | bytes 405512 | tf_op jit(solution)/shard_map/ppermute | solution.py:349
  19.7 7.0 %collective-permute-start.5 = (bf16[528,128]{1,0:T(8,128)(2,1)S(1)}, bf16[528,128]{1,0:T(8,128)(2,1)S(1)}, u32[]{:S(2)}, u32[]{:S(2)}) collective-permute-start(bf16[528,128]{1,0:T(8,128)(2,1)S(1)} %collective-permute-done.3.refs_4_), channel_id=1, source_target_pairs={{0,224},{32,0},{64,32},{96,64},{128,96},{160,128},{192,160},{224,1... | collective-permute-start | bytes 405512 | tf_op jit(solution)/shard_map/ppermute | solution.py:349
  20.2 6.5 %collective-permute-start.7 = (bf16[272,128]{1,0:T(8,128)(2,1)S(1)}, bf16[272,128]{1,0:T(8,128)(2,1)S(1)}, u32[]{:S(2)}, u32[]{:S(2)}) collective-permute-start(bf16[272,128]{1,0:T(8,128)(2,1)S(1)} %slice.7), channel_id=1, source_target_pairs={{0,192},{32,224},{64,0},{96,32},{128,64},{160,96},{192,128},{224,1... | collective-permute-start | bytes 208904 | tf_op jit(solution)/shard_map/ppermute | solution.py:349
  21.1 5.5 %collective-permute-start.6 = (bf16[256,128]{1,0:T(8,128)(2,1)S(1)}, bf16[256,128]{1,0:T(8,128)(2,1)S(1)}, u32[]{:S(2)}, u32[]{:S(2)}) collective-permute-start(bf16[256,128]{1,0:T(8,128)(2,1)S(1)} %slice.6), channel_id=1, source_target_pairs={{0,64},{32,96},{64,128},{96,160},{128,192},{160,224},{192,0},{224,... | collective-permute-start | bytes 196616 | tf_op jit(solution)/shard_map/ppermute | solution.py:349
  87.1 10.1 %collective-permute-start.8 = (f32[40,4224]{1,0:T(8,128)S(1)}, f32[40,4224]{1,0:T(8,128)S(1)}, u32[]{:S(2)}, u32[]{:S(2)}) collective-permute-start(f32[40,4224]{1,0:T(8,128)S(1)} %get-tuple-element.25), channel_id=1, source_target_pairs={{0,1},{1,0},{2,3},{3,2},{4,5},{5,4},{6,7},{7,6},{8,9},{9,8},{10,11... | collective-permute-start | bytes 2027528 | tf_op jit(solution)/shard_map/ppermute | solution.py:410

commit v4 on v3

--- a/solution.py
+++ b/solution.py
@@ -223,51 +223,13 @@
     tile_ref[3 * parts :] = jnp.zeros_like(tile_ref[3 * parts :])
 
 
-def sum_kernel(s_ref, x_ref, mine_ref, all_ref, keep_ref, give_ref, w_ref, y_ref):
-    groups = s_ref.shape[0]
+def sum_half(w_ref, x_ref, out_ref, y_ref):
     slots = x_ref.shape[0]
     pixels = x_ref.shape[1] - 2 * LANES
-    owners = all_ref.shape[0] // 8
-    count = groups // len(COL_SHIFTS)
-    half_count = count // 2
-    parts = slots // LANES
+    count = y_ref.shape[0] // len(COL_SHIFTS)
     side = LANES // 2
-    lane = lane_row()
-    second = (lane // PLANES) % SLOTS == 1
-
-    def partner(row):
-        return jnp.where(second, pltpu.roll(row, PLANES, 1), pltpu.roll(row, LANES - PLANES, 1))
-
-    peaks, scales = [], []
-    for h in range(parts):
-        own = mine_ref[2 * parts + h : 2 * parts + h + 1]
-        across = partner(own)
-        shown = [all_ref[pl.ds(i * parts + h, owners, stride=8), :] for i in range(3)]
-        found = []
-        for slot in range(SLOTS):
-            target = jnp.where(second == (slot == 1), own, across)
-            same = shown[2] == target
-            peak = jnp.max(jnp.where(same, shown[0], -jnp.inf), axis=0, keepdims=True)
-            peak = jnp.maximum(peak, partner(peak))
-            part = shown[1] * jnp.exp(jnp.minimum(shown[0] - peak, 0.0))
-            total = jnp.sum(jnp.where(same, part, 0.0), axis=0, keepdims=True)
-            found.append((peak, total + partner(total)))
-        peaks.append(jnp.where(second, found[1][0], found[0][0]))
-        total = jnp.where(second, found[1][1], found[0][1])
-        scales.append(jnp.where(own > 0, 1.0 / total, 0.0))
-    peak = jnp.concatenate(peaks, axis=1)
-    scale = jnp.concatenate(scales, axis=1)
-    row_total = jnp.zeros((groups, 1), F32)
-    for i in range(len(ROW_SHIFTS)):
-        part = slice(i * slots, (i + 1) * slots)
-        weights = (jnp.exp(jnp.minimum(s_ref[:, part] - peak, 0.0)) * scale).astype(BF16)
-        w_ref[:, part] = weights
-        row_total = row_total + jnp.sum(weights.astype(F32), axis=1, keepdims=True)
-    class_total = sum(row_total[i * count : (i + 1) * count] for i in range(len(COL_SHIFTS)))
-    keep_ref[:, pixels:] = jnp.broadcast_to(class_total[:half_count], (half_count, LANES))
-    give_ref[:, pixels:] = jnp.broadcast_to(class_total[half_count:], (half_count, LANES))
     width = y_ref.shape[1]
-    column = lane % side
+    column = lane_row() % side
     for first in range(0, pixels, width):
         y_ref[...] = sum(
             jnp.dot(
@@ -289,13 +251,63 @@
             forth = jnp.where(
                 column == 0, pltpu.roll(left, LANES - side + 1, 1), pltpu.roll(left, 1, 1)
             )
-            moved = plain + back + forth
-            at = slice(first + t * LANES, first + (t + 1) * LANES)
-            keep_ref[:, at] = moved[:half_count]
-            give_ref[:, at] = moved[half_count:]
-
-
-def finish_kernel(keep_ref, other_ref, sums_ref, totals_ref):
+            out_ref[:, first + t * LANES : first + (t + 1) * LANES] = plain + back + forth
+
+
+def give_kernel(s_ref, x_ref, mine_ref, all_ref, give_ref, w_ref, total_ref, w_give_ref, y_ref):
+    groups = s_ref.shape[0]
+    slots = x_ref.shape[0]
+    pixels = x_ref.shape[1] - 2 * LANES
+    owners = all_ref.shape[0] // 8
+    count = groups // len(COL_SHIFTS)
+    half_count = count // 2
+    parts = slots // LANES
+    lane = lane_row()
+    second = (lane // PLANES) % SLOTS == 1
+
+    def partner(row):
+        return jnp.where(second, pltpu.roll(row, PLANES, 1), pltpu.roll(row, LANES - PLANES, 1))
+
+    peaks, scales = [], []
+    for h in range(parts):
+        own = mine_ref[2 * parts + h : 2 * parts + h + 1]
+        across = partner(own)
+        shown = [all_ref[pl.ds(i * parts + h, owners, stride=8), :] for i in range(3)]
+        found = []
+        for slot in range(SLOTS):
+            target = jnp.where(second == (slot == 1), own, across)
+            same = shown[2] == target
+            peak = jnp.max(jnp.where(same, shown[0], -jnp.inf), axis=0, keepdims=True)
+            peak = jnp.maximum(peak, partner(peak))
+            part = shown[1] * jnp.exp(jnp.minimum(shown[0] - peak, 0.0))
+            total = jnp.sum(jnp.where(same, part, 0.0), axis=0, keepdims=True)
+            found.append((peak, total + partner(total)))
+        peaks.append(jnp.where(second, found[1][0], found[0][0]))
+        total = jnp.where(second, found[1][1], found[0][1])
+        scales.append(jnp.where(own > 0, 1.0 / total, 0.0))
+    peak = jnp.concatenate(peaks, axis=1)
+    scale = jnp.concatenate(scales, axis=1)
+    for half, to_ref, sums_ref in ((0, w_ref, total_ref), (1, w_give_ref, give_ref.at[:, pixels:])):
+        class_total = jnp.zeros((half_count, 1), F32)
+        for i in range(len(ROW_SHIFTS)):
+            part = slice(i * slots, (i + 1) * slots)
+            for j in range(len(COL_SHIFTS)):
+                first = j * count + half * half_count
+                weights = s_ref[first : first + half_count, part]
+                weights = jnp.exp(jnp.minimum(weights - peak, 0.0)) * scale
+                weights = weights.astype(BF16).astype(F32)
+                class_total = class_total + jnp.sum(weights, axis=1, keepdims=True)
+                y_ref[j * half_count : (j + 1) * half_count, :slots] = weights
+            to_ref[:, part] = y_ref[:, :slots].astype(BF16)
+        sums_ref[...] = jnp.broadcast_to(class_total, (half_count, LANES))
+    sum_half(w_give_ref, x_ref, give_ref, y_ref)
+
+
+def keep_kernel(w_ref, x_ref, keep_ref, y_ref):
+    sum_half(w_ref, x_ref, keep_ref, y_ref)
+
+
+def finish_kernel(keep_ref, total_ref, other_ref, sums_ref, totals_ref):
     rots = totals_ref.shape[1]
     tiles = sums_ref.shape[0] // rots
     low = lane_row() < LANES // 2
@@ -305,7 +317,7 @@
 
     for t in range(tiles):
         sums_ref[pl.ds(t, rots, stride=tiles), :] = unfold_tile(load, t, tiles, low)
-    total = load(tiles)
+    total = total_ref[:rots] + other_ref[:rots, tile_of(tiles)]
     here = lax.broadcasted_iota(jnp.int32, (rots, LANES), 0) == lax.broadcasted_iota(
         jnp.int32, (rots, LANES), 1
     )
@@ -394,27 +406,38 @@
     by_plane = exchange(jnp.broadcast_to(tile[None], (planes, 8, LANES)), "z")
     by_plane = by_plane.reshape(1, planes * 8, LANES)
     everyone = exchange(jnp.broadcast_to(by_plane, (owners, planes * 8, LANES)), "xy")
-    half_shape = shape((half_count, pixels + LANES), F32)
-    keep, give = call(
-        sum_kernel,
-        (half_shape, half_shape),
+    weight_shape = (groups // 2, len(ROW_SHIFTS) * slots)
+    scratch = pltpu.VMEM((groups // 2, 4 * LANES), F32)
+    give, weights, total = call(
+        give_kernel,
+        (
+            shape((half_count, pixels + LANES), F32),
+            shape(weight_shape, BF16),
+            shape((half_count, LANES), F32),
+        ),
         4,
         8,
-        [
-            pltpu.VMEM((groups, len(ROW_SHIFTS) * slots), BF16),
-            pltpu.VMEM((groups, 4 * LANES), F32),
-        ],
-        flops=work,
+        [pltpu.VMEM(weight_shape, BF16), scratch],
+        flops=work // 2,
         moved=5 * MIB,
     )(scores, x, tile, everyone.reshape(owners * planes * 8, LANES))
     other = lax.ppermute(give, "dp", [(0, 1), (1, 0)])
+    keep = call(
+        keep_kernel,
+        shape((half_count, pixels), F32),
+        2,
+        8,
+        [scratch],
+        flops=work // 2,
+        moved=4 * MIB,
+    )(weights, x)
     sums, totals = call(
         finish_kernel,
         (shape((half_rots * tiles, LANES), F32), shape((1, half_rots), F32)),
-        2,
+        3,
         8,
         moved=2 * MIB,
-    )(keep, other)
+    )(keep, total, other)
     return sums.reshape(1, half_rots, pixels), totals
 
 

time: 99 us -> 98.2 us (level)
  waiting for transfers between devices: 7.56 us -> 6.39 us
    ppermute x1, waiting for transfers between devices: 1.75 us -> 0.58 us  [on_device(): other = lax.ppermute(give, 'dp', [(0, 1), (1, 0)])]
    pallas_call x1 -> x2, Pallas kernels: 2.34 us -> 2.73 us  [the longest x1 1.57 us: on_device(): call(give_kernel, (shape((half_count, pixels + LANES), F32), shape(weight...]
  transfers between devices with their start and end apart: 9 -> 9, of which waited for: 3 -> 3; matrix products, arithmetic and copies ran while one was open for 0% -> 0% of each run, Pallas kernels for 2% -> 3%
where the time goes in v4:
time: 98.2 us; the launch traced here: 97.9 us
  blocking collectives  54.8 us (56%)
  starting transfers between devices  23.5 us (24%)
  Pallas kernels  9.23 us (9%)
  waiting for transfers between devices  6.39 us (7%)
  local copies, waits for them, and re-layouts  3.36 us (3%)
    all_to_all x1, blocking collectives, on_device(): received = exchange(picked, 'xy')  31.3 us
    ppermute x8, starting transfers between devices, move(): lax.ppermute(part, 'z', [(i, (i + step) % planes) for i in range(planes)])  15.1 us
    all_to_all x1, blocking collectives, on_device(): exchange(jnp.broadcast_to(by_plane, (owners, planes * 8, LANES)), 'xy')  11.8 us
    all_to_all x1, blocking collectives, on_device(): by_plane = exchange(jnp.broadcast_to(tile[None], (planes, 8, LANES)), 'z')  11.6 us
    ppermute x1, starting transfers between devices, on_device(): other = lax.ppermute(give, 'dp', [(0, 1), (1, 0)])  8.36 us
    ppermute x8, waiting for transfers between devices, move(): lax.ppermute(part, 'z', [(i, (i + step) % planes) for i in range(planes)])  5.81 us
    unnamed x8, local copies, waits for them, and re-layouts  3.3 us
    pallas_call x1, Pallas kernels, on_device(): call(functools.partial(score_kernel, pad=pad), (shape((slots, pixels + 2...  2.09 us
  transfers between devices with their start and end apart: 9, of which 3 were waited for; matrix products, arithmetic and copies ran while one was open for 0% of the time, Pallas kernels for 3%

profile of v4, /device:TPU:1, one launch (start us, length us, event | category | flops | bytes accessed | tf_op | source)
XLA Modules:
  0.0 97.9 jit_solution(17444278638862560523)
XLA Ops:
  0.6 0.0 copy-start.1
  0.6 0.9 copy-done.1
  1.5 0.0 copy-start.2
  1.5 0.7 copy-done.2
  2.2 0.0 copy-start.3
  2.2 0.7 copy-done.3
  2.9 0.2 shard_map.59.refs_0_
  3.0 6.9 %collective-permute-start.3 = (bf16[528,128]{1,0:T(8,128)(2,1)S(1)}, bf16[528,128]{1,0:T(8,128)(2,1)S(1)}, u32[]{:S(2)}, u32[]{:S(2)}) collective-permute-start(bf16[528,128]{1,0:T(8,128)(2,1)S(1)} %shard_map.59.refs_0_), channel_id=1, source_target_pairs={{0,192},{32,224},{64,0},{96,32},{128,64},{160,96},{192,128},{224,1... | collective-permute-start | bytes 405512 | tf_op jit(solution)/shard_map/ppermute | solution.py:361
  9.9 0.0 collective-permute-start.2
  9.9 3.1 %collective-permute-start.1 = (bf16[528,128]{1,0:T(8,128)(2,1)S(1)}, bf16[528,128]{1,0:T(8,128)(2,1)S(1)}, u32[]{:S(2)}, u32[]{:S(2)}) collective-permute-start(bf16[528,128]{1,0:T(8,128)(2,1)S(1)} %shard_map.59.refs_0_), channel_id=1, source_target_pairs={{0,224},{32,0},{64,32},{96,64},{128,96},{160,128},{192,160},{224,1... | collective-permute-start | bytes 405512 | tf_op jit(solution)/shard_map/ppermute | solution.py:361
  13.1 0.0 collective-permute-start
  13.1 0.0 copy-start
  13.1 1.1 %copy-done = bf16[1,72,4096]{2,1,0:T(8,128)(2,1)S(1)} copy-done((bf16[1,72,4096]{2,1,0:T(8,128)(2,1)S(1)}, bf16[1,72,4096]{2,1,0:T(8,128)(2,1)}, u32[]{:S(2)}) %copy-start) | copy-done | bytes 589848
  14.1 1.6 %shard_map.60 = (bf16[720,4096]{1,0:T(8,128)(2,1)S(1)}, f32[80,128]{1,0:T(8,128)S(1)}) custom-call(bf16[72,4096]{1,0:T(8,128)(2,1)S(1)} %bitcast.7), custom_call_target="tpu_custom_call" | custom-call | bytes 12582912 | tf_op jit(solution)/shard_map/pallas_call | solution.py:370
  15.7 0.0 collective-permute-done.3.refs_4_
  15.7 1.8 %collective-permute-done.2.refs_3_ = bf16[528,128]{1,0:T(8,128)(2,1)S(1)} collective-permute-done((bf16[528,128]{1,0:T(8,128)(2,1)S(1)}, bf16[528,128]{1,0:T(8,128)(2,1)S(1)}, u32[]{:S(2)}, u32[]{:S(2)}) %collective-permute-start.2) | collective-permute-done | bytes 135200 | tf_op jit(solution)/shard_map/ppermute | solution.py:361
  17.5 2.2 %collective-permute-start.4 = (bf16[528,128]{1,0:T(8,128)(2,1)S(1)}, bf16[528,128]{1,0:T(8,128)(2,1)S(1)}, u32[]{:S(2)}, u32[]{:S(2)}) collective-permute-start(bf16[528,128]{1,0:T(8,128)(2,1)S(1)} %collective-permute-done.2.refs_3_), channel_id=1, source_target_pairs={{0,32},{32,64},{64,96},{96,128},{128,160},{160,192},{192,224},{224... | collective-permute-start | bytes 405512 | tf_op jit(solution)/shard_map/ppermute | solution.py:361
  19.7 0.5 collective-permute-start.5
  20.2 0.9 collective-permute-start.7
  21.1 0.0 collective-permute-done.1.refs_2_
  21.1 1.5 %collective-permute-start.6 = (bf16[256,128]{1,0:T(8,128)(2,1)S(1)}, bf16[256,128]{1,0:T(8,128)(2,1)S(1)}, u32[]{:S(2)}, u32[]{:S(2)}) collective-permute-start(bf16[256,128]{1,0:T(8,128)(2,1)S(1)} %slice.6), channel_id=1, source_target_pairs={{0,64},{32,96},{64,128},{96,160},{128,192},{160,224},{192,0},{224,... | collective-permute-start | bytes 196616 | tf_op jit(solution)/shard_map/ppermute | solution.py:361
  22.7 0.0 collective-permute-done.refs_1_
  22.7 4.0 %collective-permute-done.6.refs_7_ = bf16[256,128]{1,0:T(8,128)(2,1)S(1)} collective-permute-done((bf16[256,128]{1,0:T(8,128)(2,1)S(1)}, bf16[256,128]{1,0:T(8,128)(2,1)S(1)}, u32[]{:S(2)}, u32[]{:S(2)}) %collective-permute-start.6) | collective-permute-done | bytes 65568 | tf_op jit(solution)/shard_map/ppermute | solution.py:361
  26.7 0.0 collective-permute-done.7.refs_8_
  26.7 0.0 collective-permute-done.4.refs_5_
  26.7 0.0 collective-permute-done.5.refs_6_
  26.7 1.2 %shard_map.61 = bf16[16,528,128]{2,1,0:T(8,128)(2,1)S(1)} custom-call(bf16[528,128]{1,0:T(8,128)(2,1)S(1)} %shard_map.59.refs_0_, bf16[528,128]{1,0:T(8,128)(2,1)S(1)} %collective-permute-done.refs_1_, bf16[528,128]{1,0:T(8,128)(2,1)S(1)} %collective-permute-done.1.refs_2_, bf16[528,128]{1,0:T(8,128)(2,1)S(1)} %collective-permute-done.2.refs_3_, ...), custom_call_target="tpu_custom_call" | custom-call | bytes 3145728 | tf_op jit(solution)/shard_map/pallas_call | solution.py:384
  27.9 31.3 %all_to_all.15.recv_ref = bf16[16,528,128]{2,1,0:T(8,128)(2,1)S(1)} all-to-all(bf16[16,528,128]{2,1,0:T(8,128)(2,1)S(1)} %shard_map.61), channel_id=1, replica_groups=mesh['z'=8,'xy'=16,'dp'=2] {'xy'}, dimensions={0} | all-to-all | bytes 4325376 | tf_op jit(solution)/shard_map/all_to_all | solution.py:392
  59.2 2.1 %shard_map.62 = (bf16[256,4352]{1,0:T(8,128)(2,1)S(1)}, f32[240,768]{1,0:T(8,128)S(1)}, f32[8,128]{1,0:T(8,128)S(1)}) custom-call(bf16[16,528,128]{2,1,0:T(8,128)(2,1)S(1)} %all_to_all.15.recv_ref, bf16[720,4096]{1,0:T(8,128)(2,1)S(1)} %get-tuple-element.20.shifted_ref, f32[80,128]{1,0:T(8,128)S(1)} %get-tuple-element.21.half_ref), custom_call_target="tpu_custom_call" | custom-call | flops 1509949440 | bytes 10485760 | tf_op jit(solution)/shard_map/pallas_call | solution.py:394
  61.3 11.6 %all_to_all.16 = f32[8,8,128]{2,1,0:T(8,128)S(1)} all-to-all(f32[8,8,128]{2,1,0:T(8,128)S(1)} %broadcast_in_dim.17), channel_id=1, replica_groups=mesh['z'=8,'xy'=16,'dp'=2] {'z'}, dimensions={0} | all-to-all | bytes 65536 | tf_op jit(solution)/shard_map/all_to_all | solution.py:406
  72.9 11.8 %all_to_all.17 = f32[16,64,128]{2,1,0:T(8,128)S(1)} all-to-all(f32[16,64,128]{2,1,0:T(8,128)S(1)} %broadcast_in_dim.19), channel_id=1, replica_groups=mesh['z'=8,'xy'=16,'dp'=2] {'xy'}, dimensions={0} | all-to-all | bytes 1048576 | tf_op jit(solution)/shard_map/all_to_all | solution.py:408
  84.8 1.6 %shard_map.63 = (f32[40,4224]{1,0:T(8,128)S(1)}, bf16[120,768]{1,0:T(8,128)(2,1)S(1)}, f32[40,128]{1,0:T(8,128)S(1)}) custom-call(f32[240,768]{1,0:T(8,128)S(1)} %get-tuple-element.22.s_ref, bf16[256,4352]{1,0:T(8,128)(2,1)S(1)} %get-tuple-element.23.x_ref, f32[8,128]{1,0:T(8,128)S(1)} %get-tuple-element.24.mine_ref, f32[1024,128]{1,0:T(8,128)S(1)} %bitcast.6), custom_call_target="tpu_custom_call" | custom-call | flops 754974720 | bytes 5242880 | tf_op jit(solution)/shard_map/pallas_call | solution.py:411
  86.4 8.4 %collective-permute-start.8 = (f32[40,4224]{1,0:T(8,128)S(1)}, f32[40,4224]{1,0:T(8,128)S(1)}, u32[]{:S(2)}, u32[]{:S(2)}) collective-permute-start(f32[40,4224]{1,0:T(8,128)S(1)} %get-tuple-element.27), channel_id=1, source_target_pairs={{0,1},{1,0},{2,3},{3,2},{4,5},{5,4},{6,7},{7,6},{8,9},{9,8},{10,11... | collective-permute-start | bytes 2027528 | tf_op jit(solution)/shard_map/ppermute | solution.py:424
  94.7 1.2 %shard_map.64.keep_ref = f32[40,4096]{1,0:T(8,128)S(1)} custom-call(bf16[120,768]{1,0:T(8,128)(2,1)S(1)} %get-tuple-element.25.w_ref, bf16[256,4352]{1,0:T(8,128)(2,1)S(1)} %get-tuple-element.23.x_ref), custom_call_target="tpu_custom_call" | custom-call | flops 754974720 | bytes 4194304 | tf_op jit(solution)/shard_map/pallas_call | solution.py:425
  95.9 0.6 collective-permute-done.8.other_ref
  96.5 1.5 %shard_map.65 = (f32[1152,128]{1,0:T(8,128)}, f32[1,36]{1,0:T(1,128)}) custom-call(f32[40,4096]{1,0:T(8,128)S(1)} %shard_map.64.keep_ref, f32[40,128]{1,0:T(8,128)S(1)} %get-tuple-element.26.total_ref, f32[40,4224]{1,0:T(8,128)S(1)} %collective-permute-done.8.other_ref), custom_call_target="tpu_custom_call" | custom-call | bytes 2097152 | tf_op jit(solution)/shard_map/pallas_call | solution.py:434
  (4 shorter events, 0.1 us)
Async XLA Ops:
  0.6 0.9 copy-start.1
  1.5 0.7 copy-start.2
  2.2 0.7 copy-start.3
  3.0 12.7 %collective-permute-start.3 = (bf16[528,128]{1,0:T(8,128)(2,1)S(1)}, bf16[528,128]{1,0:T(8,128)(2,1)S(1)}, u32[]{:S(2)}, u32[]{:S(2)}) collective-permute-start(bf16[528,128]{1,0:T(8,128)(2,1)S(1)} %shard_map.59.refs_0_), channel_id=1, source_target_pairs={{0,192},{32,224},{64,0},{96,32},{128,64},{160,96},{192,128},{224,1... | collective-permute-start | bytes 405512 | tf_op jit(solution)/shard_map/ppermute | solution.py:361
  9.9 7.6 %collective-permute-start.2 = (bf16[528,128]{1,0:T(8,128)(2,1)S(1)}, bf16[528,128]{1,0:T(8,128)(2,1)S(1)}, u32[]{:S(2)}, u32[]{:S(2)}) collective-permute-start(bf16[528,128]{1,0:T(8,128)(2,1)S(1)} %shard_map.59.refs_0_), channel_id=1, source_target_pairs={{0,64},{32,96},{64,128},{96,160},{128,192},{160,224},{192,0},{224,... | collective-permute-start | bytes 405512 | tf_op jit(solution)/shard_map/ppermute | solution.py:361
  9.9 11.2 %collective-permute-start.1 = (bf16[528,128]{1,0:T(8,128)(2,1)S(1)}, bf16[528,128]{1,0:T(8,128)(2,1)S(1)}, u32[]{:S(2)}, u32[]{:S(2)}) collective-permute-start(bf16[528,128]{1,0:T(8,128)(2,1)S(1)} %shard_map.59.refs_0_), channel_id=1, source_target_pairs={{0,224},{32,0},{64,32},{96,64},{128,96},{160,128},{192,160},{224,1... | collective-permute-start | bytes 405512 | tf_op jit(solution)/shard_map/ppermute | solution.py:361
  13.1 9.6 %collective-permute-start = (bf16[528,128]{1,0:T(8,128)(2,1)S(1)}, bf16[528,128]{1,0:T(8,128)(2,1)S(1)}, u32[]{:S(2)}, u32[]{:S(2)}) collective-permute-start(bf16[528,128]{1,0:T(8,128)(2,1)S(1)} %shard_map.59.refs_0_), channel_id=1, source_target_pairs={{0,32},{32,64},{64,96},{96,128},{128,160},{160,192},{192,224},{224... | collective-permute-start | bytes 405512 | tf_op jit(solution)/shard_map/ppermute | solution.py:361
  13.1 1.1 %copy-start = (bf16[1,72,4096]{2,1,0:T(8,128)(2,1)S(1)}, bf16[1,72,4096]{2,1,0:T(8,128)(2,1)}, u32[]{:S(2)}) copy-start(bf16[1,72,4096]{2,1,0:T(8,128)(2,1)} %param.5) | copy-start | bytes 1769476
  17.5 9.2 %collective-permute-start.4 = (bf16[528,128]{1,0:T(8,128)(2,1)S(1)}, bf16[528,128]{1,0:T(8,128)(2,1)S(1)}, u32[]{:S(2)}, u32[]{:S(2)}) collective-permute-start(bf16[528,128]{1,0:T(8,128)(2,1)S(1)} %collective-permute-done.2.refs_3_), channel_id=1, source_target_pairs={{0,32},{32,64},{64,96},{96,128},{128,160},{160,192},{192,224},{224... | collective-permute-start | bytes 405512 | tf_op jit(solution)/shard_map/ppermute | solution.py:361
  19.7 7.0 %collective-permute-start.5 = (bf16[528,128]{1,0:T(8,128)(2,1)S(1)}, bf16[528,128]{1,0:T(8,128)(2,1)S(1)}, u32[]{:S(2)}, u32[]{:S(2)}) collective-permute-start(bf16[528,128]{1,0:T(8,128)(2,1)S(1)} %collective-permute-done.3.refs_4_), channel_id=1, source_target_pairs={{0,224},{32,0},{64,32},{96,64},{128,96},{160,128},{192,160},{224,1... | collective-permute-start | bytes 405512 | tf_op jit(solution)/shard_map/ppermute | solution.py:361
  20.2 6.5 %collective-permute-start.7 = (bf16[272,128]{1,0:T(8,128)(2,1)S(1)}, bf16[272,128]{1,0:T(8,128)(2,1)S(1)}, u32[]{:S(2)}, u32[]{:S(2)}) collective-permute-start(bf16[272,128]{1,0:T(8,128)(2,1)S(1)} %slice.7), channel_id=1, source_target_pairs={{0,192},{32,224},{64,0},{96,32},{128,64},{160,96},{192,128},{224,1... | collective-permute-start | bytes 208904 | tf_op jit(solution)/shard_map/ppermute | solution.py:361
  21.1 5.5 %collective-permute-start.6 = (bf16[256,128]{1,0:T(8,128)(2,1)S(1)}, bf16[256,128]{1,0:T(8,128)(2,1)S(1)}, u32[]{:S(2)}, u32[]{:S(2)}) collective-permute-start(bf16[256,128]{1,0:T(8,128)(2,1)S(1)} %slice.6), channel_id=1, source_target_pairs={{0,64},{32,96},{64,128},{96,160},{128,192},{160,224},{192,0},{224,... | collective-permute-start | bytes 196616 | tf_op jit(solution)/shard_map/ppermute | solution.py:361
  86.4 10.1 %collective-permute-start.8 = (f32[40,4224]{1,0:T(8,128)S(1)}, f32[40,4224]{1,0:T(8,128)S(1)}, u32[]{:S(2)}, u32[]{:S(2)}) collective-permute-start(f32[40,4224]{1,0:T(8,128)S(1)} %get-tuple-element.27), channel_id=1, source_target_pairs={{0,1},{1,0},{2,3},{3,2},{4,5},{5,4},{6,7},{7,6},{8,9},{9,8},{10,11... | collective-permute-start | bytes 2027528 | tf_op jit(solution)/shard_map/ppermute | solution.py:424

commit v5 on v4

--- a/solution.py
+++ b/solution.py
@@ -73,29 +73,26 @@
 
 
 def pick_kernel(*refs, steps, top):
-    planes = len(steps) - 1
-    recv_refs, send_ref, column_ref = refs[: len(steps)], refs[-2], refs[-1]
+    planes = len(steps)
+    recv_refs, send_ref, column_ref = refs[:planes], refs[-2], refs[-1]
     owners, depth, _ = send_ref.shape
     rows = column_ref.shape[0] // planes
     tiles = column_ref.shape[1] // LANES
     group = depth // tiles
     slots = owners * group
-    cut = recv_refs[-2].shape[0] // rows
     for j in range(planes):
         for t in range(tiles):
-            from_ref, at = recv_refs[j], t
-            if j == planes - 1 and t >= cut:
-                from_ref, at = recv_refs[j + 1], t - cut
-            column_ref[j * rows : (j + 1) * rows, tile_of(t)] = from_ref[
-                at * rows : (at + 1) * rows
+            column_ref[j * rows : (j + 1) * rows, tile_of(t)] = recv_refs[j][
+                t * rows : (t + 1) * rows
             ]
     count = planes * rows
     facts = column_ref[:, tile_of(tiles - 1)].astype(F32)
     here = lax.axis_index("z")
+    way = 1 - 2 * lax.axis_index("dp")
     row = lax.broadcasted_iota(jnp.int32, (count, 1), 0)
     sender = jnp.zeros((count, 1), jnp.int32)
     for j in range(planes):
-        plane = lax.rem(here + steps[j] + planes, planes)
+        plane = lax.rem(here + way * steps[j] + planes, planes)
         sender = jnp.where(row // rows == j, plane, sender)
     lane = lax.broadcasted_iota(jnp.int32, (1, slots), 1)
     cls = (here * owners + lane // group).astype(F32)
@@ -123,7 +120,8 @@
                 ]
 
 
-def shift_kernel(from_ref, out_ref, half_ref, rot_ref):
+def shift_kernel(from_ref, packed_ref, out_ref, half_ref, own_ref, rot_ref):
+    own_ref[...] = packed_ref[...]
     count, pixels = rot_ref.shape
     rots = from_ref.shape[0]
     half_count, half_rots = count // 2, rots // 2
@@ -353,34 +351,45 @@
         pack_kernel,
         shape(((tiles + 1) * rows, LANES), BF16),
         3,
-        4,
+        54,
         moved=MIB // 4,
     )(candidates.T, inv_noise[None, :], images)
 
     def move(part, step):
-        return lax.ppermute(part, "z", [(i, (i + step) % planes) for i in range(planes)])
+        pairs = []
+        for z in range(planes):
+            pairs += [
+                (2 * z, (z + step) % planes * 2),
+                (2 * z + 1, (z - step) % planes * 2 + 1),
+            ]
+        return lax.ppermute(part, ("z", "dp"), pairs)
 
     near = [move(packed, step) for step in (1, -1)]
     next_near = [move(packed, step) for step in (2, -2)]
+
     half_rots = rots // 2
     half_count = -(-half_rots // 8) * 8
     pad = half_count - half_rots
     count = 2 * half_count
     groups = len(COL_SHIFTS) * count
-    shifted, half_norm = call(
+    shifted, half_norm, own = call(
         shift_kernel,
-        (shape((len(ROW_SHIFTS) * groups, pixels), BF16), shape((count, LANES), F32)),
-        1,
+        (
+            shape((len(ROW_SHIFTS) * groups, pixels), BF16),
+            shape((count, LANES), F32),
+            shape(packed.shape, BF16),
+        ),
+        2,
         6,
         [pltpu.VMEM((count, pixels), BF16)],
         moved=12 * MIB,
-    )(references[0])
-    next_near, shifted, half_norm = lax.optimization_barrier((next_near, shifted, half_norm))
-    cut = (tiles + 1) // 2 * rows
-    far = [move(next_near[0], 1), move(next_near[1], -1)]
-    far += [move(next_near[0][:cut], 2), move(next_near[1][cut:], -2)]
-    column = [packed, *near, *next_near, *far]
-    steps = [0, -1, 1, -2, 2, -3, 3, 4, 4]
+    )(references[0], packed)
+    next_near, shifted, half_norm, own = lax.optimization_barrier(
+        (next_near, shifted, half_norm, own)
+    )
+    far = [move(next_near[0], 1), move(next_near[1], -1), move(next_near[0], 2)]
+    column = [own, *near, *next_near, *far]
+    steps = [0, -1, 1, -2, 2, -3, 3, 4]
     picked = call(
         functools.partial(pick_kernel, steps=steps, top=top),
         shape((owners, (tiles + 1) * group, LANES), BF16),

time: 98.2 us -> 98.4 us (level)
  starting transfers between devices: 23.5 us -> 19.9 us
  blocking collectives: 54.8 us -> 56.8 us
  waiting for transfers between devices: 6.39 us -> 8.24 us
  Pallas kernels: 9.23 us -> 10.6 us
  local copies, waits for them, and re-layouts: 3.36 us -> 2.02 us
    all_to_all x1, blocking collectives: 11.6 us -> 14.4 us  [on_device(): by_plane = exchange(jnp.broadcast_to(tile[None], (planes, 8, LANES)), 'z')]
    ppermute x1, starting transfers between devices: 8.36 us -> 5.89 us  [on_device(): other = lax.ppermute(give, 'dp', [(0, 1), (1, 0)])]
    ppermute x8 -> x7, waiting for transfers between devices: 5.81 us -> 7.6 us  [move(): return lax.ppermute(part, ('z', 'dp'), pairs)]
    pallas_call x1, Pallas kernels: 0.17 us -> 1.77 us  [on_device(): call(pack_kernel, shape(((tiles + 1) * rows, LANES), BF16), 3, 54, moved=...]
    unnamed x8 -> x4, local copies, waits for them, and re-layouts: 3.3 us -> 1.97 us
    ppermute x8 -> x7, starting transfers between devices: 15.1 us -> 14 us  [move(): return lax.ppermute(part, ('z', 'dp'), pairs)]
  transfers between devices with their start and end apart: 9 -> 8, of which waited for: 3 -> 5; matrix products, arithmetic and copies ran while one was open for 0% -> 0% of each run, Pallas kernels for 3% -> 3%
where the time goes in v5:
time: 98.4 us; the launch traced here: 98.2 us
  blocking collectives  56.8 us (58%)
  starting transfers between devices  19.9 us (20%)
  Pallas kernels  10.6 us (11%)
  waiting for transfers between devices  8.24 us (8%)
  local copies, waits for them, and re-layouts  2.02 us (2%)
    all_to_all x1, blocking collectives, on_device(): received = exchange(picked, 'xy')  30.8 us
    all_to_all x1, blocking collectives, on_device(): by_plane = exchange(jnp.broadcast_to(tile[None], (planes, 8, LANES)), 'z')  14.4 us
    ppermute x7, starting transfers between devices, move(): return lax.ppermute(part, ('z', 'dp'), pairs)  14 us
    all_to_all x1, blocking collectives, on_device(): exchange(jnp.broadcast_to(by_plane, (owners, planes * 8, LANES)), 'xy')  11.6 us
    ppermute x7, waiting for transfers between devices, move(): return lax.ppermute(part, ('z', 'dp'), pairs)  7.6 us
    ppermute x1, starting transfers between devices, on_device(): other = lax.ppermute(give, 'dp', [(0, 1), (1, 0)])  5.89 us
    pallas_call x1, Pallas kernels, on_device(): call(functools.partial(score_kernel, pad=pad), (shape((slots, pixels + 2...  2.04 us
    unnamed x4, local copies, waits for them, and re-layouts  1.97 us
  transfers between devices with their start and end apart: 8, of which 5 were waited for; matrix products, arithmetic and copies ran while one was open for 0% of the time, Pallas kernels for 3%

profile of v5, /device:TPU:1, one launch (start us, length us, event | category | flops | bytes accessed | tf_op | source)
XLA Modules:
  0.0 98.2 jit_solution(13609738992741382907)
XLA Ops:
  0.6 1.8 %shard_map.59.packed_ref = bf16[528,128]{1,0:T(8,128)(2,1)} custom-call(s32[8,16]{1,0:T(8,128)} %bitcast.9, bf16[1,16]{1,0:T(2,128)(2,1)} %bitcast.10, bf16[16,4096]{1,0:T(8,128)(2,1)} %img_ref.1), custom_call_target="tpu_custom_call" | custom-call | bytes 262144 | tf_op jit(solution)/shard_map/pallas_call | solution.py:350
  2.4 3.8 %collective-permute-start.1 = (bf16[528,128]{1,0:T(8,128)(2,1)}, bf16[528,128]{1,0:T(8,128)(2,1)S(1)}, u32[]{:S(2)}, u32[]{:S(2)}) collective-permute-start(bf16[528,128]{1,0:T(8,128)(2,1)} %shard_map.59.packed_ref), channel_id=1, source_target_pairs={{0,192},{1,65},{32,224},{33,97},{64,0},{65,129},{96,32},{97,161},{... | collective-permute-start | bytes 405512 | tf_op jit(solution)/shard_map/ppermute | solution.py:365
  6.2 3.0 %collective-permute-start = (bf16[528,128]{1,0:T(8,128)(2,1)}, bf16[528,128]{1,0:T(8,128)(2,1)S(1)}, u32[]{:S(2)}, u32[]{:S(2)}) collective-permute-start(bf16[528,128]{1,0:T(8,128)(2,1)} %shard_map.59.packed_ref), channel_id=1, source_target_pairs={{0,64},{1,193},{32,96},{33,225},{64,128},{65,1},{96,160},{97,33},{... | collective-permute-start | bytes 405512 | tf_op jit(solution)/shard_map/ppermute | solution.py:365
  9.2 0.7 collective-permute-start.3
  10.0 1.9 %collective-permute-start.2 = (bf16[528,128]{1,0:T(8,128)(2,1)}, bf16[528,128]{1,0:T(8,128)(2,1)S(1)}, u32[]{:S(2)}, u32[]{:S(2)}) collective-permute-start(bf16[528,128]{1,0:T(8,128)(2,1)} %shard_map.59.packed_ref), channel_id=1, source_target_pairs={{0,32},{1,225},{32,64},{33,1},{64,96},{65,33},{96,128},{97,65},{12... | collective-permute-start | bytes 405512 | tf_op jit(solution)/shard_map/ppermute | solution.py:365
  11.9 0.0 copy-start
  11.9 1.1 %copy-done = bf16[1,72,4096]{2,1,0:T(8,128)(2,1)S(1)} copy-done((bf16[1,72,4096]{2,1,0:T(8,128)(2,1)S(1)}, bf16[1,72,4096]{2,1,0:T(8,128)(2,1)}, u32[]{:S(2)}) %copy-start) | copy-done | bytes 589848
  13.0 0.0 copy-start.1
  13.0 0.9 copy-done.1
  13.9 1.6 %shard_map.60 = (bf16[720,4096]{1,0:T(8,128)(2,1)S(1)}, f32[80,128]{1,0:T(8,128)S(1)}, bf16[528,128]{1,0:T(8,128)(2,1)S(1)}) custom-call(bf16[72,4096]{1,0:T(8,128)(2,1)S(1)} %bitcast.7, bf16[528,128]{1,0:T(8,128)(2,1)S(1)} %copy-done.1), custom_call_target="tpu_custom_call" | custom-call | bytes 12582912 | tf_op jit(solution)/shard_map/pallas_call | solution.py:375
  15.5 0.0 collective-permute-done.1.refs_4_
  15.5 0.8 collective-permute-done.refs_3_
  16.3 0.0 collective-permute-start.5
  16.3 4.3 %collective-permute-start.6 = (bf16[528,128]{1,0:T(8,128)(2,1)S(1)}, bf16[528,128]{1,0:T(8,128)(2,1)S(1)}, u32[]{:S(2)}, u32[]{:S(2)}) collective-permute-start(bf16[528,128]{1,0:T(8,128)(2,1)S(1)} %collective-permute-done.refs_3_), channel_id=1, source_target_pairs={{0,64},{1,193},{32,96},{33,225},{64,128},{65,1},{96,160},{97,33},{... | collective-permute-start | bytes 405512 | tf_op jit(solution)/shard_map/ppermute | solution.py:365
  20.6 0.2 collective-permute-start.4
  20.8 0.0 collective-permute-done.3.refs_2_
  20.8 0.0 collective-permute-done.2.refs_1_
  20.8 1.0 %collective-permute-done.5.refs_6_ = bf16[528,128]{1,0:T(8,128)(2,1)S(1)} collective-permute-done((bf16[528,128]{1,0:T(8,128)(2,1)S(1)}, bf16[528,128]{1,0:T(8,128)(2,1)S(1)}, u32[]{:S(2)}, u32[]{:S(2)}) %collective-permute-start.5) | collective-permute-done | bytes 135200 | tf_op jit(solution)/shard_map/ppermute | solution.py:365
  21.8 3.9 %collective-permute-done.6.refs_7_ = bf16[528,128]{1,0:T(8,128)(2,1)S(1)} collective-permute-done((bf16[528,128]{1,0:T(8,128)(2,1)S(1)}, bf16[528,128]{1,0:T(8,128)(2,1)S(1)}, u32[]{:S(2)}, u32[]{:S(2)}) %collective-permute-start.6) | collective-permute-done | bytes 135200 | tf_op jit(solution)/shard_map/ppermute | solution.py:365
  25.7 1.8 %collective-permute-done.4.refs_5_ = bf16[528,128]{1,0:T(8,128)(2,1)S(1)} collective-permute-done((bf16[528,128]{1,0:T(8,128)(2,1)S(1)}, bf16[528,128]{1,0:T(8,128)(2,1)S(1)}, u32[]{:S(2)}, u32[]{:S(2)}) %collective-permute-start.4) | collective-permute-done | bytes 135200 | tf_op jit(solution)/shard_map/ppermute | solution.py:365
  27.6 1.2 %shard_map.61 = bf16[16,528,128]{2,1,0:T(8,128)(2,1)S(1)} custom-call(bf16[528,128]{1,0:T(8,128)(2,1)S(1)} %get-tuple-element.21.refs_0_, bf16[528,128]{1,0:T(8,128)(2,1)S(1)} %collective-permute-done.2.refs_1_, bf16[528,128]{1,0:T(8,128)(2,1)S(1)} %collective-permute-done.3.refs_2_, bf16[528,128]{1,0:T(8,128)(2,1)S(1)} %collective-permute-done.refs_3_, ...), custom_call_target="tpu_custom_call" | custom-call | bytes 3145728 | tf_op jit(solution)/shard_map/pallas_call | solution.py:393
  28.7 30.8 %all_to_all.15.recv_ref = bf16[16,528,128]{2,1,0:T(8,128)(2,1)S(1)} all-to-all(bf16[16,528,128]{2,1,0:T(8,128)(2,1)S(1)} %shard_map.61), channel_id=1, replica_groups=mesh['z'=8,'xy'=16,'dp'=2] {'xy'}, dimensions={0} | all-to-all | bytes 4325376 | tf_op jit(solution)/shard_map/all_to_all | solution.py:401
  59.5 2.0 %shard_map.62 = (bf16[256,4352]{1,0:T(8,128)(2,1)S(1)}, f32[240,768]{1,0:T(8,128)S(1)}, f32[8,128]{1,0:T(8,128)S(1)}) custom-call(bf16[16,528,128]{2,1,0:T(8,128)(2,1)S(1)} %all_to_all.15.recv_ref, bf16[720,4096]{1,0:T(8,128)(2,1)S(1)} %get-tuple-element.24.shifted_ref, f32[80,128]{1,0:T(8,128)S(1)} %get-tuple-element.25.half_ref), custom_call_target="tpu_custom_call" | custom-call | flops 1509949440 | bytes 10485760 | tf_op jit(solution)/shard_map/pallas_call | solution.py:403
  61.5 14.4 %all_to_all.16 = f32[8,8,128]{2,1,0:T(8,128)S(1)} all-to-all(f32[8,8,128]{2,1,0:T(8,128)S(1)} %broadcast_in_dim.17), channel_id=1, replica_groups=mesh['z'=8,'xy'=16,'dp'=2] {'z'}, dimensions={0} | all-to-all | bytes 65536 | tf_op jit(solution)/shard_map/all_to_all | solution.py:415
  76.0 11.6 %all_to_all.17 = f32[16,64,128]{2,1,0:T(8,128)S(1)} all-to-all(f32[16,64,128]{2,1,0:T(8,128)S(1)} %broadcast_in_dim.19), channel_id=1, replica_groups=mesh['z'=8,'xy'=16,'dp'=2] {'xy'}, dimensions={0} | all-to-all | bytes 1048576 | tf_op jit(solution)/shard_map/all_to_all | solution.py:417
  87.6 1.4 %shard_map.63 = (f32[40,4224]{1,0:T(8,128)S(1)}, bf16[120,768]{1,0:T(8,128)(2,1)S(1)}, f32[40,128]{1,0:T(8,128)S(1)}) custom-call(f32[240,768]{1,0:T(8,128)S(1)} %get-tuple-element.26.s_ref, bf16[256,4352]{1,0:T(8,128)(2,1)S(1)} %get-tuple-element.27.x_ref, f32[8,128]{1,0:T(8,128)S(1)} %get-tuple-element.28.mine_ref, f32[1024,128]{1,0:T(8,128)S(1)} %bitcast.6), custom_call_target="tpu_custom_call" | custom-call | flops 754974720 | bytes 5242880 | tf_op jit(solution)/shard_map/pallas_call | solution.py:420
  89.1 5.9 %collective-permute-start.7 = (f32[40,4224]{1,0:T(8,128)S(1)}, f32[40,4224]{1,0:T(8,128)S(1)}, u32[]{:S(2)}, u32[]{:S(2)}) collective-permute-start(f32[40,4224]{1,0:T(8,128)S(1)} %get-tuple-element.31), channel_id=1, source_target_pairs={{0,1},{1,0},{2,3},{3,2},{4,5},{5,4},{6,7},{7,6},{8,9},{9,8},{10,11... | collective-permute-start | bytes 2027528 | tf_op jit(solution)/shard_map/ppermute | solution.py:433
  94.9 1.1 %shard_map.64.keep_ref = f32[40,4096]{1,0:T(8,128)S(1)} custom-call(bf16[120,768]{1,0:T(8,128)(2,1)S(1)} %get-tuple-element.29.w_ref, bf16[256,4352]{1,0:T(8,128)(2,1)S(1)} %get-tuple-element.27.x_ref), custom_call_target="tpu_custom_call" | custom-call | flops 754974720 | bytes 4194304 | tf_op jit(solution)/shard_map/pallas_call | solution.py:434
  96.1 0.6 collective-permute-done.7.other_ref
  96.7 1.5 %shard_map.65 = (f32[1152,128]{1,0:T(8,128)}, f32[1,36]{1,0:T(1,128)}) custom-call(f32[40,4096]{1,0:T(8,128)S(1)} %shard_map.64.keep_ref, f32[40,128]{1,0:T(8,128)S(1)} %get-tuple-element.30.total_ref, f32[40,4224]{1,0:T(8,128)S(1)} %collective-permute-done.7.other_ref), custom_call_target="tpu_custom_call" | custom-call | bytes 2097152 | tf_op jit(solution)/shard_map/pallas_call | solution.py:443
  (2 shorter events, 0.0 us)
Async XLA Ops:
  2.4 13.1 %collective-permute-start.1 = (bf16[528,128]{1,0:T(8,128)(2,1)}, bf16[528,128]{1,0:T(8,128)(2,1)S(1)}, u32[]{:S(2)}, u32[]{:S(2)}) collective-permute-start(bf16[528,128]{1,0:T(8,128)(2,1)} %shard_map.59.packed_ref), channel_id=1, source_target_pairs={{0,192},{1,65},{32,224},{33,97},{64,0},{65,129},{96,32},{97,161},{... | collective-permute-start | bytes 405512 | tf_op jit(solution)/shard_map/ppermute | solution.py:365
  6.2 10.1 %collective-permute-start = (bf16[528,128]{1,0:T(8,128)(2,1)}, bf16[528,128]{1,0:T(8,128)(2,1)S(1)}, u32[]{:S(2)}, u32[]{:S(2)}) collective-permute-start(bf16[528,128]{1,0:T(8,128)(2,1)} %shard_map.59.packed_ref), channel_id=1, source_target_pairs={{0,64},{1,193},{32,96},{33,225},{64,128},{65,1},{96,160},{97,33},{... | collective-permute-start | bytes 405512 | tf_op jit(solution)/shard_map/ppermute | solution.py:365
  9.2 11.5 %collective-permute-start.3 = (bf16[528,128]{1,0:T(8,128)(2,1)}, bf16[528,128]{1,0:T(8,128)(2,1)S(1)}, u32[]{:S(2)}, u32[]{:S(2)}) collective-permute-start(bf16[528,128]{1,0:T(8,128)(2,1)} %shard_map.59.packed_ref), channel_id=1, source_target_pairs={{0,224},{1,33},{32,0},{33,65},{64,32},{65,97},{96,64},{97,129},{12... | collective-permute-start | bytes 405512 | tf_op jit(solution)/shard_map/ppermute | solution.py:365
  10.0 10.8 %collective-permute-start.2 = (bf16[528,128]{1,0:T(8,128)(2,1)}, bf16[528,128]{1,0:T(8,128)(2,1)S(1)}, u32[]{:S(2)}, u32[]{:S(2)}) collective-permute-start(bf16[528,128]{1,0:T(8,128)(2,1)} %shard_map.59.packed_ref), channel_id=1, source_target_pairs={{0,32},{1,225},{32,64},{33,1},{64,96},{65,33},{96,128},{97,65},{12... | collective-permute-start | bytes 405512 | tf_op jit(solution)/shard_map/ppermute | solution.py:365
  11.9 1.1 %copy-start = (bf16[1,72,4096]{2,1,0:T(8,128)(2,1)S(1)}, bf16[1,72,4096]{2,1,0:T(8,128)(2,1)}, u32[]{:S(2)}) copy-start(bf16[1,72,4096]{2,1,0:T(8,128)(2,1)} %param.5) | copy-start | bytes 1769476
  13.0 0.9 copy-start.1
  16.3 5.5 %collective-permute-start.5 = (bf16[528,128]{1,0:T(8,128)(2,1)S(1)}, bf16[528,128]{1,0:T(8,128)(2,1)S(1)}, u32[]{:S(2)}, u32[]{:S(2)}) collective-permute-start(bf16[528,128]{1,0:T(8,128)(2,1)S(1)} %collective-permute-done.1.refs_4_), channel_id=1, source_target_pairs={{0,224},{1,33},{32,0},{33,65},{64,32},{65,97},{96,64},{97,129},{12... | collective-permute-start | bytes 405512 | tf_op jit(solution)/shard_map/ppermute | solution.py:365
  16.3 9.4 %collective-permute-start.6 = (bf16[528,128]{1,0:T(8,128)(2,1)S(1)}, bf16[528,128]{1,0:T(8,128)(2,1)S(1)}, u32[]{:S(2)}, u32[]{:S(2)}) collective-permute-start(bf16[528,128]{1,0:T(8,128)(2,1)S(1)} %collective-permute-done.refs_3_), channel_id=1, source_target_pairs={{0,64},{1,193},{32,96},{33,225},{64,128},{65,1},{96,160},{97,33},{... | collective-permute-start | bytes 405512 | tf_op jit(solution)/shard_map/ppermute | solution.py:365
  20.6 7.0 %collective-permute-start.4 = (bf16[528,128]{1,0:T(8,128)(2,1)S(1)}, bf16[528,128]{1,0:T(8,128)(2,1)S(1)}, u32[]{:S(2)}, u32[]{:S(2)}) collective-permute-start(bf16[528,128]{1,0:T(8,128)(2,1)S(1)} %collective-permute-done.refs_3_), channel_id=1, source_target_pairs={{0,32},{1,225},{32,64},{33,1},{64,96},{65,33},{96,128},{97,65},{12... | collective-permute-start | bytes 405512 | tf_op jit(solution)/shard_map/ppermute | solution.py:365
  89.1 7.6 %collective-permute-start.7 = (f32[40,4224]{1,0:T(8,128)S(1)}, f32[40,4224]{1,0:T(8,128)S(1)}, u32[]{:S(2)}, u32[]{:S(2)}) collective-permute-start(f32[40,4224]{1,0:T(8,128)S(1)} %get-tuple-element.31), channel_id=1, source_target_pairs={{0,1},{1,0},{2,3},{3,2},{4,5},{5,4},{6,7},{7,6},{8,9},{9,8},{10,11... | collective-permute-start | bytes 2027528 | tf_op jit(solution)/shard_map/ppermute | solution.py:433

commit v6 on v5

--- a/solution.py
+++ b/solution.py
@@ -166,7 +166,12 @@
                     out_ref[first : first + count, tile_of(at)] = value
 
 
-def score_kernel(recv_ref, shifted_ref, half_ref, x_ref, s_ref, tile_ref, *, pad):
+def score_kernel(
+    recv_at, shifted_ref, half_ref, x_ref, s_ref, tile_ref, recv_ref, sem, *, pad
+):
+    load = pltpu.make_async_copy(recv_at, recv_ref, sem)
+    load.start()
+    load.wait()
     owners, depth, _ = recv_ref.shape
     tiles = x_ref.shape[1] // LANES - 2
     group = depth // (tiles + 1)
@@ -322,12 +327,12 @@
     totals_ref[...] = jnp.sum(jnp.where(here, total, 0.0), axis=0, keepdims=True)[:, :rots]
 
 
-def call(kernel, out_shape, count, limit, scratch=(), flops=0, moved=0, space=pltpu.VMEM):
+def call(kernel, out_shape, count, limit, scratch=(), flops=0, moved=0, far=0):
     in_vmem = pl.BlockSpec(memory_space=pltpu.VMEM)
     return pl.pallas_call(
         kernel,
         out_shape=out_shape,
-        in_specs=[pl.BlockSpec(memory_space=space)] * count,
+        in_specs=[pl.BlockSpec(memory_space=pltpu.HBM)] * far + [in_vmem] * (count - far),
         out_specs=jax.tree.map(lambda _: in_vmem, out_shape),
         scratch_shapes=list(scratch),
         cost_estimate=pl.CostEstimate(flops=flops, bytes_accessed=moved, transcendentals=0),
@@ -398,7 +403,7 @@
         [pltpu.VMEM((planes * rows, (tiles + 1) * LANES), BF16)],
         moved=3 * MIB,
     )(*column)
-    received = exchange(picked, "xy")
+    received = pltpu.with_memory_space_constraint(exchange(picked, "xy"), pltpu.HBM)
     work = 2 * len(ROW_SHIFTS) * groups * slots * pixels
     x, scores, tile = call(
         functools.partial(score_kernel, pad=pad),
@@ -409,8 +414,10 @@
         ),
         3,
         8,
+        [pltpu.VMEM(picked.shape, BF16), pltpu.SemaphoreType.DMA],
         flops=work,
         moved=10 * MIB,
+        far=1,
     )(received, shifted, half_norm)
     by_plane = exchange(jnp.broadcast_to(tile[None], (planes, 8, LANES)), "z")
     by_plane = by_plane.reshape(1, planes * 8, LANES)

time: 98.4 us -> 100 us (1.016)
  Pallas kernels: 10.6 us -> 12.2 us
    pallas_call x1, Pallas kernels: 2.04 us -> 3.68 us  [on_device(): call(functools.partial(score_kernel, pad=pad), (shape((slots, pixels + 2...]
where the time goes in v6:
time: 100 us; the launch traced here: 99.9 us
  blocking collectives  56.9 us (57%)
  starting transfers between devices  19.9 us (20%)
  Pallas kernels  12.2 us (12%)
  waiting for transfers between devices  8.24 us (8%)
  local copies, waits for them, and re-layouts  2.02 us (2%)
    all_to_all x1, blocking collectives, on_device(): exchange(picked, 'xy')  30.9 us
    all_to_all x1, blocking collectives, on_device(): by_plane = exchange(jnp.broadcast_to(tile[None], (planes, 8, LANES)), 'z')  14.4 us
    ppermute x7, starting transfers between devices, move(): return lax.ppermute(part, ('z', 'dp'), pairs)  14 us
    all_to_all x1, blocking collectives, on_device(): exchange(jnp.broadcast_to(by_plane, (owners, planes * 8, LANES)), 'xy')  11.6 us
    ppermute x7, waiting for transfers between devices, move(): return lax.ppermute(part, ('z', 'dp'), pairs)  7.6 us
    ppermute x1, starting transfers between devices, on_device(): other = lax.ppermute(give, 'dp', [(0, 1), (1, 0)])  5.89 us
    pallas_call x1, Pallas kernels, on_device(): call(functools.partial(score_kernel, pad=pad), (shape((slots, pixels + 2...  3.68 us
  transfers between devices with their start and end apart: 8, of which 5 were waited for; matrix products, arithmetic and copies ran while one was open for 0% of the time, Pallas kernels for 3%

profile of v6, /device:TPU:1, one launch (start us, length us, event | category | flops | bytes accessed | tf_op | source)
XLA Modules:
  0.0 99.9 jit_solution(6857620098754475153)
XLA Ops:
  0.6 1.8 %shard_map.59.packed_ref = bf16[528,128]{1,0:T(8,128)(2,1)} custom-call(s32[8,16]{1,0:T(8,128)} %bitcast.9, bf16[1,16]{1,0:T(2,128)(2,1)} %bitcast.10, bf16[16,4096]{1,0:T(8,128)(2,1)} %img_ref.1), custom_call_target="tpu_custom_call" | custom-call | bytes 262144 | tf_op jit(solution)/shard_map/pallas_call | solution.py:355
  2.4 3.8 %collective-permute-start.1 = (bf16[528,128]{1,0:T(8,128)(2,1)}, bf16[528,128]{1,0:T(8,128)(2,1)S(1)}, u32[]{:S(2)}, u32[]{:S(2)}) collective-permute-start(bf16[528,128]{1,0:T(8,128)(2,1)} %shard_map.59.packed_ref), channel_id=1, source_target_pairs={{0,192},{1,65},{32,224},{33,97},{64,0},{65,129},{96,32},{97,161},{... | collective-permute-start | bytes 405512 | tf_op jit(solution)/shard_map/ppermute | solution.py:370
  6.2 3.0 %collective-permute-start = (bf16[528,128]{1,0:T(8,128)(2,1)}, bf16[528,128]{1,0:T(8,128)(2,1)S(1)}, u32[]{:S(2)}, u32[]{:S(2)}) collective-permute-start(bf16[528,128]{1,0:T(8,128)(2,1)} %shard_map.59.packed_ref), channel_id=1, source_target_pairs={{0,64},{1,193},{32,96},{33,225},{64,128},{65,1},{96,160},{97,33},{... | collective-permute-start | bytes 405512 | tf_op jit(solution)/shard_map/ppermute | solution.py:370
  9.2 0.7 collective-permute-start.3
  10.0 1.9 %collective-permute-start.2 = (bf16[528,128]{1,0:T(8,128)(2,1)}, bf16[528,128]{1,0:T(8,128)(2,1)S(1)}, u32[]{:S(2)}, u32[]{:S(2)}) collective-permute-start(bf16[528,128]{1,0:T(8,128)(2,1)} %shard_map.59.packed_ref), channel_id=1, source_target_pairs={{0,32},{1,225},{32,64},{33,1},{64,96},{65,33},{96,128},{97,65},{12... | collective-permute-start | bytes 405512 | tf_op jit(solution)/shard_map/ppermute | solution.py:370
  11.9 0.0 copy-start
  11.9 1.1 %copy-done = bf16[1,72,4096]{2,1,0:T(8,128)(2,1)S(1)} copy-done((bf16[1,72,4096]{2,1,0:T(8,128)(2,1)S(1)}, bf16[1,72,4096]{2,1,0:T(8,128)(2,1)}, u32[]{:S(2)}) %copy-start) | copy-done | bytes 589848
  13.0 0.0 copy-start.1
  13.0 0.9 copy-done.1
  13.9 1.6 %shard_map.60 = (bf16[720,4096]{1,0:T(8,128)(2,1)S(1)}, f32[80,128]{1,0:T(8,128)S(1)}, bf16[528,128]{1,0:T(8,128)(2,1)S(1)}) custom-call(bf16[72,4096]{1,0:T(8,128)(2,1)S(1)} %bitcast.7, bf16[528,128]{1,0:T(8,128)(2,1)S(1)} %copy-done.1), custom_call_target="tpu_custom_call" | custom-call | bytes 12582912 | tf_op jit(solution)/shard_map/pallas_call | solution.py:380
  15.5 0.0 collective-permute-done.1.refs_4_
  15.5 0.8 collective-permute-done.refs_3_
  16.3 0.0 collective-permute-start.5
  16.3 4.3 %collective-permute-start.6 = (bf16[528,128]{1,0:T(8,128)(2,1)S(1)}, bf16[528,128]{1,0:T(8,128)(2,1)S(1)}, u32[]{:S(2)}, u32[]{:S(2)}) collective-permute-start(bf16[528,128]{1,0:T(8,128)(2,1)S(1)} %collective-permute-done.refs_3_), channel_id=1, source_target_pairs={{0,64},{1,193},{32,96},{33,225},{64,128},{65,1},{96,160},{97,33},{... | collective-permute-start | bytes 405512 | tf_op jit(solution)/shard_map/ppermute | solution.py:370
  20.6 0.2 collective-permute-start.4
  20.8 0.0 collective-permute-done.3.refs_2_
  20.8 0.0 collective-permute-done.2.refs_1_
  20.8 1.0 %collective-permute-done.5.refs_6_ = bf16[528,128]{1,0:T(8,128)(2,1)S(1)} collective-permute-done((bf16[528,128]{1,0:T(8,128)(2,1)S(1)}, bf16[528,128]{1,0:T(8,128)(2,1)S(1)}, u32[]{:S(2)}, u32[]{:S(2)}) %collective-permute-start.5) | collective-permute-done | bytes 135200 | tf_op jit(solution)/shard_map/ppermute | solution.py:370
  21.8 3.9 %collective-permute-done.6.refs_7_ = bf16[528,128]{1,0:T(8,128)(2,1)S(1)} collective-permute-done((bf16[528,128]{1,0:T(8,128)(2,1)S(1)}, bf16[528,128]{1,0:T(8,128)(2,1)S(1)}, u32[]{:S(2)}, u32[]{:S(2)}) %collective-permute-start.6) | collective-permute-done | bytes 135200 | tf_op jit(solution)/shard_map/ppermute | solution.py:370
  25.7 1.8 %collective-permute-done.4.refs_5_ = bf16[528,128]{1,0:T(8,128)(2,1)S(1)} collective-permute-done((bf16[528,128]{1,0:T(8,128)(2,1)S(1)}, bf16[528,128]{1,0:T(8,128)(2,1)S(1)}, u32[]{:S(2)}, u32[]{:S(2)}) %collective-permute-start.4) | collective-permute-done | bytes 135200 | tf_op jit(solution)/shard_map/ppermute | solution.py:370
  27.6 1.2 %shard_map.61 = bf16[16,528,128]{2,1,0:T(8,128)(2,1)S(1)} custom-call(bf16[528,128]{1,0:T(8,128)(2,1)S(1)} %get-tuple-element.21.refs_0_, bf16[528,128]{1,0:T(8,128)(2,1)S(1)} %collective-permute-done.2.refs_1_, bf16[528,128]{1,0:T(8,128)(2,1)S(1)} %collective-permute-done.3.refs_2_, bf16[528,128]{1,0:T(8,128)(2,1)S(1)} %collective-permute-done.refs_3_, ...), custom_call_target="tpu_custom_call" | custom-call | bytes 3145728 | tf_op jit(solution)/shard_map/pallas_call | solution.py:398
  28.7 30.9 %all_to_all.15.recv_at = bf16[16,528,128]{2,1,0:T(8,128)(2,1)} all-to-all(bf16[16,528,128]{2,1,0:T(8,128)(2,1)S(1)} %shard_map.61), channel_id=1, replica_groups=mesh['z'=8,'xy'=16,'dp'=2] {'xy'}, dimensions={0} | all-to-all | bytes 4325376 | tf_op jit(solution)/shard_map/all_to_all | solution.py:406
  59.6 3.7 %shard_map.62 = (bf16[256,4352]{1,0:T(8,128)(2,1)S(1)}, f32[240,768]{1,0:T(8,128)S(1)}, f32[8,128]{1,0:T(8,128)S(1)}) custom-call(bf16[16,528,128]{2,1,0:T(8,128)(2,1)} %all_to_all.15.recv_at, bf16[720,4096]{1,0:T(8,128)(2,1)S(1)} %get-tuple-element.24.shifted_ref, f32[80,128]{1,0:T(8,128)S(1)} %get-tuple-element.25.half_ref), custom_call_target="tpu_custom_call" | custom-call | flops 1509949440 | bytes 10485760 | tf_op jit(solution)/shard_map/pallas_call | solution.py:408
  63.3 14.4 %all_to_all.16 = f32[8,8,128]{2,1,0:T(8,128)S(1)} all-to-all(f32[8,8,128]{2,1,0:T(8,128)S(1)} %broadcast_in_dim.17), channel_id=1, replica_groups=mesh['z'=8,'xy'=16,'dp'=2] {'z'}, dimensions={0} | all-to-all | bytes 65536 | tf_op jit(solution)/shard_map/all_to_all | solution.py:422
  77.7 11.6 %all_to_all.17 = f32[16,64,128]{2,1,0:T(8,128)S(1)} all-to-all(f32[16,64,128]{2,1,0:T(8,128)S(1)} %broadcast_in_dim.19), channel_id=1, replica_groups=mesh['z'=8,'xy'=16,'dp'=2] {'xy'}, dimensions={0} | all-to-all | bytes 1048576 | tf_op jit(solution)/shard_map/all_to_all | solution.py:424
  89.4 1.4 %shard_map.63 = (f32[40,4224]{1,0:T(8,128)S(1)}, bf16[120,768]{1,0:T(8,128)(2,1)S(1)}, f32[40,128]{1,0:T(8,128)S(1)}) custom-call(f32[240,768]{1,0:T(8,128)S(1)} %get-tuple-element.26.s_ref, bf16[256,4352]{1,0:T(8,128)(2,1)S(1)} %get-tuple-element.27.x_ref, f32[8,128]{1,0:T(8,128)S(1)} %get-tuple-element.28.mine_ref, f32[1024,128]{1,0:T(8,128)S(1)} %bitcast.6), custom_call_target="tpu_custom_call" | custom-call | flops 754974720 | bytes 5242880 | tf_op jit(solution)/shard_map/pallas_call | solution.py:427
  90.8 5.9 %collective-permute-start.7 = (f32[40,4224]{1,0:T(8,128)S(1)}, f32[40,4224]{1,0:T(8,128)S(1)}, u32[]{:S(2)}, u32[]{:S(2)}) collective-permute-start(f32[40,4224]{1,0:T(8,128)S(1)} %get-tuple-element.31), channel_id=1, source_target_pairs={{0,1},{1,0},{2,3},{3,2},{4,5},{5,4},{6,7},{7,6},{8,9},{9,8},{10,11... | collective-permute-start | bytes 2027528 | tf_op jit(solution)/shard_map/ppermute | solution.py:440
  96.7 1.1 %shard_map.64.keep_ref = f32[40,4096]{1,0:T(8,128)S(1)} custom-call(bf16[120,768]{1,0:T(8,128)(2,1)S(1)} %get-tuple-element.29.w_ref, bf16[256,4352]{1,0:T(8,128)(2,1)S(1)} %get-tuple-element.27.x_ref), custom_call_target="tpu_custom_call" | custom-call | flops 754974720 | bytes 4194304 | tf_op jit(solution)/shard_map/pallas_call | solution.py:441
  97.8 0.6 collective-permute-done.7.other_ref
  98.4 1.5 %shard_map.65 = (f32[1152,128]{1,0:T(8,128)}, f32[1,36]{1,0:T(1,128)}) custom-call(f32[40,4096]{1,0:T(8,128)S(1)} %shard_map.64.keep_ref, f32[40,128]{1,0:T(8,128)S(1)} %get-tuple-element.30.total_ref, f32[40,4224]{1,0:T(8,128)S(1)} %collective-permute-done.7.other_ref), custom_call_target="tpu_custom_call" | custom-call | bytes 2097152 | tf_op jit(solution)/shard_map/pallas_call | solution.py:450
  (2 shorter events, 0.0 us)
Async XLA Ops:
  2.4 13.1 %collective-permute-start.1 = (bf16[528,128]{1,0:T(8,128)(2,1)}, bf16[528,128]{1,0:T(8,128)(2,1)S(1)}, u32[]{:S(2)}, u32[]{:S(2)}) collective-permute-start(bf16[528,128]{1,0:T(8,128)(2,1)} %shard_map.59.packed_ref), channel_id=1, source_target_pairs={{0,192},{1,65},{32,224},{33,97},{64,0},{65,129},{96,32},{97,161},{... | collective-permute-start | bytes 405512 | tf_op jit(solution)/shard_map/ppermute | solution.py:370
  6.2 10.1 %collective-permute-start = (bf16[528,128]{1,0:T(8,128)(2,1)}, bf16[528,128]{1,0:T(8,128)(2,1)S(1)}, u32[]{:S(2)}, u32[]{:S(2)}) collective-permute-start(bf16[528,128]{1,0:T(8,128)(2,1)} %shard_map.59.packed_ref), channel_id=1, source_target_pairs={{0,64},{1,193},{32,96},{33,225},{64,128},{65,1},{96,160},{97,33},{... | collective-permute-start | bytes 405512 | tf_op jit(solution)/shard_map/ppermute | solution.py:370
  9.2 11.5 %collective-permute-start.3 = (bf16[528,128]{1,0:T(8,128)(2,1)}, bf16[528,128]{1,0:T(8,128)(2,1)S(1)}, u32[]{:S(2)}, u32[]{:S(2)}) collective-permute-start(bf16[528,128]{1,0:T(8,128)(2,1)} %shard_map.59.packed_ref), channel_id=1, source_target_pairs={{0,224},{1,33},{32,0},{33,65},{64,32},{65,97},{96,64},{97,129},{12... | collective-permute-start | bytes 405512 | tf_op jit(solution)/shard_map/ppermute | solution.py:370
  10.0 10.8 %collective-permute-start.2 = (bf16[528,128]{1,0:T(8,128)(2,1)}, bf16[528,128]{1,0:T(8,128)(2,1)S(1)}, u32[]{:S(2)}, u32[]{:S(2)}) collective-permute-start(bf16[528,128]{1,0:T(8,128)(2,1)} %shard_map.59.packed_ref), channel_id=1, source_target_pairs={{0,32},{1,225},{32,64},{33,1},{64,96},{65,33},{96,128},{97,65},{12... | collective-permute-start | bytes 405512 | tf_op jit(solution)/shard_map/ppermute | solution.py:370
  11.9 1.1 %copy-start = (bf16[1,72,4096]{2,1,0:T(8,128)(2,1)S(1)}, bf16[1,72,4096]{2,1,0:T(8,128)(2,1)}, u32[]{:S(2)}) copy-start(bf16[1,72,4096]{2,1,0:T(8,128)(2,1)} %param.5) | copy-start | bytes 1769476
  13.0 0.9 copy-start.1
  16.3 5.5 %collective-permute-start.5 = (bf16[528,128]{1,0:T(8,128)(2,1)S(1)}, bf16[528,128]{1,0:T(8,128)(2,1)S(1)}, u32[]{:S(2)}, u32[]{:S(2)}) collective-permute-start(bf16[528,128]{1,0:T(8,128)(2,1)S(1)} %collective-permute-done.1.refs_4_), channel_id=1, source_target_pairs={{0,224},{1,33},{32,0},{33,65},{64,32},{65,97},{96,64},{97,129},{12... | collective-permute-start | bytes 405512 | tf_op jit(solution)/shard_map/ppermute | solution.py:370
  16.3 9.4 %collective-permute-start.6 = (bf16[528,128]{1,0:T(8,128)(2,1)S(1)}, bf16[528,128]{1,0:T(8,128)(2,1)S(1)}, u32[]{:S(2)}, u32[]{:S(2)}) collective-permute-start(bf16[528,128]{1,0:T(8,128)(2,1)S(1)} %collective-permute-done.refs_3_), channel_id=1, source_target_pairs={{0,64},{1,193},{32,96},{33,225},{64,128},{65,1},{96,160},{97,33},{... | collective-permute-start | bytes 405512 | tf_op jit(solution)/shard_map/ppermute | solution.py:370
  20.6 7.0 %collective-permute-start.4 = (bf16[528,128]{1,0:T(8,128)(2,1)S(1)}, bf16[528,128]{1,0:T(8,128)(2,1)S(1)}, u32[]{:S(2)}, u32[]{:S(2)}) collective-permute-start(bf16[528,128]{1,0:T(8,128)(2,1)S(1)} %collective-permute-done.refs_3_), channel_id=1, source_target_pairs={{0,32},{1,225},{32,64},{33,1},{64,96},{65,33},{96,128},{97,65},{12... | collective-permute-start | bytes 405512 | tf_op jit(solution)/shard_map/ppermute | solution.py:370
  90.8 7.6 %collective-permute-start.7 = (f32[40,4224]{1,0:T(8,128)S(1)}, f32[40,4224]{1,0:T(8,128)S(1)}, u32[]{:S(2)}, u32[]{:S(2)}) collective-permute-start(f32[40,4224]{1,0:T(8,128)S(1)} %get-tuple-element.31), channel_id=1, source_target_pairs={{0,1},{1,0},{2,3},{3,2},{4,5},{5,4},{6,7},{7,6},{8,9},{9,8},{10,11... | collective-permute-start | bytes 2027528 | tf_op jit(solution)/shard_map/ppermute | solution.py:440

commit v7 on v4

--- a/solution.py
+++ b/solution.py
@@ -123,7 +123,8 @@
                 ]
 
 
-def shift_kernel(from_ref, out_ref, half_ref, rot_ref):
+def shift_kernel(from_ref, packed_ref, out_ref, half_ref, own_ref, rot_ref):
+    own_ref[...] = packed_ref[...]
     count, pixels = rot_ref.shape
     rots = from_ref.shape[0]
     half_count, half_rots = count // 2, rots // 2
@@ -219,8 +220,46 @@
     parts = slots // LANES
     for i, value in enumerate((peak, total, number)):
         for h in range(parts):
-            tile_ref[i * parts + h : i * parts + h + 1] = value[:, tile_of(h)]
-    tile_ref[3 * parts :] = jnp.zeros_like(tile_ref[3 * parts :])
+            tile_ref[0, i * parts + h : i * parts + h + 1] = value[:, tile_of(h)]
+    tile_ref[0, 3 * parts :] = jnp.zeros_like(tile_ref[0, 3 * parts :])
+    for i in range(1, tile_ref.shape[0]):
+        tile_ref[i] = tile_ref[0]
+
+
+def partner_of(rows):
+    second = (lane_row() // PLANES) % SLOTS == 1
+    return jnp.where(
+        second, pltpu.roll(rows, PLANES, 1), pltpu.roll(rows, LANES - PLANES, 1)
+    )
+
+
+def fold_kernel(shown_ref, out_ref):
+    planes = shown_ref.shape[0]
+    rows = out_ref.shape[1] // 2
+    second = (lane_row() // PLANES) % SLOTS == 1
+    parts = 2
+    shown = [
+        [
+            jnp.concatenate(
+                [shown_ref[z, i * parts + h : i * parts + h + 1] for z in range(planes)], axis=0
+            )
+            for h in range(parts)
+        ]
+        for i in range(3)
+    ]
+    for p in range(rows):
+        found = []
+        for h in range(parts):
+            same = shown[2][h] == p + 1
+            peak = jnp.max(jnp.where(same, shown[0][h], -FAR), axis=0, keepdims=True)
+            peak = jnp.maximum(peak, partner_of(peak))
+            part = shown[1][h] * jnp.exp(jnp.minimum(shown[0][h] - peak, 0.0))
+            total = jnp.sum(jnp.where(same, part, 0.0), axis=0, keepdims=True)
+            found.append((peak, total + partner_of(total)))
+        out_ref[0, p : p + 1] = jnp.where(second, found[1][0], found[0][0])
+        out_ref[0, rows + p : rows + p + 1] = jnp.where(second, found[1][1], found[0][1])
+    for i in range(1, out_ref.shape[0]):
+        out_ref[i] = out_ref[0]
 
 
 def sum_half(w_ref, x_ref, out_ref, y_ref):
@@ -258,33 +297,33 @@
     groups = s_ref.shape[0]
     slots = x_ref.shape[0]
     pixels = x_ref.shape[1] - 2 * LANES
-    owners = all_ref.shape[0] // 8
+    rows = all_ref.shape[1] // 2
     count = groups // len(COL_SHIFTS)
     half_count = count // 2
     parts = slots // LANES
-    lane = lane_row()
-    second = (lane // PLANES) % SLOTS == 1
-
-    def partner(row):
-        return jnp.where(second, pltpu.roll(row, PLANES, 1), pltpu.roll(row, LANES - PLANES, 1))
-
+    second = (lane_row() // PLANES) % SLOTS == 1
+    tables = range(all_ref.shape[0])
+    peak = all_ref[0, :rows]
+    for i in tables:
+        peak = jnp.maximum(peak, all_ref[i, :rows])
+    total = jnp.zeros_like(peak)
+    for i in tables:
+        total = total + all_ref[i, rows:] * jnp.exp(all_ref[i, :rows] - peak)
+    number = lax.broadcasted_iota(jnp.int32, (rows, LANES), 0).astype(F32) + 1
     peaks, scales = [], []
     for h in range(parts):
-        own = mine_ref[2 * parts + h : 2 * parts + h + 1]
-        across = partner(own)
-        shown = [all_ref[pl.ds(i * parts + h, owners, stride=8), :] for i in range(3)]
-        found = []
-        for slot in range(SLOTS):
-            target = jnp.where(second == (slot == 1), own, across)
-            same = shown[2] == target
-            peak = jnp.max(jnp.where(same, shown[0], -jnp.inf), axis=0, keepdims=True)
-            peak = jnp.maximum(peak, partner(peak))
-            part = shown[1] * jnp.exp(jnp.minimum(shown[0] - peak, 0.0))
-            total = jnp.sum(jnp.where(same, part, 0.0), axis=0, keepdims=True)
-            found.append((peak, total + partner(total)))
-        peaks.append(jnp.where(second, found[1][0], found[0][0]))
-        total = jnp.where(second, found[1][1], found[0][1])
-        scales.append(jnp.where(own > 0, 1.0 / total, 0.0))
+        own = mine_ref[0, 2 * parts + h : 2 * parts + h + 1]
+        here = second == (h == 1)
+        mine = [
+            jnp.sum(
+                jnp.where(number == own, jnp.where(here, table, partner_of(table)), 0.0),
+                axis=0,
+                keepdims=True,
+            )
+            for table in (peak, total)
+        ]
+        peaks.append(mine[0])
+        scales.append(jnp.where(own > 0, 1.0 / jnp.where(own > 0, mine[1], 1.0), 0.0))
     peak = jnp.concatenate(peaks, axis=1)
     scale = jnp.concatenate(scales, axis=1)
     for half, to_ref, sums_ref in ((0, w_ref, total_ref), (1, w_give_ref, give_ref.at[:, pixels:])):
@@ -353,7 +392,7 @@
         pack_kernel,
         shape(((tiles + 1) * rows, LANES), BF16),
         3,
-        4,
+        54,
         moved=MIB // 4,
     )(candidates.T, inv_noise[None, :], images)
 
@@ -367,19 +406,25 @@
     pad = half_count - half_rots
     count = 2 * half_count
     groups = len(COL_SHIFTS) * count
-    shifted, half_norm = call(
+    shifted, half_norm, own = call(
         shift_kernel,
-        (shape((len(ROW_SHIFTS) * groups, pixels), BF16), shape((count, LANES), F32)),
-        1,
+        (
+            shape((len(ROW_SHIFTS) * groups, pixels), BF16),
+            shape((count, LANES), F32),
+            shape(packed.shape, BF16),
+        ),
+        2,
         6,
         [pltpu.VMEM((count, pixels), BF16)],
         moved=12 * MIB,
-    )(references[0])
-    next_near, shifted, half_norm = lax.optimization_barrier((next_near, shifted, half_norm))
+    )(references[0], packed)
+    next_near, shifted, half_norm, own = lax.optimization_barrier(
+        (next_near, shifted, half_norm, own)
+    )
     cut = (tiles + 1) // 2 * rows
     far = [move(next_near[0], 1), move(next_near[1], -1)]
     far += [move(next_near[0][:cut], 2), move(next_near[1][cut:], -2)]
-    column = [packed, *near, *next_near, *far]
+    column = [own, *near, *next_near, *far]
     steps = [0, -1, 1, -2, 2, -3, 3, 4, 4]
     picked = call(
         functools.partial(pick_kernel, steps=steps, top=top),
@@ -396,16 +441,17 @@
         (
             shape((slots, pixels + 2 * LANES), BF16),
             shape((groups, len(ROW_SHIFTS) * slots), F32),
-            shape((8, LANES), F32),
+            shape((planes, 8, LANES), F32),
         ),
         3,
         8,
         flops=work,
         moved=10 * MIB,
     )(received, shifted, half_norm)
-    by_plane = exchange(jnp.broadcast_to(tile[None], (planes, 8, LANES)), "z")
-    by_plane = by_plane.reshape(1, planes * 8, LANES)
-    everyone = exchange(jnp.broadcast_to(by_plane, (owners, planes * 8, LANES)), "xy")
+    folded = call(
+        fold_kernel, shape((owners, 2 * rows, LANES), F32), 1, 4, moved=MIB // 4
+    )(exchange(tile, "z"))
+    everyone = exchange(folded, "xy")
     weight_shape = (groups // 2, len(ROW_SHIFTS) * slots)
     scratch = pltpu.VMEM((groups // 2, 4 * LANES), F32)
     give, weights, total = call(
@@ -420,7 +466,7 @@
         [pltpu.VMEM(weight_shape, BF16), scratch],
         flops=work // 2,
         moved=5 * MIB,
-    )(scores, x, tile, everyone.reshape(owners * planes * 8, LANES))
+    )(scores, x, tile, everyone)
     other = lax.ppermute(give, "dp", [(0, 1), (1, 0)])
     keep = call(
         keep_kernel,

time: 98.2 us -> 96.1 us (0.979)
  blocking collectives: 54.8 us -> 53.2 us
  Pallas kernels: 9.23 us -> 10.8 us
  local copies, waits for them, and re-layouts: 3.36 us -> 1.98 us
    pallas_call x1 -> x2, Pallas kernels: 0.17 us -> 2.02 us  [the longest x1 1.77 us: on_device(): call(pack_kernel, shape(((tiles + 1) * rows, LANES), BF16), 3, 54, moved=...]
    all_to_all x2, blocking collectives: 23.4 us -> 21.7 us  [the longest x1 11.3 us: on_device(): exchange(tile, 'z')]
    unnamed x8 -> x4, local copies, waits for them, and re-layouts: 3.3 us -> 1.97 us
  transfers between devices with their start and end apart: 9 -> 9, of which waited for: 3 -> 4; matrix products, arithmetic and copies ran while one was open for 0% -> 0% of each run, Pallas kernels for 3% -> 3%
where the time goes in v7:
time: 96.1 us; the launch traced here: 95.8 us
  blocking collectives  53.2 us (55%)
  starting transfers between devices  23.4 us (24%)
  Pallas kernels  10.8 us (11%)
  waiting for transfers between devices  5.75 us (6%)
  local copies, waits for them, and re-layouts  1.98 us (2%)
    all_to_all x1, blocking collectives, on_device(): received = exchange(picked, 'xy')  31.5 us
    ppermute x8, starting transfers between devices, move(): lax.ppermute(part, 'z', [(i, (i + step) % planes) for i in range(planes)])  15.1 us
    all_to_all x1, blocking collectives, on_device(): exchange(tile, 'z')  11.3 us
    all_to_all x1, blocking collectives, on_device(): everyone = exchange(folded, 'xy')  10.4 us
    ppermute x1, starting transfers between devices, on_device(): other = lax.ppermute(give, 'dp', [(0, 1), (1, 0)])  8.32 us
    ppermute x8, waiting for transfers between devices, move(): lax.ppermute(part, 'z', [(i, (i + step) % planes) for i in range(planes)])  5.14 us
    pallas_call x1, Pallas kernels, on_device(): call(functools.partial(score_kernel, pad=pad), (shape((slots, pixels + 2...  2.07 us
    unnamed x4, local copies, waits for them, and re-layouts  1.97 us
  transfers between devices with their start and end apart: 9, of which 4 were waited for; matrix products, arithmetic and copies ran while one was open for 0% of the time, Pallas kernels for 3%

profile of v7, /device:TPU:1, one launch (start us, length us, event | category | flops | bytes accessed | tf_op | source)
XLA Modules:
  0.0 95.8 jit_solution(15664406528596298463)
XLA Ops:
  0.6 1.8 %shard_map.59.packed_ref = bf16[528,128]{1,0:T(8,128)(2,1)} custom-call(s32[8,16]{1,0:T(8,128)} %bitcast.5, bf16[1,16]{1,0:T(2,128)(2,1)} %bitcast.6, bf16[16,4096]{1,0:T(8,128)(2,1)} %img_ref.1), custom_call_target="tpu_custom_call" | custom-call | bytes 262144 | tf_op jit(solution)/shard_map/pallas_call | solution.py:391
  2.4 6.8 %collective-permute-start.1 = (bf16[528,128]{1,0:T(8,128)(2,1)}, bf16[528,128]{1,0:T(8,128)(2,1)S(1)}, u32[]{:S(2)}, u32[]{:S(2)}) collective-permute-start(bf16[528,128]{1,0:T(8,128)(2,1)} %shard_map.59.packed_ref), channel_id=1, source_target_pairs={{0,192},{32,224},{64,0},{96,32},{128,64},{160,96},{192,128},{224,1... | collective-permute-start | bytes 405512 | tf_op jit(solution)/shard_map/ppermute | solution.py:400
  9.2 0.0 collective-permute-start
  9.2 3.1 %collective-permute-start.3 = (bf16[528,128]{1,0:T(8,128)(2,1)}, bf16[528,128]{1,0:T(8,128)(2,1)S(1)}, u32[]{:S(2)}, u32[]{:S(2)}) collective-permute-start(bf16[528,128]{1,0:T(8,128)(2,1)} %shard_map.59.packed_ref), channel_id=1, source_target_pairs={{0,224},{32,0},{64,32},{96,64},{128,96},{160,128},{192,160},{224,1... | collective-permute-start | bytes 405512 | tf_op jit(solution)/shard_map/ppermute | solution.py:400
  12.4 0.0 collective-permute-start.2
  12.4 0.0 copy-start
  12.4 1.1 %copy-done = bf16[1,72,4096]{2,1,0:T(8,128)(2,1)S(1)} copy-done((bf16[1,72,4096]{2,1,0:T(8,128)(2,1)S(1)}, bf16[1,72,4096]{2,1,0:T(8,128)(2,1)}, u32[]{:S(2)}) %copy-start) | copy-done | bytes 589848
  13.4 0.0 copy-start.1
  13.4 0.9 copy-done.1
  14.4 1.6 %shard_map.60 = (bf16[720,4096]{1,0:T(8,128)(2,1)S(1)}, f32[80,128]{1,0:T(8,128)S(1)}, bf16[528,128]{1,0:T(8,128)(2,1)S(1)}) custom-call(bf16[72,4096]{1,0:T(8,128)(2,1)S(1)} %bitcast.4, bf16[528,128]{1,0:T(8,128)(2,1)S(1)} %copy-done.1), custom_call_target="tpu_custom_call" | custom-call | bytes 12582912 | tf_op jit(solution)/shard_map/pallas_call | solution.py:409
  15.9 0.0 collective-permute-done.1.refs_4_
  16.0 0.7 collective-permute-done.refs_3_
  16.6 2.5 %collective-permute-start.4 = (bf16[528,128]{1,0:T(8,128)(2,1)S(1)}, bf16[528,128]{1,0:T(8,128)(2,1)S(1)}, u32[]{:S(2)}, u32[]{:S(2)}) collective-permute-start(bf16[528,128]{1,0:T(8,128)(2,1)S(1)} %collective-permute-done.refs_3_), channel_id=1, source_target_pairs={{0,32},{32,64},{64,96},{96,128},{128,160},{160,192},{192,224},{224... | collective-permute-start | bytes 405512 | tf_op jit(solution)/shard_map/ppermute | solution.py:400
  19.2 0.2 collective-permute-start.5
  19.3 1.3 %collective-permute-start.7 = (bf16[272,128]{1,0:T(8,128)(2,1)S(1)}, bf16[272,128]{1,0:T(8,128)(2,1)S(1)}, u32[]{:S(2)}, u32[]{:S(2)}) collective-permute-start(bf16[272,128]{1,0:T(8,128)(2,1)S(1)} %slice.7), channel_id=1, source_target_pairs={{0,192},{32,224},{64,0},{96,32},{128,64},{160,96},{192,128},{224,1... | collective-permute-start | bytes 208904 | tf_op jit(solution)/shard_map/ppermute | solution.py:400
  20.6 0.0 collective-permute-done.3.refs_2_
  20.6 1.1 %collective-permute-start.6 = (bf16[256,128]{1,0:T(8,128)(2,1)S(1)}, bf16[256,128]{1,0:T(8,128)(2,1)S(1)}, u32[]{:S(2)}, u32[]{:S(2)}) collective-permute-start(bf16[256,128]{1,0:T(8,128)(2,1)S(1)} %slice.6), channel_id=1, source_target_pairs={{0,64},{32,96},{64,128},{96,160},{128,192},{160,224},{192,0},{224,... | collective-permute-start | bytes 196616 | tf_op jit(solution)/shard_map/ppermute | solution.py:400
  21.8 0.1 collective-permute-done.2.refs_1_
  21.8 4.4 %collective-permute-done.6.refs_7_ = bf16[256,128]{1,0:T(8,128)(2,1)S(1)} collective-permute-done((bf16[256,128]{1,0:T(8,128)(2,1)S(1)}, bf16[256,128]{1,0:T(8,128)(2,1)S(1)}, u32[]{:S(2)}, u32[]{:S(2)}) %collective-permute-start.6) | collective-permute-done | bytes 65568 | tf_op jit(solution)/shard_map/ppermute | solution.py:400
  26.2 0.0 collective-permute-done.7.refs_8_
  26.2 0.0 collective-permute-done.4.refs_5_
  26.2 0.0 collective-permute-done.5.refs_6_
  26.2 1.2 %shard_map.61 = bf16[16,528,128]{2,1,0:T(8,128)(2,1)S(1)} custom-call(bf16[528,128]{1,0:T(8,128)(2,1)S(1)} %get-tuple-element.21.refs_0_, bf16[528,128]{1,0:T(8,128)(2,1)S(1)} %collective-permute-done.2.refs_1_, bf16[528,128]{1,0:T(8,128)(2,1)S(1)} %collective-permute-done.3.refs_2_, bf16[528,128]{1,0:T(8,128)(2,1)S(1)} %collective-permute-done.refs_3_, ...), custom_call_target="tpu_custom_call" | custom-call | bytes 3145728 | tf_op jit(solution)/shard_map/pallas_call | solution.py:429
  27.4 31.5 %all_to_all.15.recv_ref = bf16[16,528,128]{2,1,0:T(8,128)(2,1)S(1)} all-to-all(bf16[16,528,128]{2,1,0:T(8,128)(2,1)S(1)} %shard_map.61), channel_id=1, replica_groups=mesh['z'=8,'xy'=16,'dp'=2] {'xy'}, dimensions={0} | all-to-all | bytes 4325376 | tf_op jit(solution)/shard_map/all_to_all | solution.py:437
  58.9 2.1 %shard_map.62 = (bf16[256,4352]{1,0:T(8,128)(2,1)S(1)}, f32[240,768]{1,0:T(8,128)S(1)}, f32[8,8,128]{2,1,0:T(8,128)S(1)}) custom-call(bf16[16,528,128]{2,1,0:T(8,128)(2,1)S(1)} %all_to_all.15.recv_ref, bf16[720,4096]{1,0:T(8,128)(2,1)S(1)} %get-tuple-element.24.shifted_ref, f32[80,128]{1,0:T(8,128)S(1)} %get-tuple-element.25.half_ref), custom_call_target="tpu_custom_call" | custom-call | flops 1509949440 | bytes 10485760 | tf_op jit(solution)/shard_map/pallas_call | solution.py:439
  60.9 11.3 %all_to_all.16.shown_ref = f32[8,8,128]{2,1,0:T(8,128)S(1)} all-to-all(f32[8,8,128]{2,1,0:T(8,128)S(1)} %get-tuple-element.28.mine_ref), channel_id=1, replica_groups=mesh['z'=8,'xy'=16,'dp'=2] {'z'}, dimensions={0} | all-to-all | bytes 65536 | tf_op jit(solution)/shard_map/all_to_all | solution.py:453
  72.3 0.3 shard_map.63
  72.5 10.4 %all_to_all.17.all_ref = f32[16,32,128]{2,1,0:T(8,128)S(1)} all-to-all(f32[16,32,128]{2,1,0:T(8,128)S(1)} %shard_map.63), channel_id=1, replica_groups=mesh['z'=8,'xy'=16,'dp'=2] {'xy'}, dimensions={0} | all-to-all | bytes 524288 | tf_op jit(solution)/shard_map/all_to_all | solution.py:454
  82.9 1.3 %shard_map.64 = (f32[40,4224]{1,0:T(8,128)S(1)}, bf16[120,768]{1,0:T(8,128)(2,1)S(1)}, f32[40,128]{1,0:T(8,128)S(1)}) custom-call(f32[240,768]{1,0:T(8,128)S(1)} %get-tuple-element.26.s_ref, bf16[256,4352]{1,0:T(8,128)(2,1)S(1)} %get-tuple-element.27.x_ref, f32[8,8,128]{2,1,0:T(8,128)S(1)} %get-tuple-element.28.mine_ref, f32[16,32,128]{2,1,0:T(8,128)S(1)} %all_to_all.17.all_ref), custom_call_target="tpu_custom_call" | custom-call | flops 754974720 | bytes 5242880 | tf_op jit(solution)/shard_map/pallas_call | solution.py:457
  84.2 8.3 %collective-permute-start.8 = (f32[40,4224]{1,0:T(8,128)S(1)}, f32[40,4224]{1,0:T(8,128)S(1)}, u32[]{:S(2)}, u32[]{:S(2)}) collective-permute-start(f32[40,4224]{1,0:T(8,128)S(1)} %get-tuple-element.31), channel_id=1, source_target_pairs={{0,1},{1,0},{2,3},{3,2},{4,5},{5,4},{6,7},{7,6},{8,9},{9,8},{10,11... | collective-permute-start | bytes 2027528 | tf_op jit(solution)/shard_map/ppermute | solution.py:470
  92.5 1.1 %shard_map.65.keep_ref = f32[40,4096]{1,0:T(8,128)S(1)} custom-call(bf16[120,768]{1,0:T(8,128)(2,1)S(1)} %get-tuple-element.29.w_ref, bf16[256,4352]{1,0:T(8,128)(2,1)S(1)} %get-tuple-element.27.x_ref), custom_call_target="tpu_custom_call" | custom-call | flops 754974720 | bytes 4194304 | tf_op jit(solution)/shard_map/pallas_call | solution.py:471
  93.7 0.6 collective-permute-done.8.other_ref
  94.3 1.5 %shard_map.66 = (f32[1152,128]{1,0:T(8,128)}, f32[1,36]{1,0:T(1,128)}) custom-call(f32[40,4096]{1,0:T(8,128)S(1)} %shard_map.65.keep_ref, f32[40,128]{1,0:T(8,128)S(1)} %get-tuple-element.30.total_ref, f32[40,4224]{1,0:T(8,128)S(1)} %collective-permute-done.8.other_ref), custom_call_target="tpu_custom_call" | custom-call | bytes 2097152 | tf_op jit(solution)/shard_map/pallas_call | solution.py:480
  (2 shorter events, 0.0 us)
Async XLA Ops:
  2.4 13.6 %collective-permute-start.1 = (bf16[528,128]{1,0:T(8,128)(2,1)}, bf16[528,128]{1,0:T(8,128)(2,1)S(1)}, u32[]{:S(2)}, u32[]{:S(2)}) collective-permute-start(bf16[528,128]{1,0:T(8,128)(2,1)} %shard_map.59.packed_ref), channel_id=1, source_target_pairs={{0,192},{32,224},{64,0},{96,32},{128,64},{160,96},{192,128},{224,1... | collective-permute-start | bytes 405512 | tf_op jit(solution)/shard_map/ppermute | solution.py:400
  9.2 7.4 %collective-permute-start = (bf16[528,128]{1,0:T(8,128)(2,1)}, bf16[528,128]{1,0:T(8,128)(2,1)S(1)}, u32[]{:S(2)}, u32[]{:S(2)}) collective-permute-start(bf16[528,128]{1,0:T(8,128)(2,1)} %shard_map.59.packed_ref), channel_id=1, source_target_pairs={{0,64},{32,96},{64,128},{96,160},{128,192},{160,224},{192,0},{224,... | collective-permute-start | bytes 405512 | tf_op jit(solution)/shard_map/ppermute | solution.py:400
  9.2 11.4 %collective-permute-start.3 = (bf16[528,128]{1,0:T(8,128)(2,1)}, bf16[528,128]{1,0:T(8,128)(2,1)S(1)}, u32[]{:S(2)}, u32[]{:S(2)}) collective-permute-start(bf16[528,128]{1,0:T(8,128)(2,1)} %shard_map.59.packed_ref), channel_id=1, source_target_pairs={{0,224},{32,0},{64,32},{96,64},{128,96},{160,128},{192,160},{224,1... | collective-permute-start | bytes 405512 | tf_op jit(solution)/shard_map/ppermute | solution.py:400
  12.4 9.5 %collective-permute-start.2 = (bf16[528,128]{1,0:T(8,128)(2,1)}, bf16[528,128]{1,0:T(8,128)(2,1)S(1)}, u32[]{:S(2)}, u32[]{:S(2)}) collective-permute-start(bf16[528,128]{1,0:T(8,128)(2,1)} %shard_map.59.packed_ref), channel_id=1, source_target_pairs={{0,32},{32,64},{64,96},{96,128},{128,160},{160,192},{192,224},{224... | collective-permute-start | bytes 405512 | tf_op jit(solution)/shard_map/ppermute | solution.py:400
  12.4 1.1 %copy-start = (bf16[1,72,4096]{2,1,0:T(8,128)(2,1)S(1)}, bf16[1,72,4096]{2,1,0:T(8,128)(2,1)}, u32[]{:S(2)}) copy-start(bf16[1,72,4096]{2,1,0:T(8,128)(2,1)} %param.5) | copy-start | bytes 1769476
  13.4 0.9 copy-start.1
  16.6 9.6 %collective-permute-start.4 = (bf16[528,128]{1,0:T(8,128)(2,1)S(1)}, bf16[528,128]{1,0:T(8,128)(2,1)S(1)}, u32[]{:S(2)}, u32[]{:S(2)}) collective-permute-start(bf16[528,128]{1,0:T(8,128)(2,1)S(1)} %collective-permute-done.refs_3_), channel_id=1, source_target_pairs={{0,32},{32,64},{64,96},{96,128},{128,160},{160,192},{192,224},{224... | collective-permute-start | bytes 405512 | tf_op jit(solution)/shard_map/ppermute | solution.py:400
  19.2 7.1 %collective-permute-start.5 = (bf16[528,128]{1,0:T(8,128)(2,1)S(1)}, bf16[528,128]{1,0:T(8,128)(2,1)S(1)}, u32[]{:S(2)}, u32[]{:S(2)}) collective-permute-start(bf16[528,128]{1,0:T(8,128)(2,1)S(1)} %collective-permute-done.1.refs_4_), channel_id=1, source_target_pairs={{0,224},{32,0},{64,32},{96,64},{128,96},{160,128},{192,160},{224,1... | collective-permute-start | bytes 405512 | tf_op jit(solution)/shard_map/ppermute | solution.py:400
  19.3 6.9 %collective-permute-start.7 = (bf16[272,128]{1,0:T(8,128)(2,1)S(1)}, bf16[272,128]{1,0:T(8,128)(2,1)S(1)}, u32[]{:S(2)}, u32[]{:S(2)}) collective-permute-start(bf16[272,128]{1,0:T(8,128)(2,1)S(1)} %slice.7), channel_id=1, source_target_pairs={{0,192},{32,224},{64,0},{96,32},{128,64},{160,96},{192,128},{224,1... | collective-permute-start | bytes 208904 | tf_op jit(solution)/shard_map/ppermute | solution.py:400
  20.6 5.6 %collective-permute-start.6 = (bf16[256,128]{1,0:T(8,128)(2,1)S(1)}, bf16[256,128]{1,0:T(8,128)(2,1)S(1)}, u32[]{:S(2)}, u32[]{:S(2)}) collective-permute-start(bf16[256,128]{1,0:T(8,128)(2,1)S(1)} %slice.6), channel_id=1, source_target_pairs={{0,64},{32,96},{64,128},{96,160},{128,192},{160,224},{192,0},{224,... | collective-permute-start | bytes 196616 | tf_op jit(solution)/shard_map/ppermute | solution.py:400
  84.2 10.1 %collective-permute-start.8 = (f32[40,4224]{1,0:T(8,128)S(1)}, f32[40,4224]{1,0:T(8,128)S(1)}, u32[]{:S(2)}, u32[]{:S(2)}) collective-permute-start(f32[40,4224]{1,0:T(8,128)S(1)} %get-tuple-element.31), channel_id=1, source_target_pairs={{0,1},{1,0},{2,3},{3,2},{4,5},{5,4},{6,7},{7,6},{8,9},{9,8},{10,11... | collective-permute-start | bytes 2027528 | tf_op jit(solution)/shard_map/ppermute | solution.py:470

commit v8 on v7

--- a/solution.py
+++ b/solution.py
@@ -43,7 +43,13 @@
     return jnp.where(low, pltpu.roll(load(first), half, 1), load(first + 1))
 
 
-def pack_kernel(cand_ref, noise_ref, img_ref, send_ref):
+def pack_kernel(cand_at, noise_at, img_at, send_ref, cand_ref, noise_ref, img_ref, sems):
+    pairs = ((cand_at, cand_ref), (noise_at, noise_ref), (img_at, img_ref))
+    loads = [pltpu.make_async_copy(at, ref, sems.at[i]) for i, (at, ref) in enumerate(pairs)]
+    for load in loads:
+        load.start()
+    for load in loads:
+        load.wait()
     top, rows = cand_ref.shape
     tiles = img_ref.shape[1] // LANES
     low = lane_row() < LANES // 2
@@ -123,8 +129,10 @@
                 ]
 
 
-def shift_kernel(from_ref, packed_ref, out_ref, half_ref, own_ref, rot_ref):
-    own_ref[...] = packed_ref[...]
+def shift_kernel(from_at, out_ref, half_ref, from_ref, rot_ref, sem):
+    load = pltpu.make_async_copy(from_at, from_ref, sem)
+    load.start()
+    load.wait()
     count, pixels = rot_ref.shape
     rots = from_ref.shape[0]
     half_count, half_rots = count // 2, rots // 2
@@ -363,12 +371,16 @@
     totals_ref[...] = jnp.sum(jnp.where(here, total, 0.0), axis=0, keepdims=True)[:, :rots]
 
 
-def call(kernel, out_shape, count, limit, scratch=(), flops=0, moved=0, space=pltpu.VMEM):
+def far_away(value):
+    return pltpu.with_memory_space_constraint(value, pltpu.HBM)
+
+
+def call(kernel, out_shape, count, limit, scratch=(), flops=0, moved=0, far=0):
     in_vmem = pl.BlockSpec(memory_space=pltpu.VMEM)
     return pl.pallas_call(
         kernel,
         out_shape=out_shape,
-        in_specs=[pl.BlockSpec(memory_space=space)] * count,
+        in_specs=[pl.BlockSpec(memory_space=pltpu.HBM)] * far + [in_vmem] * (count - far),
         out_specs=jax.tree.map(lambda _: in_vmem, out_shape),
         scratch_shapes=list(scratch),
         cost_estimate=pl.CostEstimate(flops=flops, bytes_accessed=moved, transcendentals=0),
@@ -392,9 +404,16 @@
         pack_kernel,
         shape(((tiles + 1) * rows, LANES), BF16),
         3,
-        54,
+        4,
+        [
+            pltpu.VMEM((top, rows), jnp.int32),
+            pltpu.VMEM((1, rows), BF16),
+            pltpu.VMEM((rows, pixels), BF16),
+            pltpu.SemaphoreType.DMA((3,)),
+        ],
         moved=MIB // 4,
-    )(candidates.T, inv_noise[None, :], images)
+        far=3,
+    )(far_away(candidates.T), far_away(inv_noise[None, :]), far_away(images))
 
     def move(part, step):
         return lax.ppermute(part, "z", [(i, (i + step) % planes) for i in range(planes)])
@@ -406,25 +425,24 @@
     pad = half_count - half_rots
     count = 2 * half_count
     groups = len(COL_SHIFTS) * count
-    shifted, half_norm, own = call(
+    shifted, half_norm = call(
         shift_kernel,
-        (
-            shape((len(ROW_SHIFTS) * groups, pixels), BF16),
-            shape((count, LANES), F32),
-            shape(packed.shape, BF16),
-        ),
-        2,
+        (shape((len(ROW_SHIFTS) * groups, pixels), BF16), shape((count, LANES), F32)),
+        1,
         6,
-        [pltpu.VMEM((count, pixels), BF16)],
+        [
+            pltpu.VMEM((rots, pixels), BF16),
+            pltpu.VMEM((count, pixels), BF16),
+            pltpu.SemaphoreType.DMA,
+        ],
         moved=12 * MIB,
-    )(references[0], packed)
-    next_near, shifted, half_norm, own = lax.optimization_barrier(
-        (next_near, shifted, half_norm, own)
-    )
+        far=1,
+    )(far_away(references[0]))
+    next_near, shifted, half_norm = lax.optimization_barrier((next_near, shifted, half_norm))
     cut = (tiles + 1) // 2 * rows
     far = [move(next_near[0], 1), move(next_near[1], -1)]
     far += [move(next_near[0][:cut], 2), move(next_near[1][cut:], -2)]
-    column = [own, *near, *next_near, *far]
+    column = [packed, *near, *next_near, *far]
     steps = [0, -1, 1, -2, 2, -3, 3, 4, 4]
     picked = call(
         functools.partial(pick_kernel, steps=steps, top=top),

time: 96.1 us -> 95.5 us (level)
  local copies, waits for them, and re-layouts: 1.98 us -> 0.01 us
    unnamed x4 -> x0, local copies, waits for them, and re-layouts: 1.97 us -> none
    pallas_call x1, Pallas kernels: 1.59 us -> 2.65 us  [on_device(): call(shift_kernel, (shape((len(ROW_SHIFTS) * groups, pixels), BF16), shap...]
  transfers between devices with their start and end apart: 9 -> 9, of which waited for: 4 -> 3; matrix products, arithmetic and copies ran while one was open for 0% -> 0% of each run, Pallas kernels for 3% -> 4%
where the time goes in v8:
time: 95.5 us; the launch traced here: 95.3 us
  blocking collectives  53.3 us (56%)
  starting transfers between devices  23.5 us (25%)
  Pallas kernels  11.4 us (12%)
  waiting for transfers between devices  6.36 us (7%)
    all_to_all x1, blocking collectives, on_device(): received = exchange(picked, 'xy')  31.3 us
    ppermute x8, starting transfers between devices, move(): lax.ppermute(part, 'z', [(i, (i + step) % planes) for i in range(planes)])  15.2 us
    all_to_all x1, blocking collectives, on_device(): exchange(tile, 'z')  11.6 us
    all_to_all x1, blocking collectives, on_device(): everyone = exchange(folded, 'xy')  10.4 us
    ppermute x1, starting transfers between devices, on_device(): other = lax.ppermute(give, 'dp', [(0, 1), (1, 0)])  8.36 us
    ppermute x8, waiting for transfers between devices, move(): lax.ppermute(part, 'z', [(i, (i + step) % planes) for i in range(planes)])  5.81 us
    pallas_call x1, Pallas kernels, on_device(): call(shift_kernel, (shape((len(ROW_SHIFTS) * groups, pixels), BF16), shap...  2.65 us
    pallas_call x1, Pallas kernels, on_device(): call(functools.partial(score_kernel, pad=pad), (shape((slots, pixels + 2...  2.06 us
  transfers between devices with their start and end apart: 9, of which 3 were waited for; matrix products, arithmetic and copies ran while one was open for 0% of the time, Pallas kernels for 4%

profile of v8, /device:TPU:1, one launch (start us, length us, event | category | flops | bytes accessed | tf_op | source)
XLA Modules:
  0.0 95.3 jit_solution(4579498129406774347)
XLA Ops:
  0.6 1.1 %shard_map.59.refs_0_ = bf16[528,128]{1,0:T(8,128)(2,1)S(1)} custom-call(s32[8,16]{1,0:T(8,128)} %bitcast.5, bf16[1,16]{1,0:T(2,128)(2,1)} %bitcast.6, bf16[16,4096]{1,0:T(8,128)(2,1)} %img_at.1), custom_call_target="tpu_custom_call" | custom-call | bytes 262144 | tf_op jit(solution)/shard_map/pallas_call | solution.py:403
  1.8 6.9 %collective-permute-start.3 = (bf16[528,128]{1,0:T(8,128)(2,1)S(1)}, bf16[528,128]{1,0:T(8,128)(2,1)S(1)}, u32[]{:S(2)}, u32[]{:S(2)}) collective-permute-start(bf16[528,128]{1,0:T(8,128)(2,1)S(1)} %shard_map.59.refs_0_), channel_id=1, source_target_pairs={{0,192},{32,224},{64,0},{96,32},{128,64},{160,96},{192,128},{224,1... | collective-permute-start | bytes 405512 | tf_op jit(solution)/shard_map/ppermute | solution.py:419
  8.7 0.0 collective-permute-start.2
  8.7 3.1 %collective-permute-start.1 = (bf16[528,128]{1,0:T(8,128)(2,1)S(1)}, bf16[528,128]{1,0:T(8,128)(2,1)S(1)}, u32[]{:S(2)}, u32[]{:S(2)}) collective-permute-start(bf16[528,128]{1,0:T(8,128)(2,1)S(1)} %shard_map.59.refs_0_), channel_id=1, source_target_pairs={{0,224},{32,0},{64,32},{96,64},{128,96},{160,128},{192,160},{224,1... | collective-permute-start | bytes 405512 | tf_op jit(solution)/shard_map/ppermute | solution.py:419
  11.8 0.0 collective-permute-start
  11.8 2.7 %shard_map.60 = (bf16[720,4096]{1,0:T(8,128)(2,1)S(1)}, f32[80,128]{1,0:T(8,128)S(1)}) custom-call(bf16[72,4096]{1,0:T(8,128)(2,1)} %bitcast.4), custom_call_target="tpu_custom_call" | custom-call | bytes 12582912 | tf_op jit(solution)/shard_map/pallas_call | solution.py:428
  14.5 0.0 collective-permute-done.3.refs_4_
  14.5 1.8 %collective-permute-done.2.refs_3_ = bf16[528,128]{1,0:T(8,128)(2,1)S(1)} collective-permute-done((bf16[528,128]{1,0:T(8,128)(2,1)S(1)}, bf16[528,128]{1,0:T(8,128)(2,1)S(1)}, u32[]{:S(2)}, u32[]{:S(2)}) %collective-permute-start.2) | collective-permute-done | bytes 135200 | tf_op jit(solution)/shard_map/ppermute | solution.py:419
  16.3 2.2 %collective-permute-start.4 = (bf16[528,128]{1,0:T(8,128)(2,1)S(1)}, bf16[528,128]{1,0:T(8,128)(2,1)S(1)}, u32[]{:S(2)}, u32[]{:S(2)}) collective-permute-start(bf16[528,128]{1,0:T(8,128)(2,1)S(1)} %collective-permute-done.2.refs_3_), channel_id=1, source_target_pairs={{0,32},{32,64},{64,96},{96,128},{128,160},{160,192},{192,224},{224... | collective-permute-start | bytes 405512 | tf_op jit(solution)/shard_map/ppermute | solution.py:419
  18.5 0.5 collective-permute-start.5
  19.0 0.9 collective-permute-start.7
  19.9 0.0 collective-permute-done.1.refs_2_
  19.9 1.5 %collective-permute-start.6 = (bf16[256,128]{1,0:T(8,128)(2,1)S(1)}, bf16[256,128]{1,0:T(8,128)(2,1)S(1)}, u32[]{:S(2)}, u32[]{:S(2)}) collective-permute-start(bf16[256,128]{1,0:T(8,128)(2,1)S(1)} %slice.6), channel_id=1, source_target_pairs={{0,64},{32,96},{64,128},{96,160},{128,192},{160,224},{192,0},{224,... | collective-permute-start | bytes 196616 | tf_op jit(solution)/shard_map/ppermute | solution.py:419
  21.4 0.0 collective-permute-done.refs_1_
  21.4 4.0 %collective-permute-done.6.refs_7_ = bf16[256,128]{1,0:T(8,128)(2,1)S(1)} collective-permute-done((bf16[256,128]{1,0:T(8,128)(2,1)S(1)}, bf16[256,128]{1,0:T(8,128)(2,1)S(1)}, u32[]{:S(2)}, u32[]{:S(2)}) %collective-permute-start.6) | collective-permute-done | bytes 65568 | tf_op jit(solution)/shard_map/ppermute | solution.py:419
  25.4 0.0 collective-permute-done.7.refs_8_
  25.4 0.0 collective-permute-done.4.refs_5_
  25.4 0.0 collective-permute-done.5.refs_6_
  25.5 1.2 %shard_map.61 = bf16[16,528,128]{2,1,0:T(8,128)(2,1)S(1)} custom-call(bf16[528,128]{1,0:T(8,128)(2,1)S(1)} %shard_map.59.refs_0_, bf16[528,128]{1,0:T(8,128)(2,1)S(1)} %collective-permute-done.refs_1_, bf16[528,128]{1,0:T(8,128)(2,1)S(1)} %collective-permute-done.1.refs_2_, bf16[528,128]{1,0:T(8,128)(2,1)S(1)} %collective-permute-done.2.refs_3_, ...), custom_call_target="tpu_custom_call" | custom-call | bytes 3145728 | tf_op jit(solution)/shard_map/pallas_call | solution.py:447
  26.6 31.3 %all_to_all.15.recv_ref = bf16[16,528,128]{2,1,0:T(8,128)(2,1)S(1)} all-to-all(bf16[16,528,128]{2,1,0:T(8,128)(2,1)S(1)} %shard_map.61), channel_id=1, replica_groups=mesh['z'=8,'xy'=16,'dp'=2] {'xy'}, dimensions={0} | all-to-all | bytes 4325376 | tf_op jit(solution)/shard_map/all_to_all | solution.py:455
  58.0 2.1 %shard_map.62 = (bf16[256,4352]{1,0:T(8,128)(2,1)S(1)}, f32[240,768]{1,0:T(8,128)S(1)}, f32[8,8,128]{2,1,0:T(8,128)S(1)}) custom-call(bf16[16,528,128]{2,1,0:T(8,128)(2,1)S(1)} %all_to_all.15.recv_ref, bf16[720,4096]{1,0:T(8,128)(2,1)S(1)} %get-tuple-element.20.shifted_ref, f32[80,128]{1,0:T(8,128)S(1)} %get-tuple-element.21.half_ref), custom_call_target="tpu_custom_call" | custom-call | flops 1509949440 | bytes 10485760 | tf_op jit(solution)/shard_map/pallas_call | solution.py:457
  60.0 11.6 %all_to_all.16.shown_ref = f32[8,8,128]{2,1,0:T(8,128)S(1)} all-to-all(f32[8,8,128]{2,1,0:T(8,128)S(1)} %get-tuple-element.24.mine_ref), channel_id=1, replica_groups=mesh['z'=8,'xy'=16,'dp'=2] {'z'}, dimensions={0} | all-to-all | bytes 65536 | tf_op jit(solution)/shard_map/all_to_all | solution.py:471
  71.6 0.3 shard_map.63
  71.9 10.4 %all_to_all.17.all_ref = f32[16,32,128]{2,1,0:T(8,128)S(1)} all-to-all(f32[16,32,128]{2,1,0:T(8,128)S(1)} %shard_map.63), channel_id=1, replica_groups=mesh['z'=8,'xy'=16,'dp'=2] {'xy'}, dimensions={0} | all-to-all | bytes 524288 | tf_op jit(solution)/shard_map/all_to_all | solution.py:472
  82.2 1.4 %shard_map.64 = (f32[40,4224]{1,0:T(8,128)S(1)}, bf16[120,768]{1,0:T(8,128)(2,1)S(1)}, f32[40,128]{1,0:T(8,128)S(1)}) custom-call(f32[240,768]{1,0:T(8,128)S(1)} %get-tuple-element.22.s_ref, bf16[256,4352]{1,0:T(8,128)(2,1)S(1)} %get-tuple-element.23.x_ref, f32[8,8,128]{2,1,0:T(8,128)S(1)} %get-tuple-element.24.mine_ref, f32[16,32,128]{2,1,0:T(8,128)S(1)} %all_to_all.17.all_ref), custom_call_target="tpu_custom_call" | custom-call | flops 754974720 | bytes 5242880 | tf_op jit(solution)/shard_map/pallas_call | solution.py:475
  83.7 8.4 %collective-permute-start.8 = (f32[40,4224]{1,0:T(8,128)S(1)}, f32[40,4224]{1,0:T(8,128)S(1)}, u32[]{:S(2)}, u32[]{:S(2)}) collective-permute-start(f32[40,4224]{1,0:T(8,128)S(1)} %get-tuple-element.27), channel_id=1, source_target_pairs={{0,1},{1,0},{2,3},{3,2},{4,5},{5,4},{6,7},{7,6},{8,9},{9,8},{10,11... | collective-permute-start | bytes 2027528 | tf_op jit(solution)/shard_map/ppermute | solution.py:488
  92.0 1.2 %shard_map.65.keep_ref = f32[40,4096]{1,0:T(8,128)S(1)} custom-call(bf16[120,768]{1,0:T(8,128)(2,1)S(1)} %get-tuple-element.25.w_ref, bf16[256,4352]{1,0:T(8,128)(2,1)S(1)} %get-tuple-element.23.x_ref), custom_call_target="tpu_custom_call" | custom-call | flops 754974720 | bytes 4194304 | tf_op jit(solution)/shard_map/pallas_call | solution.py:489
  93.2 0.6 collective-permute-done.8.other_ref
  93.8 1.5 %shard_map.66 = (f32[1152,128]{1,0:T(8,128)}, f32[1,36]{1,0:T(1,128)}) custom-call(f32[40,4096]{1,0:T(8,128)S(1)} %shard_map.65.keep_ref, f32[40,128]{1,0:T(8,128)S(1)} %get-tuple-element.26.total_ref, f32[40,4224]{1,0:T(8,128)S(1)} %collective-permute-done.8.other_ref), custom_call_target="tpu_custom_call" | custom-call | bytes 2097152 | tf_op jit(solution)/shard_map/pallas_call | solution.py:498
  (2 shorter events, 0.0 us)
Async XLA Ops:
  1.8 12.7 %collective-permute-start.3 = (bf16[528,128]{1,0:T(8,128)(2,1)S(1)}, bf16[528,128]{1,0:T(8,128)(2,1)S(1)}, u32[]{:S(2)}, u32[]{:S(2)}) collective-permute-start(bf16[528,128]{1,0:T(8,128)(2,1)S(1)} %shard_map.59.refs_0_), channel_id=1, source_target_pairs={{0,192},{32,224},{64,0},{96,32},{128,64},{160,96},{192,128},{224,1... | collective-permute-start | bytes 405512 | tf_op jit(solution)/shard_map/ppermute | solution.py:419
  8.7 7.6 %collective-permute-start.2 = (bf16[528,128]{1,0:T(8,128)(2,1)S(1)}, bf16[528,128]{1,0:T(8,128)(2,1)S(1)}, u32[]{:S(2)}, u32[]{:S(2)}) collective-permute-start(bf16[528,128]{1,0:T(8,128)(2,1)S(1)} %shard_map.59.refs_0_), channel_id=1, source_target_pairs={{0,64},{32,96},{64,128},{96,160},{128,192},{160,224},{192,0},{224,... | collective-permute-start | bytes 405512 | tf_op jit(solution)/shard_map/ppermute | solution.py:419
  8.7 11.2 %collective-permute-start.1 = (bf16[528,128]{1,0:T(8,128)(2,1)S(1)}, bf16[528,128]{1,0:T(8,128)(2,1)S(1)}, u32[]{:S(2)}, u32[]{:S(2)}) collective-permute-start(bf16[528,128]{1,0:T(8,128)(2,1)S(1)} %shard_map.59.refs_0_), channel_id=1, source_target_pairs={{0,224},{32,0},{64,32},{96,64},{128,96},{160,128},{192,160},{224,1... | collective-permute-start | bytes 405512 | tf_op jit(solution)/shard_map/ppermute | solution.py:419
  11.8 9.6 %collective-permute-start = (bf16[528,128]{1,0:T(8,128)(2,1)S(1)}, bf16[528,128]{1,0:T(8,128)(2,1)S(1)}, u32[]{:S(2)}, u32[]{:S(2)}) collective-permute-start(bf16[528,128]{1,0:T(8,128)(2,1)S(1)} %shard_map.59.refs_0_), channel_id=1, source_target_pairs={{0,32},{32,64},{64,96},{96,128},{128,160},{160,192},{192,224},{224... | collective-permute-start | bytes 405512 | tf_op jit(solution)/shard_map/ppermute | solution.py:419
  16.3 9.2 %collective-permute-start.4 = (bf16[528,128]{1,0:T(8,128)(2,1)S(1)}, bf16[528,128]{1,0:T(8,128)(2,1)S(1)}, u32[]{:S(2)}, u32[]{:S(2)}) collective-permute-start(bf16[528,128]{1,0:T(8,128)(2,1)S(1)} %collective-permute-done.2.refs_3_), channel_id=1, source_target_pairs={{0,32},{32,64},{64,96},{96,128},{128,160},{160,192},{192,224},{224... | collective-permute-start | bytes 405512 | tf_op jit(solution)/shard_map/ppermute | solution.py:419
  18.5 7.0 %collective-permute-start.5 = (bf16[528,128]{1,0:T(8,128)(2,1)S(1)}, bf16[528,128]{1,0:T(8,128)(2,1)S(1)}, u32[]{:S(2)}, u32[]{:S(2)}) collective-permute-start(bf16[528,128]{1,0:T(8,128)(2,1)S(1)} %collective-permute-done.3.refs_4_), channel_id=1, source_target_pairs={{0,224},{32,0},{64,32},{96,64},{128,96},{160,128},{192,160},{224,1... | collective-permute-start | bytes 405512 | tf_op jit(solution)/shard_map/ppermute | solution.py:419
  19.0 6.5 %collective-permute-start.7 = (bf16[272,128]{1,0:T(8,128)(2,1)S(1)}, bf16[272,128]{1,0:T(8,128)(2,1)S(1)}, u32[]{:S(2)}, u32[]{:S(2)}) collective-permute-start(bf16[272,128]{1,0:T(8,128)(2,1)S(1)} %slice.7), channel_id=1, source_target_pairs={{0,192},{32,224},{64,0},{96,32},{128,64},{160,96},{192,128},{224,1... | collective-permute-start | bytes 208904 | tf_op jit(solution)/shard_map/ppermute | solution.py:419
  19.9 5.5 %collective-permute-start.6 = (bf16[256,128]{1,0:T(8,128)(2,1)S(1)}, bf16[256,128]{1,0:T(8,128)(2,1)S(1)}, u32[]{:S(2)}, u32[]{:S(2)}) collective-permute-start(bf16[256,128]{1,0:T(8,128)(2,1)S(1)} %slice.6), channel_id=1, source_target_pairs={{0,64},{32,96},{64,128},{96,160},{128,192},{160,224},{192,0},{224,... | collective-permute-start | bytes 196616 | tf_op jit(solution)/shard_map/ppermute | solution.py:419
  83.7 10.1 %collective-permute-start.8 = (f32[40,4224]{1,0:T(8,128)S(1)}, f32[40,4224]{1,0:T(8,128)S(1)}, u32[]{:S(2)}, u32[]{:S(2)}) collective-permute-start(f32[40,4224]{1,0:T(8,128)S(1)} %get-tuple-element.27), channel_id=1, source_target_pairs={{0,1},{1,0},{2,3},{3,2},{4,5},{5,4},{6,7},{7,6},{8,9},{9,8},{10,11... | collective-permute-start | bytes 2027528 | tf_op jit(solution)/shard_map/ppermute | solution.py:488

commit v9 on v8

--- a/solution.py
+++ b/solution.py
@@ -438,12 +438,12 @@
         moved=12 * MIB,
         far=1,
     )(far_away(references[0]))
-    next_near, shifted, half_norm = lax.optimization_barrier((next_near, shifted, half_norm))
     cut = (tiles + 1) // 2 * rows
     far = [move(next_near[0], 1), move(next_near[1], -1)]
     far += [move(next_near[0][:cut], 2), move(next_near[1][cut:], -2)]
     column = [packed, *near, *next_near, *far]
     steps = [0, -1, 1, -2, 2, -3, 3, 4, 4]
+    column, shifted, half_norm = lax.optimization_barrier((column, shifted, half_norm))
     picked = call(
         functools.partial(pick_kernel, steps=steps, top=top),
         shape((owners, (tiles + 1) * group, LANES), BF16),

time: 95.5 us -> 94.1 us (0.985)
  waiting for transfers between devices: 6.36 us -> 3.73 us
  starting transfers between devices: 23.5 us -> 25.5 us
    ppermute x8, starting transfers between devices: 15.2 us -> 18.7 us  [move(): lax.ppermute(part, 'z', [(i, (i + step) % planes) for i in range(planes)])]
    ppermute x8, waiting for transfers between devices: 5.81 us -> 3.17 us  [move(): lax.ppermute(part, 'z', [(i, (i + step) % planes) for i in range(planes)])]
    ppermute x1, starting transfers between devices: 8.36 us -> 6.81 us  [on_device(): other = lax.ppermute(give, 'dp', [(0, 1), (1, 0)])]
    all_to_all x1, blocking collectives: 11.6 us -> 10.1 us  [on_device(): exchange(tile, 'z')]
where the time goes in v9:
time: 94.1 us; the launch traced here: 93.8 us
  blocking collectives  52.5 us (56%)
  starting transfers between devices  25.5 us (27%)
  Pallas kernels  11.3 us (12%)
  waiting for transfers between devices  3.73 us (4%)
    all_to_all x1, blocking collectives, on_device(): received = exchange(picked, 'xy')  32 us
    ppermute x8, starting transfers between devices, move(): lax.ppermute(part, 'z', [(i, (i + step) % planes) for i in range(planes)])  18.7 us
    all_to_all x1, blocking collectives, on_device(): everyone = exchange(folded, 'xy')  10.4 us
    all_to_all x1, blocking collectives, on_device(): exchange(tile, 'z')  10.1 us
    ppermute x1, starting transfers between devices, on_device(): other = lax.ppermute(give, 'dp', [(0, 1), (1, 0)])  6.81 us
    ppermute x8, waiting for transfers between devices, move(): lax.ppermute(part, 'z', [(i, (i + step) % planes) for i in range(planes)])  3.17 us
    pallas_call x1, Pallas kernels, on_device(): call(shift_kernel, (shape((len(ROW_SHIFTS) * groups, pixels), BF16), shap...  2.65 us
    pallas_call x1, Pallas kernels, on_device(): call(functools.partial(score_kernel, pad=pad), (shape((slots, pixels + 2...  2.06 us
  transfers between devices with their start and end apart: 9, of which 3 were waited for; matrix products, arithmetic and copies ran while one was open for 0% of the time, Pallas kernels for 4%

profile of v9, /device:TPU:1, one launch (start us, length us, event | category | flops | bytes accessed | tf_op | source)
XLA Modules:
  0.0 93.8 jit_solution(393267892651649837)
XLA Ops:
  0.6 1.1 %shard_map.59.refs_0_ = bf16[528,128]{1,0:T(8,128)(2,1)S(1)} custom-call(s32[8,16]{1,0:T(8,128)} %bitcast.5, bf16[1,16]{1,0:T(2,128)(2,1)} %bitcast.6, bf16[16,4096]{1,0:T(8,128)(2,1)} %img_at.1), custom_call_target="tpu_custom_call" | custom-call | bytes 262144 | tf_op jit(solution)/shard_map/pallas_call | solution.py:403
  1.8 6.9 %collective-permute-start.3 = (bf16[528,128]{1,0:T(8,128)(2,1)S(1)}, bf16[528,128]{1,0:T(8,128)(2,1)S(1)}, u32[]{:S(2)}, u32[]{:S(2)}) collective-permute-start(bf16[528,128]{1,0:T(8,128)(2,1)S(1)} %shard_map.59.refs_0_), channel_id=1, source_target_pairs={{0,192},{32,224},{64,0},{96,32},{128,64},{160,96},{192,128},{224,1... | collective-permute-start | bytes 405512 | tf_op jit(solution)/shard_map/ppermute | solution.py:419
  8.7 0.0 collective-permute-start.2
  8.7 3.1 %collective-permute-start.1 = (bf16[528,128]{1,0:T(8,128)(2,1)S(1)}, bf16[528,128]{1,0:T(8,128)(2,1)S(1)}, u32[]{:S(2)}, u32[]{:S(2)}) collective-permute-start(bf16[528,128]{1,0:T(8,128)(2,1)S(1)} %shard_map.59.refs_0_), channel_id=1, source_target_pairs={{0,224},{32,0},{64,32},{96,64},{128,96},{160,128},{192,160},{224,1... | collective-permute-start | bytes 405512 | tf_op jit(solution)/shard_map/ppermute | solution.py:419
  11.8 0.0 collective-permute-start
  11.8 0.4 collective-permute-done.3.refs_4_
  12.2 4.7 %collective-permute-start.5 = (bf16[528,128]{1,0:T(8,128)(2,1)S(1)}, bf16[528,128]{1,0:T(8,128)(2,1)S(1)}, u32[]{:S(2)}, u32[]{:S(2)}) collective-permute-start(bf16[528,128]{1,0:T(8,128)(2,1)S(1)} %collective-permute-done.3.refs_4_), channel_id=1, source_target_pairs={{0,224},{32,0},{64,32},{96,64},{128,96},{160,128},{192,160},{224,1... | collective-permute-start | bytes 405512 | tf_op jit(solution)/shard_map/ppermute | solution.py:419
  17.0 0.0 collective-permute-done.2.refs_3_
  17.0 1.5 %collective-permute-start.4 = (bf16[528,128]{1,0:T(8,128)(2,1)S(1)}, bf16[528,128]{1,0:T(8,128)(2,1)S(1)}, u32[]{:S(2)}, u32[]{:S(2)}) collective-permute-start(bf16[528,128]{1,0:T(8,128)(2,1)S(1)} %collective-permute-done.2.refs_3_), channel_id=1, source_target_pairs={{0,32},{32,64},{64,96},{96,128},{128,160},{160,192},{192,224},{224... | collective-permute-start | bytes 405512 | tf_op jit(solution)/shard_map/ppermute | solution.py:419
  18.5 1.4 %collective-permute-start.7 = (bf16[272,128]{1,0:T(8,128)(2,1)S(1)}, bf16[272,128]{1,0:T(8,128)(2,1)S(1)}, u32[]{:S(2)}, u32[]{:S(2)}) collective-permute-start(bf16[272,128]{1,0:T(8,128)(2,1)S(1)} %slice.9), channel_id=1, source_target_pairs={{0,192},{32,224},{64,0},{96,32},{128,64},{160,96},{192,128},{224,1... | collective-permute-start | bytes 208904 | tf_op jit(solution)/shard_map/ppermute | solution.py:419
  19.9 0.0 collective-permute-done.1.refs_2_
  19.9 1.1 %collective-permute-start.6 = (bf16[256,128]{1,0:T(8,128)(2,1)S(1)}, bf16[256,128]{1,0:T(8,128)(2,1)S(1)}, u32[]{:S(2)}, u32[]{:S(2)}) collective-permute-start(bf16[256,128]{1,0:T(8,128)(2,1)S(1)} %slice.8), channel_id=1, source_target_pairs={{0,64},{32,96},{64,128},{96,160},{128,192},{160,224},{192,0},{224,... | collective-permute-start | bytes 196616 | tf_op jit(solution)/shard_map/ppermute | solution.py:419
  21.0 2.7 %shard_map.60 = (bf16[720,4096]{1,0:T(8,128)(2,1)S(1)}, f32[80,128]{1,0:T(8,128)S(1)}) custom-call(bf16[72,4096]{1,0:T(8,128)(2,1)} %bitcast.4), custom_call_target="tpu_custom_call" | custom-call | bytes 12582912 | tf_op jit(solution)/shard_map/pallas_call | solution.py:428
  23.6 0.0 collective-permute-done.refs_1_
  23.6 2.7 %collective-permute-done.6.refs_7_ = bf16[256,128]{1,0:T(8,128)(2,1)S(1)} collective-permute-done((bf16[256,128]{1,0:T(8,128)(2,1)S(1)}, bf16[256,128]{1,0:T(8,128)(2,1)S(1)}, u32[]{:S(2)}, u32[]{:S(2)}) %collective-permute-start.6) | collective-permute-done | bytes 65568 | tf_op jit(solution)/shard_map/ppermute | solution.py:419
  26.4 0.0 collective-permute-done.7.refs_8_
  26.4 0.0 collective-permute-done.5.refs_6_
  26.4 0.0 collective-permute-done.4.refs_5_
  26.4 1.2 %shard_map.61 = bf16[16,528,128]{2,1,0:T(8,128)(2,1)S(1)} custom-call(bf16[528,128]{1,0:T(8,128)(2,1)S(1)} %shard_map.59.refs_0_, bf16[528,128]{1,0:T(8,128)(2,1)S(1)} %collective-permute-done.refs_1_, bf16[528,128]{1,0:T(8,128)(2,1)S(1)} %collective-permute-done.1.refs_2_, bf16[528,128]{1,0:T(8,128)(2,1)S(1)} %collective-permute-done.2.refs_3_, ...), custom_call_target="tpu_custom_call" | custom-call | bytes 3145728 | tf_op jit(solution)/shard_map/pallas_call | solution.py:447
  27.5 32.0 %all_to_all.15.recv_ref = bf16[16,528,128]{2,1,0:T(8,128)(2,1)S(1)} all-to-all(bf16[16,528,128]{2,1,0:T(8,128)(2,1)S(1)} %shard_map.61), channel_id=1, replica_groups=mesh['z'=8,'xy'=16,'dp'=2] {'xy'}, dimensions={0} | all-to-all | bytes 4325376 | tf_op jit(solution)/shard_map/all_to_all | solution.py:455
  59.5 2.1 %shard_map.62 = (bf16[256,4352]{1,0:T(8,128)(2,1)S(1)}, f32[240,768]{1,0:T(8,128)S(1)}, f32[8,8,128]{2,1,0:T(8,128)S(1)}) custom-call(bf16[16,528,128]{2,1,0:T(8,128)(2,1)S(1)} %all_to_all.15.recv_ref, bf16[720,4096]{1,0:T(8,128)(2,1)S(1)} %get-tuple-element.34.shifted_ref, f32[80,128]{1,0:T(8,128)S(1)} %get-tuple-element.35.half_ref), custom_call_target="tpu_custom_call" | custom-call | flops 1509949440 | bytes 10485760 | tf_op jit(solution)/shard_map/pallas_call | solution.py:457
  61.6 10.1 %all_to_all.16.shown_ref = f32[8,8,128]{2,1,0:T(8,128)S(1)} all-to-all(f32[8,8,128]{2,1,0:T(8,128)S(1)} %get-tuple-element.38.mine_ref), channel_id=1, replica_groups=mesh['z'=8,'xy'=16,'dp'=2] {'z'}, dimensions={0} | all-to-all | bytes 65536 | tf_op jit(solution)/shard_map/all_to_all | solution.py:471
  71.7 0.3 shard_map.63
  72.0 10.4 %all_to_all.17.all_ref = f32[16,32,128]{2,1,0:T(8,128)S(1)} all-to-all(f32[16,32,128]{2,1,0:T(8,128)S(1)} %shard_map.63), channel_id=1, replica_groups=mesh['z'=8,'xy'=16,'dp'=2] {'xy'}, dimensions={0} | all-to-all | bytes 524288 | tf_op jit(solution)/shard_map/all_to_all | solution.py:472
  82.4 1.4 %shard_map.64 = (f32[40,4224]{1,0:T(8,128)S(1)}, bf16[120,768]{1,0:T(8,128)(2,1)S(1)}, f32[40,128]{1,0:T(8,128)S(1)}) custom-call(f32[240,768]{1,0:T(8,128)S(1)} %get-tuple-element.36.s_ref, bf16[256,4352]{1,0:T(8,128)(2,1)S(1)} %get-tuple-element.37.x_ref, f32[8,8,128]{2,1,0:T(8,128)S(1)} %get-tuple-element.38.mine_ref, f32[16,32,128]{2,1,0:T(8,128)S(1)} %all_to_all.17.all_ref), custom_call_target="tpu_custom_call" | custom-call | flops 754974720 | bytes 5242880 | tf_op jit(solution)/shard_map/pallas_call | solution.py:475
  83.8 6.8 %collective-permute-start.8 = (f32[40,4224]{1,0:T(8,128)S(1)}, f32[40,4224]{1,0:T(8,128)S(1)}, u32[]{:S(2)}, u32[]{:S(2)}) collective-permute-start(f32[40,4224]{1,0:T(8,128)S(1)} %get-tuple-element.41), channel_id=1, source_target_pairs={{0,1},{1,0},{2,3},{3,2},{4,5},{5,4},{6,7},{7,6},{8,9},{9,8},{10,11... | collective-permute-start | bytes 2027528 | tf_op jit(solution)/shard_map/ppermute | solution.py:488
  90.6 1.2 %shard_map.65.keep_ref = f32[40,4096]{1,0:T(8,128)S(1)} custom-call(bf16[120,768]{1,0:T(8,128)(2,1)S(1)} %get-tuple-element.39.w_ref, bf16[256,4352]{1,0:T(8,128)(2,1)S(1)} %get-tuple-element.37.x_ref), custom_call_target="tpu_custom_call" | custom-call | flops 754974720 | bytes 4194304 | tf_op jit(solution)/shard_map/pallas_call | solution.py:489
  91.8 0.6 collective-permute-done.8.other_ref
  92.4 1.5 %shard_map.66 = (f32[1152,128]{1,0:T(8,128)}, f32[1,36]{1,0:T(1,128)}) custom-call(f32[40,4096]{1,0:T(8,128)S(1)} %shard_map.65.keep_ref, f32[40,128]{1,0:T(8,128)S(1)} %get-tuple-element.40.total_ref, f32[40,4224]{1,0:T(8,128)S(1)} %collective-permute-done.8.other_ref), custom_call_target="tpu_custom_call" | custom-call | bytes 2097152 | tf_op jit(solution)/shard_map/pallas_call | solution.py:498
  (2 shorter events, 0.0 us)
Async XLA Ops:
  1.8 10.5 %collective-permute-start.3 = (bf16[528,128]{1,0:T(8,128)(2,1)S(1)}, bf16[528,128]{1,0:T(8,128)(2,1)S(1)}, u32[]{:S(2)}, u32[]{:S(2)}) collective-permute-start(bf16[528,128]{1,0:T(8,128)(2,1)S(1)} %shard_map.59.refs_0_), channel_id=1, source_target_pairs={{0,192},{32,224},{64,0},{96,32},{128,64},{160,96},{192,128},{224,1... | collective-permute-start | bytes 405512 | tf_op jit(solution)/shard_map/ppermute | solution.py:419
  8.7 8.3 %collective-permute-start.2 = (bf16[528,128]{1,0:T(8,128)(2,1)S(1)}, bf16[528,128]{1,0:T(8,128)(2,1)S(1)}, u32[]{:S(2)}, u32[]{:S(2)}) collective-permute-start(bf16[528,128]{1,0:T(8,128)(2,1)S(1)} %shard_map.59.refs_0_), channel_id=1, source_target_pairs={{0,64},{32,96},{64,128},{96,160},{128,192},{160,224},{192,0},{224,... | collective-permute-start | bytes 405512 | tf_op jit(solution)/shard_map/ppermute | solution.py:419
  8.7 11.2 %collective-permute-start.1 = (bf16[528,128]{1,0:T(8,128)(2,1)S(1)}, bf16[528,128]{1,0:T(8,128)(2,1)S(1)}, u32[]{:S(2)}, u32[]{:S(2)}) collective-permute-start(bf16[528,128]{1,0:T(8,128)(2,1)S(1)} %shard_map.59.refs_0_), channel_id=1, source_target_pairs={{0,224},{32,0},{64,32},{96,64},{128,96},{160,128},{192,160},{224,1... | collective-permute-start | bytes 405512 | tf_op jit(solution)/shard_map/ppermute | solution.py:419
  11.8 11.8 %collective-permute-start = (bf16[528,128]{1,0:T(8,128)(2,1)S(1)}, bf16[528,128]{1,0:T(8,128)(2,1)S(1)}, u32[]{:S(2)}, u32[]{:S(2)}) collective-permute-start(bf16[528,128]{1,0:T(8,128)(2,1)S(1)} %shard_map.59.refs_0_), channel_id=1, source_target_pairs={{0,32},{32,64},{64,96},{96,128},{128,160},{160,192},{192,224},{224... | collective-permute-start | bytes 405512 | tf_op jit(solution)/shard_map/ppermute | solution.py:419
  12.2 14.1 %collective-permute-start.5 = (bf16[528,128]{1,0:T(8,128)(2,1)S(1)}, bf16[528,128]{1,0:T(8,128)(2,1)S(1)}, u32[]{:S(2)}, u32[]{:S(2)}) collective-permute-start(bf16[528,128]{1,0:T(8,128)(2,1)S(1)} %collective-permute-done.3.refs_4_), channel_id=1, source_target_pairs={{0,224},{32,0},{64,32},{96,64},{128,96},{160,128},{192,160},{224,1... | collective-permute-start | bytes 405512 | tf_op jit(solution)/shard_map/ppermute | solution.py:419
  17.0 9.4 %collective-permute-start.4 = (bf16[528,128]{1,0:T(8,128)(2,1)S(1)}, bf16[528,128]{1,0:T(8,128)(2,1)S(1)}, u32[]{:S(2)}, u32[]{:S(2)}) collective-permute-start(bf16[528,128]{1,0:T(8,128)(2,1)S(1)} %collective-permute-done.2.refs_3_), channel_id=1, source_target_pairs={{0,32},{32,64},{64,96},{96,128},{128,160},{160,192},{192,224},{224... | collective-permute-start | bytes 405512 | tf_op jit(solution)/shard_map/ppermute | solution.py:419
  18.5 7.9 %collective-permute-start.7 = (bf16[272,128]{1,0:T(8,128)(2,1)S(1)}, bf16[272,128]{1,0:T(8,128)(2,1)S(1)}, u32[]{:S(2)}, u32[]{:S(2)}) collective-permute-start(bf16[272,128]{1,0:T(8,128)(2,1)S(1)} %slice.9), channel_id=1, source_target_pairs={{0,192},{32,224},{64,0},{96,32},{128,64},{160,96},{192,128},{224,1... | collective-permute-start | bytes 208904 | tf_op jit(solution)/shard_map/ppermute | solution.py:419
  19.9 6.5 %collective-permute-start.6 = (bf16[256,128]{1,0:T(8,128)(2,1)S(1)}, bf16[256,128]{1,0:T(8,128)(2,1)S(1)}, u32[]{:S(2)}, u32[]{:S(2)}) collective-permute-start(bf16[256,128]{1,0:T(8,128)(2,1)S(1)} %slice.8), channel_id=1, source_target_pairs={{0,64},{32,96},{64,128},{96,160},{128,192},{160,224},{192,0},{224,... | collective-permute-start | bytes 196616 | tf_op jit(solution)/shard_map/ppermute | solution.py:419
  83.8 8.6 %collective-permute-start.8 = (f32[40,4224]{1,0:T(8,128)S(1)}, f32[40,4224]{1,0:T(8,128)S(1)}, u32[]{:S(2)}, u32[]{:S(2)}) collective-permute-start(f32[40,4224]{1,0:T(8,128)S(1)} %get-tuple-element.41), channel_id=1, source_target_pairs={{0,1},{1,0},{2,3},{3,2},{4,5},{5,4},{6,7},{7,6},{8,9},{9,8},{10,11... | collective-permute-start | bytes 2027528 | tf_op jit(solution)/shard_map/ppermute | solution.py:488

commit v10 on v9

--- a/solution.py
+++ b/solution.py
@@ -79,29 +79,26 @@
 
 
 def pick_kernel(*refs, steps, top):
-    planes = len(steps) - 1
-    recv_refs, send_ref, column_ref = refs[: len(steps)], refs[-2], refs[-1]
+    planes = len(steps)
+    recv_refs, send_ref, column_ref = refs[:planes], refs[-2], refs[-1]
     owners, depth, _ = send_ref.shape
     rows = column_ref.shape[0] // planes
     tiles = column_ref.shape[1] // LANES
     group = depth // tiles
     slots = owners * group
-    cut = recv_refs[-2].shape[0] // rows
     for j in range(planes):
         for t in range(tiles):
-            from_ref, at = recv_refs[j], t
-            if j == planes - 1 and t >= cut:
-                from_ref, at = recv_refs[j + 1], t - cut
-            column_ref[j * rows : (j + 1) * rows, tile_of(t)] = from_ref[
-                at * rows : (at + 1) * rows
+            column_ref[j * rows : (j + 1) * rows, tile_of(t)] = recv_refs[j][
+                t * rows : (t + 1) * rows
             ]
     count = planes * rows
     facts = column_ref[:, tile_of(tiles - 1)].astype(F32)
     here = lax.axis_index("z")
+    way = 1 - 2 * lax.axis_index("dp")
     row = lax.broadcasted_iota(jnp.int32, (count, 1), 0)
     sender = jnp.zeros((count, 1), jnp.int32)
     for j in range(planes):
-        plane = lax.rem(here + steps[j] + planes, planes)
+        plane = lax.rem(here + way * steps[j] + planes, planes)
         sender = jnp.where(row // rows == j, plane, sender)
     lane = lax.broadcasted_iota(jnp.int32, (1, slots), 1)
     cls = (here * owners + lane // group).astype(F32)
@@ -416,7 +413,13 @@
     )(far_away(candidates.T), far_away(inv_noise[None, :]), far_away(images))
 
     def move(part, step):
-        return lax.ppermute(part, "z", [(i, (i + step) % planes) for i in range(planes)])
+        pairs = []
+        for z in range(planes):
+            pairs += [
+                (2 * z, (z + step) % planes * 2),
+                (2 * z + 1, (z - step) % planes * 2 + 1),
+            ]
+        return lax.ppermute(part, ("z", "dp"), pairs)
 
     near = [move(packed, step) for step in (1, -1)]
     next_near = [move(packed, step) for step in (2, -2)]
@@ -438,11 +441,9 @@
         moved=12 * MIB,
         far=1,
     )(far_away(references[0]))
-    cut = (tiles + 1) // 2 * rows
-    far = [move(next_near[0], 1), move(next_near[1], -1)]
-    far += [move(next_near[0][:cut], 2), move(next_near[1][cut:], -2)]
+    far = [move(next_near[0], 1), move(next_near[1], -1), move(next_near[0], 2)]
     column = [packed, *near, *next_near, *far]
-    steps = [0, -1, 1, -2, 2, -3, 3, 4, 4]
+    steps = [0, -1, 1, -2, 2, -3, 3, 4]
     column, shifted, half_norm = lax.optimization_barrier((column, shifted, half_norm))
     picked = call(
         functools.partial(pick_kernel, steps=steps, top=top),

time: 94.1 us -> 95.8 us (1.018)
  blocking collectives: 52.5 us -> 57.2 us
  starting transfers between devices: 25.5 us -> 21.3 us
  waiting for transfers between devices: 3.73 us -> 5.13 us
    all_to_all x1, blocking collectives: 10.1 us -> 14.7 us  [on_device(): exchange(tile, 'z')]
    ppermute x8 -> x7, starting transfers between devices: 18.7 us -> 16 us  [move(): return lax.ppermute(part, ('z', 'dp'), pairs)]
    ppermute x1, starting transfers between devices: 6.81 us -> 5.22 us  [on_device(): other = lax.ppermute(give, 'dp', [(0, 1), (1, 0)])]
    ppermute x8 -> x7, waiting for transfers between devices: 3.17 us -> 4.57 us  [move(): return lax.ppermute(part, ('z', 'dp'), pairs)]
  transfers between devices with their start and end apart: 9 -> 8, of which waited for: 3 -> 4; matrix products, arithmetic and copies ran while one was open for 0% -> 0% of each run, Pallas kernels for 4% -> 4%
where the time goes in v10:
time: 95.8 us; the launch traced here: 95.6 us
  blocking collectives  57.2 us (60%)
  starting transfers between devices  21.3 us (22%)
  Pallas kernels  11.4 us (12%)
  waiting for transfers between devices  5.13 us (5%)
    all_to_all x1, blocking collectives, on_device(): received = exchange(picked, 'xy')  32.3 us
    ppermute x7, starting transfers between devices, move(): return lax.ppermute(part, ('z', 'dp'), pairs)  16 us
    all_to_all x1, blocking collectives, on_device(): exchange(tile, 'z')  14.7 us
    all_to_all x1, blocking collectives, on_device(): everyone = exchange(folded, 'xy')  10.1 us
    ppermute x1, starting transfers between devices, on_device(): other = lax.ppermute(give, 'dp', [(0, 1), (1, 0)])  5.22 us
    ppermute x7, waiting for transfers between devices, move(): return lax.ppermute(part, ('z', 'dp'), pairs)  4.57 us
    pallas_call x1, Pallas kernels, on_device(): call(shift_kernel, (shape((len(ROW_SHIFTS) * groups, pixels), BF16), shap...  2.65 us
    pallas_call x1, Pallas kernels, on_device(): call(functools.partial(score_kernel, pad=pad), (shape((slots, pixels + 2...  2.06 us
  transfers between devices with their start and end apart: 8, of which 4 were waited for; matrix products, arithmetic and copies ran while one was open for 0% of the time, Pallas kernels for 4%

profile of v10, /device:TPU:1, one launch (start us, length us, event | category | flops | bytes accessed | tf_op | source)
XLA Modules:
  0.0 95.6 jit_solution(11955555332933228979)
XLA Ops:
  0.6 1.1 %shard_map.59.refs_0_ = bf16[528,128]{1,0:T(8,128)(2,1)S(1)} custom-call(s32[8,16]{1,0:T(8,128)} %bitcast.5, bf16[1,16]{1,0:T(2,128)(2,1)} %bitcast.6, bf16[16,4096]{1,0:T(8,128)(2,1)} %img_at.1), custom_call_target="tpu_custom_call" | custom-call | bytes 262144 | tf_op jit(solution)/shard_map/pallas_call | solution.py:400
  1.8 3.9 %collective-permute-start.3 = (bf16[528,128]{1,0:T(8,128)(2,1)S(1)}, bf16[528,128]{1,0:T(8,128)(2,1)S(1)}, u32[]{:S(2)}, u32[]{:S(2)}) collective-permute-start(bf16[528,128]{1,0:T(8,128)(2,1)S(1)} %shard_map.59.refs_0_), channel_id=1, source_target_pairs={{0,192},{1,65},{32,224},{33,97},{64,0},{65,129},{96,32},{97,161},{... | collective-permute-start | bytes 405512 | tf_op jit(solution)/shard_map/ppermute | solution.py:422
  5.7 3.1 %collective-permute-start.2 = (bf16[528,128]{1,0:T(8,128)(2,1)S(1)}, bf16[528,128]{1,0:T(8,128)(2,1)S(1)}, u32[]{:S(2)}, u32[]{:S(2)}) collective-permute-start(bf16[528,128]{1,0:T(8,128)(2,1)S(1)} %shard_map.59.refs_0_), channel_id=1, source_target_pairs={{0,64},{1,193},{32,96},{33,225},{64,128},{65,1},{96,160},{97,33},{... | collective-permute-start | bytes 405512 | tf_op jit(solution)/shard_map/ppermute | solution.py:422
  8.8 0.7 collective-permute-start.1
  9.5 1.9 %collective-permute-start = (bf16[528,128]{1,0:T(8,128)(2,1)S(1)}, bf16[528,128]{1,0:T(8,128)(2,1)S(1)}, u32[]{:S(2)}, u32[]{:S(2)}) collective-permute-start(bf16[528,128]{1,0:T(8,128)(2,1)S(1)} %shard_map.59.refs_0_), channel_id=1, source_target_pairs={{0,32},{1,225},{32,64},{33,1},{64,96},{65,33},{96,128},{97,65},{12... | collective-permute-start | bytes 405512 | tf_op jit(solution)/shard_map/ppermute | solution.py:422
  11.5 0.0 collective-permute-done.3.refs_4_
  11.5 1.9 %collective-permute-start.5 = (bf16[528,128]{1,0:T(8,128)(2,1)S(1)}, bf16[528,128]{1,0:T(8,128)(2,1)S(1)}, u32[]{:S(2)}, u32[]{:S(2)}) collective-permute-start(bf16[528,128]{1,0:T(8,128)(2,1)S(1)} %collective-permute-done.3.refs_4_), channel_id=1, source_target_pairs={{0,224},{1,33},{32,0},{33,65},{64,32},{65,97},{96,64},{97,129},{12... | collective-permute-start | bytes 405512 | tf_op jit(solution)/shard_map/ppermute | solution.py:422
  13.4 2.1 %collective-permute-done.2.refs_3_ = bf16[528,128]{1,0:T(8,128)(2,1)S(1)} collective-permute-done((bf16[528,128]{1,0:T(8,128)(2,1)S(1)}, bf16[528,128]{1,0:T(8,128)(2,1)S(1)}, u32[]{:S(2)}, u32[]{:S(2)}) %collective-permute-start.2) | collective-permute-done | bytes 135200 | tf_op jit(solution)/shard_map/ppermute | solution.py:422
  15.5 0.8 collective-permute-start.6
  16.3 3.6 %collective-permute-start.4 = (bf16[528,128]{1,0:T(8,128)(2,1)S(1)}, bf16[528,128]{1,0:T(8,128)(2,1)S(1)}, u32[]{:S(2)}, u32[]{:S(2)}) collective-permute-start(bf16[528,128]{1,0:T(8,128)(2,1)S(1)} %collective-permute-done.2.refs_3_), channel_id=1, source_target_pairs={{0,32},{1,225},{32,64},{33,1},{64,96},{65,33},{96,128},{97,65},{12... | collective-permute-start | bytes 405512 | tf_op jit(solution)/shard_map/ppermute | solution.py:422
  19.9 2.7 %shard_map.60 = (bf16[720,4096]{1,0:T(8,128)(2,1)S(1)}, f32[80,128]{1,0:T(8,128)S(1)}) custom-call(bf16[72,4096]{1,0:T(8,128)(2,1)} %bitcast.4), custom_call_target="tpu_custom_call" | custom-call | bytes 12582912 | tf_op jit(solution)/shard_map/pallas_call | solution.py:431
  22.6 0.0 collective-permute-done.1.refs_2_
  22.6 0.0 collective-permute-done.refs_1_
  22.6 0.0 collective-permute-done.5.refs_6_
  22.6 0.3 collective-permute-done.6.refs_7_
  22.9 2.2 %collective-permute-done.4.refs_5_ = bf16[528,128]{1,0:T(8,128)(2,1)S(1)} collective-permute-done((bf16[528,128]{1,0:T(8,128)(2,1)S(1)}, bf16[528,128]{1,0:T(8,128)(2,1)S(1)}, u32[]{:S(2)}, u32[]{:S(2)}) %collective-permute-start.4) | collective-permute-done | bytes 135200 | tf_op jit(solution)/shard_map/ppermute | solution.py:422
  25.1 1.2 %shard_map.61 = bf16[16,528,128]{2,1,0:T(8,128)(2,1)S(1)} custom-call(bf16[528,128]{1,0:T(8,128)(2,1)S(1)} %shard_map.59.refs_0_, bf16[528,128]{1,0:T(8,128)(2,1)S(1)} %collective-permute-done.refs_1_, bf16[528,128]{1,0:T(8,128)(2,1)S(1)} %collective-permute-done.1.refs_2_, bf16[528,128]{1,0:T(8,128)(2,1)S(1)} %collective-permute-done.2.refs_3_, ...), custom_call_target="tpu_custom_call" | custom-call | bytes 3145728 | tf_op jit(solution)/shard_map/pallas_call | solution.py:448
  26.2 32.3 %all_to_all.15.recv_ref = bf16[16,528,128]{2,1,0:T(8,128)(2,1)S(1)} all-to-all(bf16[16,528,128]{2,1,0:T(8,128)(2,1)S(1)} %shard_map.61), channel_id=1, replica_groups=mesh['z'=8,'xy'=16,'dp'=2] {'xy'}, dimensions={0} | all-to-all | bytes 4325376 | tf_op jit(solution)/shard_map/all_to_all | solution.py:456
  58.5 2.1 %shard_map.62 = (bf16[256,4352]{1,0:T(8,128)(2,1)S(1)}, f32[240,768]{1,0:T(8,128)S(1)}, f32[8,8,128]{2,1,0:T(8,128)S(1)}) custom-call(bf16[16,528,128]{2,1,0:T(8,128)(2,1)S(1)} %all_to_all.15.recv_ref, bf16[720,4096]{1,0:T(8,128)(2,1)S(1)} %get-tuple-element.32.shifted_ref, f32[80,128]{1,0:T(8,128)S(1)} %get-tuple-element.33.half_ref), custom_call_target="tpu_custom_call" | custom-call | flops 1509949440 | bytes 10485760 | tf_op jit(solution)/shard_map/pallas_call | solution.py:458
  60.6 14.7 %all_to_all.16.shown_ref = f32[8,8,128]{2,1,0:T(8,128)S(1)} all-to-all(f32[8,8,128]{2,1,0:T(8,128)S(1)} %get-tuple-element.36.mine_ref), channel_id=1, replica_groups=mesh['z'=8,'xy'=16,'dp'=2] {'z'}, dimensions={0} | all-to-all | bytes 65536 | tf_op jit(solution)/shard_map/all_to_all | solution.py:472
  75.3 0.3 shard_map.63
  75.6 10.1 %all_to_all.17.all_ref = f32[16,32,128]{2,1,0:T(8,128)S(1)} all-to-all(f32[16,32,128]{2,1,0:T(8,128)S(1)} %shard_map.63), channel_id=1, replica_groups=mesh['z'=8,'xy'=16,'dp'=2] {'xy'}, dimensions={0} | all-to-all | bytes 524288 | tf_op jit(solution)/shard_map/all_to_all | solution.py:473
  85.7 1.4 %shard_map.64 = (f32[40,4224]{1,0:T(8,128)S(1)}, bf16[120,768]{1,0:T(8,128)(2,1)S(1)}, f32[40,128]{1,0:T(8,128)S(1)}) custom-call(f32[240,768]{1,0:T(8,128)S(1)} %get-tuple-element.34.s_ref, bf16[256,4352]{1,0:T(8,128)(2,1)S(1)} %get-tuple-element.35.x_ref, f32[8,8,128]{2,1,0:T(8,128)S(1)} %get-tuple-element.36.mine_ref, f32[16,32,128]{2,1,0:T(8,128)S(1)} %all_to_all.17.all_ref), custom_call_target="tpu_custom_call" | custom-call | flops 754974720 | bytes 5242880 | tf_op jit(solution)/shard_map/pallas_call | solution.py:476
  87.1 5.2 %collective-permute-start.7 = (f32[40,4224]{1,0:T(8,128)S(1)}, f32[40,4224]{1,0:T(8,128)S(1)}, u32[]{:S(2)}, u32[]{:S(2)}) collective-permute-start(f32[40,4224]{1,0:T(8,128)S(1)} %get-tuple-element.39), channel_id=1, source_target_pairs={{0,1},{1,0},{2,3},{3,2},{4,5},{5,4},{6,7},{7,6},{8,9},{9,8},{10,11... | collective-permute-start | bytes 2027528 | tf_op jit(solution)/shard_map/ppermute | solution.py:489
  92.4 1.2 %shard_map.65.keep_ref = f32[40,4096]{1,0:T(8,128)S(1)} custom-call(bf16[120,768]{1,0:T(8,128)(2,1)S(1)} %get-tuple-element.37.w_ref, bf16[256,4352]{1,0:T(8,128)(2,1)S(1)} %get-tuple-element.35.x_ref), custom_call_target="tpu_custom_call" | custom-call | flops 754974720 | bytes 4194304 | tf_op jit(solution)/shard_map/pallas_call | solution.py:490
  93.6 0.6 collective-permute-done.7.other_ref
  94.1 1.5 %shard_map.66 = (f32[1152,128]{1,0:T(8,128)}, f32[1,36]{1,0:T(1,128)}) custom-call(f32[40,4096]{1,0:T(8,128)S(1)} %shard_map.65.keep_ref, f32[40,128]{1,0:T(8,128)S(1)} %get-tuple-element.38.total_ref, f32[40,4224]{1,0:T(8,128)S(1)} %collective-permute-done.7.other_ref), custom_call_target="tpu_custom_call" | custom-call | bytes 2097152 | tf_op jit(solution)/shard_map/pallas_call | solution.py:499
Async XLA Ops:
  1.8 9.7 %collective-permute-start.3 = (bf16[528,128]{1,0:T(8,128)(2,1)S(1)}, bf16[528,128]{1,0:T(8,128)(2,1)S(1)}, u32[]{:S(2)}, u32[]{:S(2)}) collective-permute-start(bf16[528,128]{1,0:T(8,128)(2,1)S(1)} %shard_map.59.refs_0_), channel_id=1, source_target_pairs={{0,192},{1,65},{32,224},{33,97},{64,0},{65,129},{96,32},{97,161},{... | collective-permute-start | bytes 405512 | tf_op jit(solution)/shard_map/ppermute | solution.py:422
  5.7 9.9 %collective-permute-start.2 = (bf16[528,128]{1,0:T(8,128)(2,1)S(1)}, bf16[528,128]{1,0:T(8,128)(2,1)S(1)}, u32[]{:S(2)}, u32[]{:S(2)}) collective-permute-start(bf16[528,128]{1,0:T(8,128)(2,1)S(1)} %shard_map.59.refs_0_), channel_id=1, source_target_pairs={{0,64},{1,193},{32,96},{33,225},{64,128},{65,1},{96,160},{97,33},{... | collective-permute-start | bytes 405512 | tf_op jit(solution)/shard_map/ppermute | solution.py:422
  8.8 13.8 %collective-permute-start.1 = (bf16[528,128]{1,0:T(8,128)(2,1)S(1)}, bf16[528,128]{1,0:T(8,128)(2,1)S(1)}, u32[]{:S(2)}, u32[]{:S(2)}) collective-permute-start(bf16[528,128]{1,0:T(8,128)(2,1)S(1)} %shard_map.59.refs_0_), channel_id=1, source_target_pairs={{0,224},{1,33},{32,0},{33,65},{64,32},{65,97},{96,64},{97,129},{12... | collective-permute-start | bytes 405512 | tf_op jit(solution)/shard_map/ppermute | solution.py:422
  9.5 13.1 %collective-permute-start = (bf16[528,128]{1,0:T(8,128)(2,1)S(1)}, bf16[528,128]{1,0:T(8,128)(2,1)S(1)}, u32[]{:S(2)}, u32[]{:S(2)}) collective-permute-start(bf16[528,128]{1,0:T(8,128)(2,1)S(1)} %shard_map.59.refs_0_), channel_id=1, source_target_pairs={{0,32},{1,225},{32,64},{33,1},{64,96},{65,33},{96,128},{97,65},{12... | collective-permute-start | bytes 405512 | tf_op jit(solution)/shard_map/ppermute | solution.py:422
  11.5 11.2 %collective-permute-start.5 = (bf16[528,128]{1,0:T(8,128)(2,1)S(1)}, bf16[528,128]{1,0:T(8,128)(2,1)S(1)}, u32[]{:S(2)}, u32[]{:S(2)}) collective-permute-start(bf16[528,128]{1,0:T(8,128)(2,1)S(1)} %collective-permute-done.3.refs_4_), channel_id=1, source_target_pairs={{0,224},{1,33},{32,0},{33,65},{64,32},{65,97},{96,64},{97,129},{12... | collective-permute-start | bytes 405512 | tf_op jit(solution)/shard_map/ppermute | solution.py:422
  15.5 7.4 %collective-permute-start.6 = (bf16[528,128]{1,0:T(8,128)(2,1)S(1)}, bf16[528,128]{1,0:T(8,128)(2,1)S(1)}, u32[]{:S(2)}, u32[]{:S(2)}) collective-permute-start(bf16[528,128]{1,0:T(8,128)(2,1)S(1)} %collective-permute-done.2.refs_3_), channel_id=1, source_target_pairs={{0,64},{1,193},{32,96},{33,225},{64,128},{65,1},{96,160},{97,33},{... | collective-permute-start | bytes 405512 | tf_op jit(solution)/shard_map/ppermute | solution.py:422
  16.3 8.7 %collective-permute-start.4 = (bf16[528,128]{1,0:T(8,128)(2,1)S(1)}, bf16[528,128]{1,0:T(8,128)(2,1)S(1)}, u32[]{:S(2)}, u32[]{:S(2)}) collective-permute-start(bf16[528,128]{1,0:T(8,128)(2,1)S(1)} %collective-permute-done.2.refs_3_), channel_id=1, source_target_pairs={{0,32},{1,225},{32,64},{33,1},{64,96},{65,33},{96,128},{97,65},{12... | collective-permute-start | bytes 405512 | tf_op jit(solution)/shard_map/ppermute | solution.py:422
  87.1 7.0 %collective-permute-start.7 = (f32[40,4224]{1,0:T(8,128)S(1)}, f32[40,4224]{1,0:T(8,128)S(1)}, u32[]{:S(2)}, u32[]{:S(2)}) collective-permute-start(f32[40,4224]{1,0:T(8,128)S(1)} %get-tuple-element.39), channel_id=1, source_target_pairs={{0,1},{1,0},{2,3},{3,2},{4,5},{5,4},{6,7},{7,6},{8,9},{9,8},{10,11... | collective-permute-start | bytes 2027528 | tf_op jit(solution)/shard_map/ppermute | solution.py:489
